TPU v7x, 32 devices: a whole 2x2x4 slice. The times are simulated.
32 devices in a mesh: ctx: 16 (over z, y, core), head: 2 (over x).
Axes of the slice: x: 2, y: 2, z: 4, core: 2. Of those that a mesh axis runs over, the one named last changes fastest.
Arguments:
- queries: bfloat16 [2048, 8192], P('ctx', 'head'), may hold values from -5.5 to 5.5
- keys: bfloat16 [2048, 1024], P('ctx', 'head'), may hold values from -5.5 to 5.5
- values: bfloat16 [2048, 1024], P('ctx', 'head'), may hold values from -6 to 6
- feature_weights: bfloat16 [64, 128, 64], P('head'), may hold values from -1 to 1
Outputs:
- attn_error: float32 [2048, 8192], P('ctx', 'head')
- loss: float32 [], replicated
- grad_w: float32 [64, 128, 64], P('head')
All inputs are finite; a program needn't handle non-finite values.
Results may differ from a plain program's by a relative error of at most 0.004.
Values may be sent and summed in bfloat16 or wider, within the bound.
No kernel may reach another device: no remote copies, remote signals or barrier semaphores. Data moves between devices by JAX's collectives and lax.ppermute only.
A program may use at most 192 MiB of HBM per device.

v0:
```python
import math

import jax
import jax.numpy as jnp
from jax import lax
from jax.sharding import PartitionSpec as P

HEAD_SIZE = 128
QUERY_HEADS = 64
KEY_VALUE_HEADS = 8
FM = 64
WIN = 64


phi_scale = 0.00390625
big_negative = -1e30
highest = lax.Precision.HIGHEST


def swapped(value, axis, distance):
    mask = 2**distance
    pairs = [(source, source ^ mask) for source in range(lax.axis_size(axis))]
    return lax.ppermute(value, axis, pairs)


def carried_in(value, axis, combine, identity):
    devices, here = (lax.axis_size(axis), lax.axis_index(axis))
    everything = jax.tree.map(
        lambda part, kind: lax.all_gather(part.astype(kind), axis),
        value,
        (jnp.bfloat16, jnp.bfloat16),
    )
    start = jax.tree.map(
        lambda part, zero: jnp.broadcast_to(jnp.asarray(zero, part.dtype), part.shape),
        value,
        identity,
    )

    def carried_step(k, before):
        reached = k < here
        new = combine(
            before, jax.tree.map(lambda part, own: part[k].astype(own.dtype), everything, value)
        )
        return jax.tree.map(lambda a, b: jnp.where(reached, a, b), new, before)

    return lax.fori_loop(0, devices, carried_step, start)


def prefix(value, axis, combine, identity):
    devices, here = (lax.axis_size(axis), lax.axis_index(axis))
    everything = jax.tree.map(
        lambda part, kind: lax.all_gather(part.astype(kind), axis),
        value,
        jax.tree.map(lambda a: jnp.bfloat16 if a.dtype == jnp.float32 else a.dtype, value),
    )
    start = jax.tree.map(
        lambda part, zero: jnp.broadcast_to(jnp.asarray(zero, part.dtype), part.shape),
        value,
        identity,
    )

    def prefix_step(k, before):
        at = devices - 1 - k
        reached = at > here
        new = combine(
            before, jax.tree.map(lambda part, own: part[at].astype(own.dtype), everything, value)
        )
        return jax.tree.map(lambda a, b: jnp.where(reached, a, b), new, before)

    return lax.fori_loop(0, devices, prefix_step, start)


def features(projection):
    return phi_scale * jnp.concatenate(
        [1.0 + jax.nn.elu(projection), 1.0 + jax.nn.elu(-projection)], axis=-1
    )


def feature_back(projection, grad_phi):
    half = projection.shape[-1]
    slope_plus = jnp.where(projection > 0, 1.0, jnp.exp(jnp.minimum(projection, 0.0)))
    slope_minus = jnp.where(projection < 0, 1.0, jnp.exp(jnp.minimum(-projection, 0.0)))
    return phi_scale * (grad_phi[..., :half] * slope_plus - grad_phi[..., half:] * slope_minus)


def add_pair(earlier, later):
    return (earlier[0] + later[0], earlier[1] + later[1])


def split_product(form, phi_part, data):
    upper = phi_part.astype(jnp.bfloat16)
    lower = (phi_part - upper.astype(jnp.float32)).astype(jnp.bfloat16)
    return jnp.einsum(form, upper, data, preferred_element_type=jnp.float32) + jnp.einsum(
        form, lower, data, preferred_element_type=jnp.float32
    )


def visit_partner(rows):
    for bit_index in range(lax.axis_size("ctx").bit_length() - 1):
        rows = swapped(rows, "ctx", bit_index)
    return rows


def return_partner(rows):
    for bit_index in range(lax.axis_size("ctx").bit_length() - 1):
        rows = swapped(rows.astype(jnp.bfloat16), "ctx", bit_index).astype(rows.dtype)
    return rows


def teacher_part(part, query_set, pos_set, key_block, value_block, key_pos, masked):
    scale_factor = 1.0 / math.sqrt(query_set.shape[-1])
    scores = (
        jnp.einsum("qgrd,kgd->grqk", query_set, key_block, preferred_element_type=jnp.float32)
        * scale_factor
    )
    if masked:
        causal = key_pos[None, :] <= pos_set[:, None]
        top = jnp.maximum(part[0], jnp.max(jnp.where(causal, scores, big_negative), axis=-1))
        weights = jnp.exp(jnp.where(causal, scores - top[..., None], big_negative))
    else:
        top = jnp.maximum(part[0], jnp.max(scores, axis=-1))
        weights = jnp.exp(scores - top[..., None])
    rescale = jnp.exp(part[0] - top)
    total = part[1] * rescale + jnp.sum(weights, axis=-1)
    mixed = part[2] * rescale[..., None] + jnp.einsum(
        "grqk,kgd->grqd",
        weights.astype(jnp.bfloat16),
        value_block,
        preferred_element_type=jnp.float32,
    )
    return (top, total, mixed)


def advance(part, row_set, key_block, value_block, key_pos, first):
    query_set, pos_set = row_set
    needed = first <= pos_set[-1]
    straddle = key_pos[-1] > pos_set[0]
    branch_index = jnp.where(needed, jnp.where(straddle, 2, 1), 0).astype(jnp.int32)
    return lax.switch(
        branch_index,
        [
            lambda current: current,
            lambda current: teacher_part(
                current, query_set, pos_set, key_block, value_block, key_pos, False
            ),
            lambda current: teacher_part(
                current, query_set, pos_set, key_block, value_block, key_pos, True
            ),
        ],
        part,
    )


def shards(queries, keys, values, feature_weights):
    local_rows = queries.shape[0]
    half_rows = local_rows // 2
    groups = keys.shape[1] // HEAD_SIZE
    group_ratio = QUERY_HEADS // KEY_VALUE_HEADS
    heads_here = groups * group_ratio
    ctx_count = lax.axis_size("ctx")
    ctx_place = lax.axis_index("ctx")
    own_start = ctx_place * local_rows
    query4 = queries.reshape(local_rows, groups, group_ratio, HEAD_SIZE)
    own_keys = keys.reshape(local_rows, groups, HEAD_SIZE)
    own_values = values.reshape(local_rows, groups, HEAD_SIZE)
    weight4 = feature_weights.reshape(groups, group_ratio, HEAD_SIZE, FM)
    scale = 1.0 / math.sqrt(HEAD_SIZE)
    query_pos = own_start + jnp.arange(local_rows, dtype=jnp.int32)
    tail_offsets = jnp.arange(WIN, dtype=jnp.int32)
    proj_own = jnp.einsum("kgd,grdf->grkf", own_keys, weight4, preferred_element_type=jnp.float32)
    first_set = (query4[:half_rows], query_pos[:half_rows])
    partner_start = (ctx_count - 1 - ctx_place) * local_rows
    visiting = visit_partner(query4[half_rows:])
    second_set = (visiting, partner_start + half_rows + jnp.arange(half_rows, dtype=jnp.int32))
    row_sets = (first_set, second_set)

    def add_tail(tails, key_block, value_block, key_pos):
        pick = (key_pos[None, :] == own_start - WIN + tail_offsets[:, None]).astype(jnp.bfloat16)
        return (
            tails[0]
            + jnp.einsum("wk,kgd->wgd", pick, key_block, preferred_element_type=jnp.float32),
            tails[1]
            + jnp.einsum("wk,kgd->wgd", pick, value_block, preferred_element_type=jnp.float32),
        )

    part_zero = (
        jnp.full((groups, group_ratio, half_rows), big_negative, jnp.float32),
        jnp.zeros((groups, group_ratio, half_rows), jnp.float32),
        jnp.zeros((groups, group_ratio, half_rows, HEAD_SIZE), jnp.float32),
    )
    tail_zero = (
        jnp.zeros((WIN, groups, HEAD_SIZE), jnp.float32),
        jnp.zeros((WIN, groups, HEAD_SIZE), jnp.float32),
    )
    state_zero = (
        jnp.zeros((groups, group_ratio, 2 * FM, HEAD_SIZE), jnp.float32),
        jnp.zeros((groups, group_ratio, 2 * FM), jnp.float32),
    )
    carry = ((part_zero, part_zero), tail_zero, ())
    key_piece = lax.all_gather(keys, "ctx", axis=0, tiled=True)
    value_piece = lax.all_gather(values, "ctx", axis=0, tiled=True)
    piece_rows = key_piece.shape[0]
    stride = math.gcd(piece_rows, local_rows)
    count = piece_rows // stride
    key_blocks = key_piece.reshape(count, stride, groups, HEAD_SIZE)
    value_blocks = value_piece.reshape(count, stride, groups, HEAD_SIZE)

    def fold_step(state, inputs):
        key_block, value_block, number = inputs
        first = number * stride
        key_pos = first + jnp.arange(stride, dtype=jnp.int32)
        parts_now, tails_now, states_now = state
        new_parts = (
            advance(parts_now[0], row_sets[0], key_block, value_block, key_pos, first),
            advance(parts_now[1], row_sets[1], key_block, value_block, key_pos, first),
        )
        earlier_block = first < own_start
        new_tails = lax.cond(
            earlier_block,
            lambda current: add_tail(current, key_block, value_block, key_pos),
            lambda current: current,
            tails_now,
        )
        return ((new_parts, new_tails, states_now), None)

    carry, unused = lax.scan(
        fold_step, carry, (key_blocks, value_blocks, jnp.arange(count, dtype=jnp.int32))
    )
    phi_own = features(proj_own)
    local_kv = split_product("grkf,kgd->grfd", phi_own, own_values)
    state_kv, state_norm = carried_in(
        (local_kv, jnp.sum(phi_own, axis=2)), "ctx", add_pair, state_zero
    )
    parts_done, tails_done = (carry[0], carry[1])
    teacher_first = parts_done[0][2] / parts_done[0][1][..., None]
    teacher_second = parts_done[1][2] / parts_done[1][1][..., None]
    teacher_second = return_partner(teacher_second)
    teacher = jnp.concatenate([teacher_first, teacher_second], axis=2)
    tail_key = tails_done[0].astype(jnp.bfloat16)
    tail_value = tails_done[1].astype(jnp.bfloat16)
    slab_key = jnp.concatenate([tail_key, own_keys], axis=0)
    slab_value = jnp.concatenate([tail_value, own_values], axis=0).astype(jnp.float32)
    slab_rows = WIN + local_rows
    slab_pos = own_start - WIN + jnp.arange(slab_rows, dtype=jnp.int32)
    is_tail = jnp.arange(slab_rows, dtype=jnp.int32) < WIN
    proj_tail = jnp.einsum("kgd,grdf->grkf", tail_key, weight4, preferred_element_type=jnp.float32)
    proj_slab = jnp.concatenate([proj_tail, proj_own], axis=2)
    phi_slab = features(proj_slab)
    proj_query = jnp.einsum("qgrd,grdf->grqf", query4, weight4, preferred_element_type=jnp.float32)
    phi_query = features(proj_query)
    scores = (
        jnp.einsum("qgrd,kgd->grqk", query4, slab_key, preferred_element_type=jnp.float32) * scale
    )
    window = (
        (slab_pos[None, :] >= query_pos[:, None] - WIN)
        & (slab_pos[None, :] <= query_pos[:, None])
        & (slab_pos[None, :] >= 0)
    )
    far = jnp.logical_not(is_tail)[None, :] & (slab_pos[None, :] < query_pos[:, None] - WIN)
    coefficient = far.astype(jnp.float32) - (window & is_tail[None, :]).astype(jnp.float32)
    window_top = jnp.max(jnp.where(window, scores, big_negative), axis=-1)
    local = jnp.exp(jnp.where(window, scores - window_top[..., None], big_negative))
    kernel = jnp.einsum("grqf,grkf->grqk", phi_query, phi_slab, precision=highest)
    mixed = local + coefficient * kernel
    numerator = jnp.einsum("grqk,kgd->grqd", mixed, slab_value, precision=highest) + jnp.einsum(
        "grqf,grfd->grqd", phi_query, state_kv, precision=highest
    )
    denominator = jnp.sum(mixed, axis=-1) + jnp.einsum(
        "grqf,grf->grq", phi_query, state_norm, precision=highest
    )
    student = numerator / denominator[..., None]
    error = student - teacher
    attn_error = jnp.transpose(error, (2, 0, 1, 3)).reshape(local_rows, heads_here * HEAD_SIZE)
    whole_rows = local_rows * ctx_count
    loss = lax.psum(jnp.sum(error * error), ("ctx", "head")) / (whole_rows * QUERY_HEADS)
    grad_out = 2.0 * error / denominator[..., None]
    grad_den = -jnp.sum(grad_out * student, axis=-1)
    later_kv = jnp.einsum("grqf,grqd->grfd", phi_query, grad_out, precision=highest)
    later_norm = jnp.einsum("grqf,grq->grf", phi_query, grad_den, precision=highest)
    suffix_kv, suffix_norm = prefix((later_kv, later_norm), "ctx", add_pair, state_zero)
    grad_lin = coefficient * (
        jnp.einsum("grqd,kgd->grqk", grad_out, slab_value, precision=highest) + grad_den[..., None]
    )
    grad_phi_query = (
        jnp.einsum("grqk,grkf->grqf", grad_lin, phi_slab, precision=highest)
        + jnp.einsum("grqd,grfd->grqf", grad_out, state_kv, precision=highest)
        + grad_den[..., None] * state_norm[:, :, None, :]
    )
    grad_phi_slab = jnp.einsum("grqk,grqf->grkf", grad_lin, phi_query, precision=highest)
    own_extra = (
        jnp.einsum("kgd,grfd->grkf", own_values.astype(jnp.float32), suffix_kv, precision=highest)
        + suffix_norm[:, :, None, :]
    )
    grad_phi_slab = grad_phi_slab + jnp.concatenate(
        [jnp.zeros((groups, group_ratio, WIN, 2 * FM), jnp.float32), own_extra], axis=2
    )
    grad_proj_query = feature_back(proj_query, grad_phi_query)
    grad_proj_slab = feature_back(proj_slab, grad_phi_slab)
    grad_local = jnp.einsum(
        "qgrd,grqf->grdf", query4.astype(jnp.float32), grad_proj_query, precision=highest
    ) + jnp.einsum(
        "kgd,grkf->grdf", slab_key.astype(jnp.float32), grad_proj_slab, precision=highest
    )
    grad_w = lax.psum(grad_local.reshape(heads_here, HEAD_SIZE, FM), "ctx")
    return (attn_error, loss, grad_w)


def solution(mesh):
    placed = (P("ctx", "head"), P("ctx", "head"), P("ctx", "head"), P("head", None, None))
    return jax.shard_map(
        shards,
        mesh=mesh,
        in_specs=placed,
        out_specs=(P("ctx", "head"), P(), P("head", None, None)),
        check_vma=False,
    )
```

profile of v0, /device:TPU:0, one launch (start us, length us, event | category | flops | bytes accessed | tf_op | source)
XLA Modules:
  0.0 783.7 jit_solution(9861084651910707477)
XLA Ops:
  25.6 4.3 fusion.116
  29.9 8.6 %collective-permute-done.1 = bf16[64,4,8,128]{3,2,1,0:T(8,128)(2,1)} collective-permute-done((bf16[64,4,8,128]{3,2,1,0:T(8,128)(2,1)}, bf16[64,4,8,128]{3,2,1,0:T(8,128)(2,1)}, u32[]{:S(2)}, u32[]{:S(2)}) %collective-permute-start.1) | collective-permute-done | bytes 524320 | tf_op jit(solution)/shard_map/ppermute | solution.py:23
  40.3 5.5 fusion.79
  45.8 13.8 %collective-permute-done.2 = bf16[64,4,8,128]{3,2,1,0:T(8,128)(2,1)} collective-permute-done((bf16[64,4,8,128]{3,2,1,0:T(8,128)(2,1)}, bf16[64,4,8,128]{3,2,1,0:T(8,128)(2,1)}, u32[]{:S(2)}, u32[]{:S(2)}) %collective-permute-start.2) | collective-permute-done | bytes 524320 | tf_op jit(solution)/shard_map/ppermute | solution.py:23
  64.5 4.3 maximum_multiply_fusion.1
  68.9 20.4 %collective-permute-done.3 = bf16[64,4,8,128]{3,2,1,0:T(8,128)(2,1)} collective-permute-done((bf16[64,4,8,128]{3,2,1,0:T(8,128)(2,1)}, bf16[64,4,8,128]{3,2,1,0:T(8,128)(2,1)}, u32[]{:S(2)}, u32[]{:S(2)}) %collective-permute-start.3) | collective-permute-done | bytes 524320 | tf_op jit(solution)/shard_map/ppermute | solution.py:23
  91.4 4.1 reshape.276
  95.5 16.6 %all-gather.11.cloned.1.call-done = bf16[2048,512]{1,0:T(8,128)(2,1)} async-done(((bf16[128,512]{1,0:T(8,128)(2,1)}), bf16[2048,512]{1,0:T(8,128)(2,1)}) %all-gather.11.cloned.1.call-update) | async-done | bytes 2097168 | tf_op jit(solution)/shard_map/all_gather | solution.py:201
  112.2 4.0 reshape.277
  118.3 193.6 %while.59 = (s32[]{:T(128)}, f32[4,8,64]{2,1,0:T(8,128)S(1)}, f32[4,8,64]{2,1,0:T(8,128)S(1)}, f32[4,8,64,128]{3,2,1,0:T(8,128)S(1)}, f32[4,8,64]{2,1,0:T(8,128)...) while((s32[]{:T(128)}, f32[4,8,64]{2,1,0:T(8,128)S(1)}, ...), condition=%wide.region_17.18_spmd.clone, body=%wide.region_0.17_spmd.clone.sunk | while | flops 291086528 | bytes 14226523 | solution.py:226
  124.5 3.4 conditional.10
  138.9 3.4 conditional.10
  150.8 3.4 conditional.10
  162.7 3.4 conditional.10
  174.7 3.4 conditional.10
  186.6 3.4 conditional.10
  198.5 3.4 conditional.10
  210.5 3.4 conditional.10
  222.4 3.4 conditional.10
  234.3 3.4 conditional.10
  246.3 3.4 conditional.10
  258.2 3.4 conditional.10
  282.1 3.4 conditional.10
  294.0 3.4 conditional.10
  305.9 3.5 conditional.10
  313.0 3.5 collective-permute-start.4
  316.5 64.2 %all-gather.1 = bf16[64,8,128]{2,1,0:T(8,128)(2,1)} all-gather(bf16[4,8,128]{2,1,0:T(8,128)(2,1)S(1)} %fusion.143), channel_id=3, replica_groups=mesh['ctx'=16,'head'=2] {'ctx'}, dimensions={0}, use_global_device_ids=true | all-gather | bytes 139264 | tf_op jit(solution)/shard_map/all_gather | solution.py:29
  384.7 4.6 fusion.46
  389.3 4.7 fusion.109
  394.0 4.8 collective-permute-done.5
  401.1 11.1 %collective-permute-done.6 = bf16[4,8,64,128]{3,2,1,0:T(8,128)(2,1)S(1)} collective-permute-done((bf16[4,8,64,128]{3,2,1,0:T(8,128)(2,1)S(1)}, bf16[4,8,64,128]{3,2,1,0:T(8,128)(2,1)S(1)}, u32[]{:S(2)}, u32[]{:S(2)}) %collective-permute-start.6) | collective-permute-done | bytes 524320 | tf_op jit(solution)/shard_map/ppermute | solution.py:23
  413.6 4.9 fusion.122
  418.5 18.3 %collective-permute-done.7 = bf16[4,8,64,128]{3,2,1,0:T(8,128)(2,1)S(1)} collective-permute-done((bf16[4,8,64,128]{3,2,1,0:T(8,128)(2,1)S(1)}, bf16[4,8,64,128]{3,2,1,0:T(8,128)(2,1)S(1)}, u32[]{:S(2)}, u32[]{:S(2)}) %collective-permute-start.7) | collective-permute-done | bytes 524320 | tf_op jit(solution)/shard_map/ppermute | solution.py:23
  437.9 49.1 %while.60 = (s32[]{:T(128)}, f32[4,8,128,128]{3,2,1,0:T(8,128)S(1)}, f32[4,8,128]{2,1,0:T(8,128)S(1)}, s32[]{:T(128)}, bf16[16,4,8,128,128]{4,3,2,1,0:T(8,128)(2...) while((s32[]{:T(128)}, f32[4,8,128,128]{3,2,1,0:T(8,128)S(1)}, ...), condition=%wide.region_21.22_spmd.clone, body=%wide.region_20.21_spmd.clone.sunk | while | flops 2113540 | bytes 5283955 | solution.py:46
  487.0 5.7 fusion.150
  492.7 6.4 multiply_reduce_fusion
  500.4 4.6 convolution_convert_fusion
  505.6 3.6 fusion.151
  509.2 19.3 %all-gather.3 = bf16[64,8,128]{2,1,0:T(8,128)(2,1)S(1)} all-gather(bf16[4,8,128]{2,1,0:T(8,128)(2,1)S(1)} %convert_element_type.142), channel_id=5, replica_groups=mesh['ctx'=16,'head'=2] {'ctx'}, dimensions={0}, use_global_device_ids=true | all-gather | bytes 139264 | tf_op jit(solution)/shard_map/all_gather | solution.py:52
  531.8 7.9 %fusion.68 = f32[4,8,128,128]{3,2,1,0:T(8,128)S(1)} fusion(f32[4,8,128,192]{2,3,1,0:T(8,128)S(1)} %fusion.121, f32[4,8,128]{2,1,0:T(8,128)S(1)} %neg.21, f32[128,192]{0,1:T(8,128)S(1)} %convert_subtract_fusion, f32[4,8,192,64]{3,2,1,0:T(8,128)S(1)} %copy-done.11, f32[4,8,192,64]{3,2,1,0:T(8,128)S(1)} %copy-done.9), kind=kOutput, calls=%fused_computation.116 | convolution fusion | flops 1211105280 | bytes 8503296 | tf_op jit(solution)/shard_map/grqk,grkf->grqf/dot_general | solution.py:285
  539.8 4.7 multiply_add_fusion.4
  544.5 4.5 fusion.83
  549.1 81.6 %all-gather.15.cloned.1.call-done = bf16[64,8,128,128]{3,2,1,0:T(8,128)(2,1)} async-done(((bf16[4,8,128,128]{3,2,1,0:T(8,128)(2,1)}), bf16[64,8,128,128]{3,2,1,0:T(8,128)(2,1)}) %all-gather.15.cloned.1.call-update) | async-done | bytes 16777232 | tf_op jit(solution)/shard_map/all_gather | solution.py:52
  630.6 38.6 %while.61 = (s32[]{:T(128)}, f32[4,8,128,128]{3,2,1,0:T(8,128)S(1)}, f32[4,8,128]{2,1,0:T(8,128)S(1)}, s32[]{:T(128)}, bf16[16,4,8,128,128]{4,3,2,1,0:T(8,128)(2...) while((s32[]{:T(128)}, ...), condition=%wide.region_27.28_spmd.clone, body=%wide.region_26.27_spmd.clone.sunk | while | flops 2113544 | bytes 5284017 | solution.py:70
  670.8 5.7 pad_add_fusion
  676.6 5.3 fusion.102
  681.9 39.0 %psum.14 = f32[]{:T(128)} all-reduce(f32[]{:T(128)} %get-tuple-element.673), channel_id=1, replica_groups=mesh['ctx'=16,'head'=2] {'ctx','head'}, use_global_device_ids=true, to_apply=%region_24.25 | all-reduce | flops 1 | bytes 8 | tf_op jit(solution)/shard_map/psum | solution.py:275
  725.3 48.2 %all-reduce.3.cloned.1.call-done = f32[32,128,64]{1,2,0:T(8,128)} async-done(((f32[32,128,64]{1,2,0:T(8,128)}), f32[32,128,64]{1,2,0:T(8,128)}) %all-reduce.3.cloned.1.call-update) | async-done | bytes 1048592 | tf_op jit(solution)/shard_map/psum | solution.py:304
  (467 shorter events, 266.5 us)
Async XLA Ops:
  7.2 3.6 copy-start
  7.2 84.2 %all-gather.9.cloned.1.call-start = ((), (), s32[]{:S(2)}) async-start(), calls=%async_computation | async-start | bytes 2228224 | tf_op jit(solution)/shard_map/all_gather | solution.py:200
  7.9 104.2 %all-gather.11.cloned.1.call-start = ((), (), s32[]{:S(2)}) async-start(), calls=%async_computation.1 | async-start | bytes 2228224 | tf_op jit(solution)/shard_map/all_gather | solution.py:201
  8.7 429.2 %all-gather.13.cloned.1.call-start = ((), (), s32[]{:S(2)}) async-start(), calls=%async_computation.3 | async-start | bytes 17825792 | tf_op jit(solution)/shard_map/all_gather | solution.py:29
  10.8 53.0 %copy-start.22 = (bf16[128,512]{0,1:T(8,128)(2,1)}, bf16[128,512]{0,1:T(8,128)(2,1)S(1)}, u32[]{:S(2)}) copy-start(bf16[128,512]{0,1:T(8,128)(2,1)S(1)} %copy.138) | copy-start | bytes 393220
  14.1 1.4 copy-start.13
  17.9 612.7 %all-gather.15.cloned.1.call-start = ((), (), s32[]{:S(2)}) async-start(), calls=%async_computation.4 | async-start | bytes 17825792 | tf_op jit(solution)/shard_map/all_gather | solution.py:52
  20.1 2.9 collective-permute-start
  23.1 15.4 %collective-permute-start.1 = (bf16[64,4,8,128]{3,2,1,0:T(8,128)(2,1)}, bf16[64,4,8,128]{3,2,1,0:T(8,128)(2,1)}, u32[]{:S(2)}, u32[]{:S(2)}) collective-permute-start(bf16[64,4,8,128]{3,2,1,0:T(8,128)(2,1)} %collective-permute-done), channel_id=1, source_target_pairs={{0,4},{2,6},{4,0},{6,2},{8,12},{10,14},{12,8},{14,10},{16,20},{18,... | collective-permute-start | bytes 1572872 | tf_op jit(solution)/shard_map/ppermute | solution.py:23
  29.9 16.0 %copy-start.28 = (u8[4,128,64]{2,1,0:T(8,128)(4,1)}, u8[4,128,64]{2,1,0:T(8,128)(4,1)S(1)}, u32[]{:S(2)}) copy-start(u8[4,128,64]{2,1,0:T(8,128)(4,1)S(1)} %get-tuple-element.671) | copy-start | bytes 98308
  38.5 21.1 %collective-permute-start.2 = (bf16[64,4,8,128]{3,2,1,0:T(8,128)(2,1)}, bf16[64,4,8,128]{3,2,1,0:T(8,128)(2,1)}, u32[]{:S(2)}, u32[]{:S(2)}) collective-permute-start(bf16[64,4,8,128]{3,2,1,0:T(8,128)(2,1)} %collective-permute-done.1), channel_id=1, source_target_pairs={{0,8},{2,10},{4,12},{6,14},{8,0},{10,2},{12,4},{14,6},{16,24},{18,... | collective-permute-start | bytes 1572872 | tf_op jit(solution)/shard_map/ppermute | solution.py:23
  40.3 21.7 %copy-start.14 = (f32[4,8,128,64]{3,2,1,0:T(8,128)S(1)}, f32[4,8,128,64]{3,2,1,0:T(8,128)}, u32[]{:S(2)}) copy-start(f32[4,8,128,64]{3,2,1,0:T(8,128)} %copy-done.13) | copy-start | bytes 3145732
  59.6 29.8 %collective-permute-start.3 = (bf16[64,4,8,128]{3,2,1,0:T(8,128)(2,1)}, bf16[64,4,8,128]{3,2,1,0:T(8,128)(2,1)}, u32[]{:S(2)}, u32[]{:S(2)}) collective-permute-start(bf16[64,4,8,128]{3,2,1,0:T(8,128)(2,1)} %collective-permute-done.2), channel_id=1, source_target_pairs={{0,16},{2,18},{4,20},{6,22},{8,24},{10,26},{12,28},{14,30},{16,0},... | collective-permute-start | bytes 1572872 | tf_op jit(solution)/shard_map/ppermute | solution.py:23
  313.0 71.6 %collective-permute-start.4 = (bf16[4,8,64,128]{3,2,1,0:T(8,128)(2,1)}, bf16[4,8,64,128]{3,2,1,0:T(8,128)(2,1)S(1)}, u32[]{:S(2)}, u32[]{:S(2)}) collective-permute-start(bf16[4,8,64,128]{3,2,1,0:T(8,128)(2,1)} %divide_convert_fusion), channel_id=1, source_target_pairs={{0,2},{2,0},{4,6},{6,4},{8,10},{10,8},{12,14},{14,12},{16,18},{18,... | collective-permute-start | bytes 1572872 | tf_op jit(solution)/shard_map/ppermute | solution.py:23
  384.6 4.7 copy-start.18
  384.6 14.2 %collective-permute-start.5 = (bf16[4,8,64,128]{3,2,1,0:T(8,128)(2,1)S(1)}, bf16[4,8,64,128]{3,2,1,0:T(8,128)(2,1)S(1)}, u32[]{:S(2)}, u32[]{:S(2)}) collective-permute-start(bf16[4,8,64,128]{3,2,1,0:T(8,128)(2,1)S(1)} %collective-permute-done.4), channel_id=1, source_target_pairs={{0,4},{2,6},{4,0},{6,2},{8,12},{10,14},{12,8},{14,10},{16,20},{18,... | collective-permute-start | bytes 1572872 | tf_op jit(solution)/shard_map/ppermute | solution.py:23
  384.7 4.6 copy-start.5
  389.3 4.7 copy-start.8
  389.3 4.7 copy-start.10
  389.3 9.6 %copy-start.20 = (bf16[16,8,32,128]{3,2,1,0:T(8,128)(2,1)S(1)}, bf16[16,8,32,128]{3,2,1,0:T(8,128)(2,1)}, u32[]{:S(2)}) copy-start(bf16[16,8,32,128]{3,2,1,0:T(8,128)(2,1)} %copy.204) | copy-start | bytes 3145732
  389.3 9.6 %copy-start.27 = (bf16[128,4,128]{2,0,1:T(8,128)(2,1)S(1)}, bf16[128,4,128]{2,0,1:T(8,128)(2,1)}, u32[]{:S(2)}) copy-start(bf16[128,4,128]{2,0,1:T(8,128)(2,1)} %copy.128) | copy-start | bytes 393220
  394.0 5.5 copy-start.17
  398.8 13.4 %collective-permute-start.6 = (bf16[4,8,64,128]{3,2,1,0:T(8,128)(2,1)S(1)}, bf16[4,8,64,128]{3,2,1,0:T(8,128)(2,1)S(1)}, u32[]{:S(2)}, u32[]{:S(2)}) collective-permute-start(bf16[4,8,64,128]{3,2,1,0:T(8,128)(2,1)S(1)} %collective-permute-done.5), channel_id=1, source_target_pairs={{0,8},{2,10},{4,12},{6,14},{8,0},{10,2},{12,4},{14,6},{16,24},{18,... | collective-permute-start | bytes 1572872 | tf_op jit(solution)/shard_map/ppermute | solution.py:23
  401.1 12.4 %copy-start.26 = (bf16[128,4,128]{2,0,1:T(8,128)(2,1)S(1)}, bf16[128,4,128]{2,0,1:T(8,128)(2,1)}, u32[]{:S(2)}) copy-start(bf16[128,4,128]{2,0,1:T(8,128)(2,1)} %copy.139) | copy-start | bytes 393220
  412.2 24.6 %collective-permute-start.7 = (bf16[4,8,64,128]{3,2,1,0:T(8,128)(2,1)S(1)}, bf16[4,8,64,128]{3,2,1,0:T(8,128)(2,1)S(1)}, u32[]{:S(2)}, u32[]{:S(2)}) collective-permute-start(bf16[4,8,64,128]{3,2,1,0:T(8,128)(2,1)S(1)} %collective-permute-done.6), channel_id=1, source_target_pairs={{0,16},{2,18},{4,20},{6,22},{8,24},{10,26},{12,28},{14,30},{16,0},... | collective-permute-start | bytes 1572872 | tf_op jit(solution)/shard_map/ppermute | solution.py:23
  413.6 24.3 %copy-start.2 = (f32[4,8,128,128]{3,2,1,0:T(8,128)S(1)}, f32[4,8,128,128]{3,2,1,0:T(8,128)}, u32[]{:S(2)}) copy-start(f32[4,8,128,128]{3,2,1,0:T(8,128)} %custom-call) | copy-start | bytes 6291460
  487.0 12.1 %copy-start.3 = (f32[4,8,128,128]{3,2,1,0:T(8,128)}, f32[4,8,128,128]{3,2,1,0:T(8,128)S(1)}, u32[]{:S(2)}) copy-start(f32[4,8,128,128]{3,2,1,0:T(8,128)S(1)} %get-tuple-element.496) | copy-start | bytes 6291460
  487.0 5.8 copy-start.6
  499.1 1.3 copy-start.15
  500.4 4.7 copy-start.30
  505.1 268.4 %all-reduce.3.cloned.1.call-start = ((), (), s32[]{:S(2)}) async-start(), calls=%async_computation.2 | async-start | bytes 2097152 | tf_op jit(solution)/shard_map/psum | solution.py:304
  505.6 26.2 %copy-start.11 = (f32[4,8,192,64]{3,2,1,0:T(8,128)S(1)}, f32[4,8,192,64]{3,2,1,0:T(8,128)}, u32[]{:S(2)}) copy-start(f32[4,8,192,64]{3,2,1,0:T(8,128)} %copy-done.10) | copy-start | bytes 4718596
  528.5 3.3 copy-start.9
  531.8 7.9 %copy-start.12 = (f32[4,8,128,192]{2,3,1,0:T(8,128)}, f32[4,8,128,192]{2,3,1,0:T(8,128)S(1)}, u32[]{:S(2)}) copy-start(f32[4,8,128,192]{2,3,1,0:T(8,128)S(1)} %fusion.121) | copy-start | bytes 9437188
  531.8 7.9 %copy-start.4 = (f32[4,8,128,128]{3,2,1,0:T(8,128)S(1)}, f32[4,8,128,128]{3,2,1,0:T(8,128)}, u32[]{:S(2)}) copy-start(f32[4,8,128,128]{3,2,1,0:T(8,128)} %copy-done.3) | copy-start | bytes 6291460
  531.8 7.9 %copy-start.16 = (f32[4,8,128,128]{3,2,1,0:T(8,128)S(1)}, f32[4,8,128,128]{3,2,1,0:T(8,128)}, u32[]{:S(2)}) copy-start(f32[4,8,128,128]{3,2,1,0:T(8,128)} %copy-done.15) | copy-start | bytes 6291460
  539.7 4.8 copy-start.21
  539.7 4.8 copy-start.24
  539.8 4.8 copy-start.29
  630.6 38.6 %copy-start.23 = (bf16[128,512]{0,1:T(8,128)(2,1)S(1)}, bf16[128,512]{0,1:T(8,128)(2,1)}, u32[]{:S(2)}) copy-start(bf16[128,512]{0,1:T(8,128)(2,1)} %copy-done.22) | copy-start | bytes 393220
  669.2 1.6 copy-start.7
  670.8 5.7 copy-start.19
  670.8 5.8 copy-start.25
  670.8 5.8 copy-start.31
  722.8 53.0 %copy-start.1 = (bf16[32,128,64]{1,2,0:T(8,128)(2,1)S(1)}, bf16[32,128,64]{1,2,0:T(8,128)(2,1)}, u32[]{:S(2)}) copy-start(bf16[32,128,64]{1,2,0:T(8,128)(2,1)} %param.21) | copy-start | bytes 1572868
Sparse Core Ops, SparseCore 0:
  10.2 45.6 all-gather.8
  58.0 54.1 all-gather.10
  114.3 125.7 all-gather.12
  505.2 125.3 all-gather.14
  682.0 91.4 all-reduce.2
where the time goes:
time: 796 us; the launch traced here: 784 us
  waiting for transfers between devices  225 us (28%)
  blocking collectives  123 us (15%)
  matrix products  120 us (15%)
  other arithmetic  120 us (15%)
  local copies, waits for them, and re-layouts  95.9 us (12%)
  loops' own time  72.7 us (9%)
  between operations  16.3 us (2%)
  starting transfers between devices  11 us (1%)
    all_gather x1, waiting for transfers between devices, prefix(): lax.all_gather(part.astype(kind), axis)  81.6 us
    ppermute x8, waiting for transfers between devices, swapped(): return lax.ppermute(value, axis, pairs)  77 us
    another operation x1, loops' own time, shards(): lax.scan(fold_step, carry, (key_blocks, value_blocks, jnp.arange(count, d...  70.5 us
    all_gather x1, blocking collectives, carried_in(): lax.all_gather(part.astype(kind), axis)  64.2 us
    select_n x32, other arithmetic, carried_step(): return jax.tree.map(lambda a, b: jnp.where(reached, a, b), new, before)  49 us
    psum x1, waiting for transfers between devices, shards(): grad_w = lax.psum(grad_local.reshape(heads_here, HEAD_SIZE, FM), 'ctx')  48.2 us
    psum x1, blocking collectives, shards(): lax.psum(jnp.sum(error * error), ('ctx', 'head'))  39 us
    dynamic_slice x64, local copies, waits for them, and re-layouts, shards(): lax.scan(fold_step, carry, (key_blocks, value_blocks, jnp.arange(count, d...  38.7 us
  transfers between devices with their start and end apart: 13, of which 9 were waited for; matrix products, arithmetic and copies ran while one was open for 28% of the time, Pallas kernels for 0%

commit v1 on v0

v1 whole, which is shorter than its diff:
```python
import functools
import math

import jax
import jax.numpy as jnp
from jax import lax
from jax.experimental import pallas as pl
from jax.experimental.pallas import tpu as pltpu
from jax.sharding import PartitionSpec as P

HEAD_SIZE = 128
QUERY_HEADS = 64
KEY_VALUE_HEADS = 8
FM = 64
WIN = 64
RATIO = QUERY_HEADS // KEY_VALUE_HEADS

big_negative = -1e30
SIGMA = 2.0**-16
SCALE = 1.0 / math.sqrt(HEAD_SIZE)
f32 = jnp.float32
bf16 = jnp.bfloat16


def dot(a, b, ca, cb):
    return lax.dot_general(a, b, (((ca,), (cb,)), ((), ())), preferred_element_type=f32)


def key_features(x, heads):
    e = jnp.exp(-jnp.abs(x))
    pos = x > 0
    plus = jnp.where(pos, 1.0 + x, e)
    minus = jnp.where(pos, e, 1.0 - x)
    rows = []
    for h in range(heads):
        rows += [plus[h * FM : (h + 1) * FM], minus[h * FM : (h + 1) * FM]]
    return jnp.concatenate(rows, axis=0)


def key_slopes(x, g, heads):
    e = jnp.exp(-jnp.abs(x))
    pos = x > 0
    plus = jnp.concatenate([g[h * 2 * FM : h * 2 * FM + FM] for h in range(heads)], axis=0)
    minus = jnp.concatenate([g[h * 2 * FM + FM : (h + 1) * 2 * FM] for h in range(heads)], axis=0)
    return jnp.where(pos, plus - minus * e, plus * e - minus)


def kernel(where_ref, q_ref, w_ref, w2_ref, k_ref, v_ref, err_ref, gw_ref, loss_ref,
           qs, m_ref, acc, state, lstate, ln_ref, den_ref, phiq, x2q, phikd, xd, gout):
    rows = q_ref.shape[0]
    R = RATIO * rows
    D = HEAD_SIZE
    start = where_ref[0] * rows
    dbase = pl.multiple_of(jnp.maximum(start - rows, 0), rows)
    span = 2 * rows

    for h in range(RATIO):
        qs[h * rows : (h + 1) * rows, :] = q_ref[:, h * D : (h + 1) * D]
    w = w_ref[...]

    kd = k_ref[pl.ds(dbase, span), :]
    vd = v_ref[pl.ds(dbase, span), :]
    ones = jnp.ones((span, D), bf16)
    vx = jnp.concatenate([vd, ones], axis=1)
    i_pos = start + lax.broadcasted_iota(jnp.int32, (rows, span), 0)
    j_pos = dbase + lax.broadcasted_iota(jnp.int32, (rows, span), 1)
    causal = j_pos <= i_pos
    far = j_pos < i_pos - WIN
    window = jnp.logical_and(causal, jnp.logical_not(far))
    x = dot(w, kd, 1, 1)
    xd[...] = x
    phikd[...] = key_features(x, RATIO).astype(bf16)
    for h in range(RATIO):
        hr = slice(h * rows, (h + 1) * rows)
        hf = slice(h * 2 * FM, (h + 1) * 2 * FM)
        q = qs[hr, :]
        s = dot(q, kd, 1, 1) * SCALE
        sc = jnp.where(causal, s, big_negative)
        top = jnp.max(sc, axis=1, keepdims=True)
        m_ref[hr, :] = jnp.broadcast_to(top, (rows, D))
        p = jnp.exp(sc - top)
        acc[hr, :] = dot(p.astype(bf16), vx, 1, 0)
        sw = jnp.where(window, s, big_negative)
        local = jnp.exp(sw - jnp.max(sw, axis=1, keepdims=True))
        x2 = dot(q, w2_ref[h], 1, 1)
        x2q[hr, :] = x2
        fq = (jnp.where(x2 > 0, 1.0 + x2, jnp.exp(jnp.minimum(x2, 0.0))) * SIGMA).astype(bf16)
        phiq[hr, :] = fq
        lin = dot(fq, phikd[hf, :], 1, 0)
        mixed = jnp.where(far, lin, local)
        den_ref[hr, :] = dot(mixed.astype(bf16), vx, 1, 0)
    state[...] = jnp.zeros_like(state)

    def far_step(j0, n):
        kc = k_ref[pl.ds(j0, n), :]
        vc = jnp.concatenate([v_ref[pl.ds(j0, n), :], jnp.ones((n, D), bf16)], axis=1)
        s = dot(qs[...], kc, 1, 1) * SCALE
        old = m_ref[...]
        new = jnp.maximum(old, jnp.max(s, axis=1, keepdims=True))
        m_ref[...] = new
        a = jnp.exp(old - new)
        p = jnp.exp(s - new[:, :1])
        acc[...] = acc[...] * jnp.concatenate([a, a], axis=1) + dot(p.astype(bf16), vc, 1, 0)
        fk = key_features(dot(w, kc, 1, 1), RATIO).astype(bf16)
        state[...] += dot(fk, vc, 1, 0)

    chunk = 2 * rows
    full = dbase // chunk

    def loop_far(t, c):
        far_step(pl.multiple_of(t * chunk, chunk), chunk)
        return c

    lax.fori_loop(0, full, loop_far, 0)

    @pl.when(dbase > full * chunk)
    def _():
        far_step(pl.multiple_of(full * chunk, chunk), rows)

    lane = lax.broadcasted_iota(jnp.int32, (rows, D), 1)
    lanef = lax.broadcasted_iota(jnp.int32, (2 * FM, D), 1)
    total = jnp.zeros((8, D), f32)
    for h in range(RATIO):
        hr = slice(h * rows, (h + 1) * rows)
        hf = slice(h * 2 * FM, (h + 1) * 2 * FM)
        fq = phiq[hr, :]
        st = state[hf, :]
        sb = st[:, :D].astype(bf16)
        n_hi = st[:, D:].astype(bf16)
        n_lo = (st[:, D:] - n_hi.astype(f32)).astype(bf16)
        sx = jnp.concatenate([sb, n_hi], axis=1)
        nd = den_ref[hr, :] + dot(fq, sx, 1, 0)
        den = nd[:, D:]
        student = nd[:, :D] / den
        teacher = acc[hr, :D] / acc[hr, D:]
        e = student - teacher
        err_ref[:, h * D : (h + 1) * D] = e
        e2 = e * e
        for b in range(rows // 8):
            total = total + e2[b * 8 : (b + 1) * 8]
        go = (2.0 * e / den).astype(bf16)
        gd = -jnp.sum(go.astype(f32) * student, axis=1, keepdims=True)
        gd_hi = gd.astype(bf16).astype(f32)
        gd_lo = gd - gd_hi
        gdx = jnp.where(lane == 1, gd_lo, jnp.where(lane <= 2, gd_hi, 0.0)).astype(bf16)
        gx = jnp.concatenate([go, gdx], axis=1)
        nx = jnp.where(lanef == 2, n_lo.astype(f32), n_hi.astype(f32)).astype(bf16)
        gq = dot(gx, jnp.concatenate([sb, nx], axis=1), 1, 1)
        gl = jnp.where(far, dot(go, vd, 1, 1) + gd, 0.0).astype(bf16)
        gq = gq + dot(gl, phikd[hf, :], 1, 1)
        x2 = x2q[hr, :]
        y = (gq * jnp.where(x2 > 0, 1.0, jnp.exp(jnp.minimum(x2, 0.0))) * SIGMA).astype(bf16)
        gwq = dot(y, qs[hr, :], 0, 0)
        lx = dot(fq, gx, 0, 0)
        lstate[hf, :] = lx[:, :D].astype(bf16)
        ln_ref[hf, :] = jnp.broadcast_to(lx[:, D : D + 1] + lx[:, D + 1 : D + 2], (2 * FM, D))
        gout[hf, :] = dot(fq, gl, 0, 0)
        gw_ref[h * FM : (h + 1) * FM, :] = gwq[:FM] - gwq[FM:]
    loss_ref[...] = total
    gp = key_slopes(xd[...], gout[...], RATIO).astype(bf16)
    gw_ref[...] += dot(gp, kd, 1, 0)

    def back_step(j0, n):
        kc = k_ref[pl.ds(j0, n), :]
        vc = v_ref[pl.ds(j0, n), :]
        g = dot(lstate[...], vc, 1, 1)
        ln = ln_ref[...]
        g = g + (ln if n == D else jnp.concatenate([ln] * (n // D), axis=1))
        gp = key_slopes(dot(w, kc, 1, 1), g, RATIO).astype(bf16)
        gw_ref[...] += dot(gp, kc, 1, 0)

    def loop_back(t, c):
        back_step(pl.multiple_of(t * chunk, chunk), chunk)
        return c

    lax.fori_loop(0, full, loop_back, 0)

    @pl.when(dbase > full * chunk)
    def _():
        back_step(pl.multiple_of(full * chunk, chunk), rows)


def attend(place, queries, weights_t, weights_2, kv):
    rows = queries.shape[0]
    groups = kv.shape[1] // (2 * HEAD_SIZE)
    tokens = kv.shape[0]
    D = HEAD_SIZE
    R = RATIO * rows
    F = RATIO * 2 * FM
    return pl.pallas_call(
        kernel,
        name="attend",
        out_shape=(
            jax.ShapeDtypeStruct(queries.shape, f32),
            jax.ShapeDtypeStruct((groups * RATIO * FM, D), f32),
            jax.ShapeDtypeStruct((groups * 8, D), f32),
        ),
        grid_spec=pltpu.PrefetchScalarGridSpec(
            num_scalar_prefetch=1,
            grid=(groups,),
            in_specs=[
                pl.BlockSpec((rows, RATIO * D), lambda g, p: (0, g)),
                pl.BlockSpec((RATIO * FM, D), lambda g, p: (g, 0)),
                pl.BlockSpec((RATIO, 2 * FM, D), lambda g, p: (g, 0, 0)),
                pl.BlockSpec((tokens, D), lambda g, p: (0, g)),
                pl.BlockSpec((tokens, D), lambda g, p: (0, groups + g)),
            ],
            out_specs=[
                pl.BlockSpec((rows, RATIO * D), lambda g, p: (0, g)),
                pl.BlockSpec((RATIO * FM, D), lambda g, p: (g, 0)),
                pl.BlockSpec((8, D), lambda g, p: (g, 0)),
            ],
            scratch_shapes=[
                pltpu.VMEM((R, D), bf16),
                pltpu.VMEM((R, D), f32),
                pltpu.VMEM((R, 2 * D), f32),
                pltpu.VMEM((F, 2 * D), f32),
                pltpu.VMEM((F, D), bf16),
                pltpu.VMEM((F, D), f32),
                pltpu.VMEM((R, 2 * D), f32),
                pltpu.VMEM((R, 2 * FM), bf16),
                pltpu.VMEM((R, 2 * FM), f32),
                pltpu.VMEM((F, 2 * rows), bf16),
                pltpu.VMEM((RATIO * FM, 2 * rows), f32),
                pltpu.VMEM((F, 2 * rows), f32),
            ],
        ),
        compiler_params=pltpu.CompilerParams(
            dimension_semantics=("arbitrary",), vmem_limit_bytes=58 << 20
        ),
        cost_estimate=pl.CostEstimate(
            flops=groups * R * tokens * D * 10,
            bytes_accessed=tokens * 4 * D * groups + R * groups * D * 8,
            transcendentals=groups * R * tokens,
        ),
    )(place, queries, weights_t, weights_2, kv, kv)


def shards(queries, keys, values, feature_weights):
    heads = feature_weights.shape[0]
    ctx = lax.axis_size("ctx")
    place = jnp.reshape(lax.axis_index("ctx"), (1,)).astype(jnp.int32)
    weights_t = jnp.transpose(feature_weights, (0, 2, 1))
    weights_2 = jnp.concatenate([weights_t, -weights_t], axis=1)
    kv = lax.all_gather(jnp.concatenate([keys, values], axis=1), "ctx", axis=0, tiled=True)
    error, gw, squares = attend(place, queries, weights_t.reshape(heads * FM, HEAD_SIZE), weights_2, kv)
    whole_rows = queries.shape[0] * ctx
    loss = lax.psum(jnp.sum(squares), ("ctx", "head")) / (whole_rows * QUERY_HEADS)
    gw = lax.psum(gw, "ctx")
    grad_w = jnp.transpose(gw.reshape(heads, FM, HEAD_SIZE), (0, 2, 1))
    return (error, loss, grad_w)


def solution(mesh):
    placed = (P("ctx", "head"), P("ctx", "head"), P("ctx", "head"), P("head", None, None))
    return jax.shard_map(
        shards,
        mesh=mesh,
        in_specs=placed,
        out_specs=(P("ctx", "head"), P(), P("head", None, None)),
        check_vma=False,
    )
```

time: 796 us -> 248 us (0.31); the launches traced: 784 us -> 247 us
  matrix products: 120 us -> 0 us
  waiting for transfers between devices: 225 us -> 107 us
  other arithmetic: 120 us -> 5.24 us
  local copies, waits for them, and re-layouts: 95.9 us -> 2.31 us
  loops' own time: 72.7 us -> 0 us
  blocking collectives: 123 us -> 86.4 us
  Pallas kernels: 0 us -> 30.6 us
  starting transfers between devices: 11 us -> 0.08 us
    dot_general x52 -> x0, matrix products: 119 us -> none  [the longest x17 25.4 us: teacher_part(): jnp.einsum('qgrd,kgd->grqk', query_set, key_block, preferred_element_type...]
    select_n x64 -> x0, other arithmetic: 87 us -> none  [the longest x32 49 us: carried_step(): return jax.tree.map(lambda a, b: jnp.where(reached, a, b), new, before)]
    all_gather x2 -> x0, blocking collectives: 83.5 us -> none  [the longest x1 64.2 us: carried_in(): lax.all_gather(part.astype(kind), axis)]
    ppermute x8 -> x0, waiting for transfers between devices: 77 us -> none  [swapped(): return lax.ppermute(value, axis, pairs)]
    another operation x51 -> x0, loops' own time: 72.7 us -> none  [the longest x1 70.5 us: shards(): lax.scan(fold_step, carry, (key_blocks, value_blocks, jnp.arange(count, d...]
    psum x1, blocking collectives: 39 us -> 86.4 us  [shards(): lax.psum(jnp.sum(squares), ('ctx', 'head')) / (whole_rows * QUERY_HEADS)]
    all_gather x4 -> x1, waiting for transfers between devices: 98.2 us -> 52.8 us  [shards(): lax.all_gather(jnp.concatenate([keys, values], axis=1), 'ctx', axis=0, ti...]
    dynamic_slice x64 -> x0, local copies, waits for them, and re-layouts: 38.7 us -> none  [shards(): lax.scan(fold_step, carry, (key_blocks, value_blocks, jnp.arange(count, d...]
  transfers between devices with their start and end apart: 13 -> 2, of which waited for: 9 -> 2; matrix products, arithmetic and copies ran while one was open for 28% -> 1% of each run, Pallas kernels for 0% -> 0%
where the time goes in v1:
time: 248 us; the launch traced here: 247 us
  waiting for transfers between devices  107 us (43%)
  blocking collectives  86.4 us (35%)
  Pallas kernels  30.6 us (12%)
  between operations  15.8 us (6%)
  other arithmetic  5.24 us (2%)
    psum x1, blocking collectives, shards(): lax.psum(jnp.sum(squares), ('ctx', 'head')) / (whole_rows * QUERY_HEADS)  86.4 us
    psum x1, waiting for transfers between devices, shards(): gw = lax.psum(gw, 'ctx')  53.8 us
    all_gather x1, waiting for transfers between devices, shards(): lax.all_gather(jnp.concatenate([keys, values], axis=1), 'ctx', axis=0, ti...  52.8 us
    pallas_call x1, Pallas kernels, attend(): pl.pallas_call(kernel, name='attend', out_shape=(jax.ShapeDtypeStruct(que...  30.6 us
  transfers between devices with their start and end apart: 2, of which 2 were waited for; matrix products, arithmetic and copies ran while one was open for 1% of the time, Pallas kernels for 0%

profile of v1, /device:TPU:0, one launch (start us, length us, event | category | flops | bytes accessed | tf_op | source)
XLA Modules:
  0.0 247.2 jit_solution(16397592225838451255)
XLA Ops:
  7.2 0.0 copy-start
  7.2 0.0 all-gather.2.cloned.1.call-start
  7.2 1.7 pad_maximum_fusion.1
  9.0 0.0 all-gather.2.cloned.1.call-update
  9.0 0.0 all-reduce.2.cloned.1.call-start
  9.0 1.1 bitcast_negate_fusion
  10.2 0.0 copy-done
  10.2 1.1 pad_maximum_fusion.w2_ref
  11.2 52.8 %all-gather.2.cloned.1.call-done.k_ref.v_ref = bf16[2048,1024]{1,0:T(8,128)(2,1)} async-done(((bf16[128,1024]{1,0:T(8,128)(2,1)}), bf16[2048,1024]{1,0:T(8,128)(2,1)}) %all-gather.2.cloned.1.call-update) | async-done | bytes 4194320 | tf_op jit(solution)/shard_map/all_gather | solution.py:245
  64.0 30.6 %attend.1 = (f32[128,4096]{1,0:T(8,128)}, f32[2048,128]{1,0:T(8,128)}, f32[32,128]{1,0:T(8,128)}) custom-call(s32[1]{0:T(128)} %bitcast.where_ref, bf16[128,4096]{1,0:T(8,128)(2,1)} %q_ref.1, bf16[2048,128]{1,0:T(8,128)(2,1)} %bitcast.8, bf16[32,128,128]{2,1,0:T(8,128)(2,1)} %pad_maximum_fusion.w2_ref, ...), custom_call_target="tpu_custom_call" | custom-call | flops 10737418240 | bytes 8388608 | tf_op jit(solution)/shard_map/attend/pallas_call | solution.py:190
  94.7 0.0 all-reduce.2.cloned.1.call-update
  94.7 1.3 reduce_sum.9
  96.0 86.4 %psum.14 = f32[]{:T(128)} all-reduce(f32[]{:T(128)} %reduce_sum.9), channel_id=1, replica_groups=mesh['ctx'=16,'head'=2] {'ctx','head'}, use_global_device_ids=true, to_apply=%region_1.0 | all-reduce | flops 1 | bytes 8 | tf_op jit(solution)/shard_map/psum | solution.py:248
  183.0 53.8 %all-reduce.2.cloned.1.call-done = f32[32,128,64]{1,2,0:T(8,128)} async-done(((f32[32,128,64]{1,2,0:T(8,128)}), f32[32,128,64]{1,2,0:T(8,128)}) %all-reduce.2.cloned.1.call-update) | async-done | bytes 1048592 | tf_op jit(solution)/shard_map/psum | solution.py:249
  236.9 2.3 copy.8
Async XLA Ops:
  7.2 3.0 %copy-start = (bf16[32,128,64]{1,2,0:T(8,128)(2,1)S(1)}, bf16[32,128,64]{1,2,0:T(8,128)(2,1)}, u32[]{:S(2)}) copy-start(bf16[32,128,64]{1,2,0:T(8,128)(2,1)} %param.7) | copy-start | bytes 1572868
  7.2 56.9 %all-gather.2.cloned.1.call-start = ((), (), s32[]{:S(2)}) async-start(), calls=%async_computation | async-start | bytes 4456448 | tf_op jit(solution)/shard_map/all_gather | solution.py:245
  9.0 227.9 %all-reduce.2.cloned.1.call-start = ((), (), s32[]{:S(2)}) async-start(), calls=%async_computation.1 | async-start | bytes 2097152 | tf_op jit(solution)/shard_map/psum | solution.py:249
Sparse Core Ops, SparseCore 0:
  10.7 53.2 all-gather.1
  94.8 142.0 all-reduce.1

commit v2 on v1

v2 whole, which is shorter than its diff:
```python
import functools
import math

import jax
import jax.numpy as jnp
from jax import lax
from jax.experimental import pallas as pl
from jax.experimental.pallas import tpu as pltpu
from jax.sharding import PartitionSpec as P

HEAD_SIZE = 128
QUERY_HEADS = 64
KEY_VALUE_HEADS = 8
FM = 64
WIN = 64
TAIL = 16
RATIO = QUERY_HEADS // KEY_VALUE_HEADS

big_negative = -1e30
SIGMA = 2.0**-16
LOG2E = 1.4426950408889634
SCALE = 1.0 / math.sqrt(HEAD_SIZE)
f32 = jnp.float32
bf16 = jnp.bfloat16


def dot(a, b, ca, cb):
    return lax.dot_general(a, b, (((ca,), (cb,)), ((), ())), preferred_element_type=f32)


def key_features(x, heads):
    e = jnp.exp(-jnp.abs(x))
    pos = x > 0
    one = jnp.ones_like(x)
    plus = jnp.where(pos, one + x, e)
    minus = jnp.where(pos, e, one - x)
    rows = []
    for h in range(heads):
        rows += [plus[h * FM : (h + 1) * FM], minus[h * FM : (h + 1) * FM]]
    return jnp.concatenate(rows, axis=0)


def key_slopes(x, g, heads):
    e = jnp.exp(-jnp.abs(x)).astype(f32)
    pos = x.astype(f32) > 0
    plus = jnp.concatenate([g[h * 2 * FM : h * 2 * FM + FM] for h in range(heads)], axis=0)
    minus = jnp.concatenate([g[h * 2 * FM + FM : (h + 1) * 2 * FM] for h in range(heads)], axis=0)
    return jnp.where(pos, plus - minus * e, plus * e - minus)


def widened(v, other=None):
    return jnp.concatenate([v, jnp.ones_like(v) if other is None else other], axis=1)


def kernel(where_ref, q_ref, w_ref, kv_ref, err_ref, out_ref,
           gw_ref, square, qs, qc, m_ref, acc, state, lsum, lx, xs, phiq, den):
    rows = q_ref.shape[0]
    D = HEAD_SIZE
    block = pl.program_id(0)
    blocks = lsum.shape[0]
    low = pl.multiple_of(where_ref[1], rows)

    def reach(b):
        return pl.multiple_of(jnp.maximum(where_ref[0] + (b - 1) * rows, low), rows)

    start = where_ref[0] + block * rows
    dbase = reach(block)
    span = 2 * rows
    heads = range(RATIO)
    hr = [slice(h * rows, (h + 1) * rows) for h in heads]
    hf = [slice(h * 2 * FM, (h + 1) * 2 * FM) for h in heads]
    hw = [slice(h * FM, (h + 1) * FM) for h in heads]

    for h in heads:
        q = q_ref[:, h * D : (h + 1) * D]
        qs[hr[h], :] = q
        scaled = q.astype(f32) * (SCALE * LOG2E)
        high = scaled.astype(bf16)
        qc[hr[h], :] = widened(high, (scaled - high.astype(f32)).astype(bf16))
    w = w_ref[...]

    kd = kv_ref[pl.ds(dbase, span), :D]
    vd = kv_ref[pl.ds(dbase, span), D:]
    vx = widened(vd)
    i_pos = start + lax.broadcasted_iota(jnp.int32, (rows, span), 0)
    j_pos = dbase + lax.broadcasted_iota(jnp.int32, (rows, span), 1)
    causal = j_pos <= i_pos
    far = j_pos < i_pos - WIN
    window = jnp.logical_and(causal, jnp.logical_not(far))
    xd = dot(w, kd, 1, 1).astype(bf16)
    phikd = key_features(xd, RATIO)
    s = dot(qc[...], widened(kd, kd), 1, 1)
    ps, mixes = [], []
    for h in heads:
        sh = s[hr[h]]
        sc = jnp.where(causal, sh, big_negative)
        top = jnp.max(sc, axis=1, keepdims=True)
        m_ref[hr[h], :] = jnp.broadcast_to(top, (rows, D))
        ps.append(jnp.exp2(sc - top).astype(bf16))
        sw = jnp.where(window, sh, big_negative)
        local = jnp.exp2(sw - jnp.max(sw, axis=1, keepdims=True))
        q = qs[hr[h], :]
        x = dot(q, w[hw[h]], 1, 1).astype(bf16)
        e = jnp.exp(-jnp.abs(x))
        one = jnp.ones_like(x)
        fq = jnp.concatenate([jnp.where(x > 0, one + x, e), jnp.where(x > 0, e, one - x)], axis=1)
        phiq[hr[h], :] = fq * jnp.asarray(SIGMA, bf16)
        lin = dot(phiq[hr[h], :], phikd[hf[h]], 1, 0)
        mixes.append(jnp.where(far, lin, local).astype(bf16))
    acc[...] = dot(jnp.concatenate(ps, axis=0), vx, 1, 0)
    den[...] = dot(jnp.concatenate(mixes, axis=0), vx, 1, 0)

    def teacher_step(j0, n):
        kc = kv_ref[pl.ds(j0, n), :D]
        vc = widened(kv_ref[pl.ds(j0, n), D:])
        s = dot(qc[...], widened(kc, kc), 1, 1)
        old = m_ref[...]
        new = jnp.maximum(old, jnp.max(s, axis=1, keepdims=True))
        m_ref[...] = new
        a = jnp.exp2(old - new)
        p = jnp.exp2(s - jnp.concatenate([new] * (n // D), axis=1)).astype(bf16)
        acc[...] = acc[...] * jnp.concatenate([a, a], axis=1) + dot(p, vc, 1, 0)

    def state_step(j0, n):
        x = dot(w, kv_ref[pl.ds(j0, n), :D], 1, 1).astype(bf16)
        xs[:, pl.ds(j0, n)] = x
        state[...] += dot(key_features(x, RATIO), widened(kv_ref[pl.ds(j0, n), D:]), 1, 0)

    def sweep(step, stop):
        count = (stop - low) // (4 * rows)

        def body(t, c):
            step(pl.multiple_of(low + t * 4 * rows, rows), 4 * rows)
            return c

        lax.fori_loop(0, count, body, 0)
        left = (stop - low) % (4 * rows)

        @pl.when(left >= 2 * rows)
        def _():
            step(pl.multiple_of(low + count * 4 * rows, rows), 2 * rows)

        @pl.when(left % (2 * rows) > 0)
        def _():
            step(pl.multiple_of(stop - rows, rows), rows)

    sweep(teacher_step, dbase)

    @pl.when(block == 0)
    def _():
        state[...] = jnp.zeros_like(state)
        gw_ref[...] = jnp.zeros_like(gw_ref)
        square[...] = jnp.zeros_like(square)
        sweep(state_step, dbase)

    @pl.when(jnp.logical_and(block > 0, dbase > reach(block - 1)))
    def _():
        state_step(pl.multiple_of(dbase - rows, rows), rows)

    lane = lax.broadcasted_iota(jnp.int32, (rows, D), 1)
    lanef = lax.broadcasted_iota(jnp.int32, (2 * FM, D), 1)
    total = jnp.zeros((8, D), f32)
    gxs, sxs = [], []
    for h in heads:
        st = state[hf[h], :]
        sb = st[:, :D].astype(bf16)
        n = st[:, D:]
        n_hi = n.astype(bf16)
        n_lo = n - n_hi.astype(f32)
        nd = den[hr[h], :] + dot(phiq[hr[h], :], widened(sb, n_hi), 1, 0)
        inverse = 1.0 / nd[:, D:]
        student = nd[:, :D] * inverse
        teacher = acc[hr[h], :D] / acc[hr[h], D:]
        e = student - teacher
        err_ref[:, h * D : (h + 1) * D] = e.astype(err_ref.dtype)
        e2 = e * e
        for b in range(rows // 8):
            total = total + e2[b * 8 : (b + 1) * 8]
        go = (2.0 * e * inverse).astype(bf16)
        gd = -jnp.sum(go.astype(f32) * student, axis=1, keepdims=True)
        gd_hi = gd.astype(bf16).astype(f32)
        gdx = jnp.where(lane == 1, gd - gd_hi, jnp.where(lane <= 2, gd_hi, 0.0)).astype(bf16)
        gxs.append(widened(go, gdx))
        sxs.append(widened(sb, jnp.where(lanef == 2, n_lo, n).astype(bf16)))
    square[...] += total
    gx = jnp.concatenate(gxs, axis=0)
    laned = lax.broadcasted_iota(jnp.int32, (span, D), 1)
    vg = widened(vd, jnp.where(laned == 2, 0.0, 1.0).astype(bf16))
    glin = dot(gx, vg, 1, 1)
    gouts = []
    for h in heads:
        q = qs[hr[h], :]
        gl = jnp.where(far, glin[hr[h]], 0.0).astype(bf16)
        xq = dot(w[hw[h]], q, 1, 1).astype(bf16)
        fqt = key_features(xq, 1) * jnp.asarray(SIGMA, bf16)
        gq = dot(sxs[h], gxs[h], 1, 1) + dot(phikd[hf[h]], gl, 1, 1)
        y = (key_slopes(xq, gq, 1) * SIGMA).astype(bf16)
        gw_ref[hw[h], :] += dot(y, q, 1, 0)
        lsum[block, hf[h], :] = dot(fqt, gxs[h], 1, 0)
        gouts.append(dot(fqt, gl, 1, 0))
    gp = key_slopes(xd, jnp.concatenate(gouts, axis=0), RATIO).astype(bf16)
    gw_ref[...] += dot(gp, kd, 1, 0)

    def back_step(j0, n):
        kc = kv_ref[pl.ds(j0, n), :D]
        g = dot(lx[...], widened(kv_ref[pl.ds(j0, n), D:]), 1, 1)
        gp = key_slopes(xs[:, pl.ds(j0, n)], g, RATIO).astype(bf16)
        gw_ref[...] += dot(gp, kc, 1, 0)

    @pl.when(block == blocks - 1)
    def _():
        for b in reversed(range(blocks)):
            if b < blocks - 1:
                lsum[b] += lsum[b + 1]
            l = lsum[b]
            lanel = lax.broadcasted_iota(jnp.int32, (l.shape[0], D), 1)
            ln = jnp.sum(jnp.where(lanel < 2, l[:, D:], 0.0), axis=1, keepdims=True)
            ln_hi = ln.astype(bf16).astype(f32)
            ln = jnp.where(lanel == 0, ln_hi, jnp.where(lanel == 1, ln - ln_hi, 0.0))
            lx[...] = widened(l[:, :D].astype(bf16), ln.astype(bf16))
            if b == 0:
                sweep(back_step, reach(0))
            else:
                here = reach(b)

                @pl.when(here > reach(b - 1))
                def _():
                    back_step(pl.multiple_of(here - rows, rows), rows)

        out_ref[: RATIO * FM, :] = gw_ref[...].astype(out_ref.dtype)
        row = lax.broadcasted_iota(jnp.int32, (TAIL, D), 0)
        rest = jnp.broadcast_to(jnp.sum(square[...], keepdims=True), (TAIL, D))
        tail = jnp.zeros((TAIL, D), f32)
        for k in range(3):
            part = rest.astype(out_ref.dtype).astype(f32)
            tail = jnp.where(row == k, part, tail)
            rest = rest - part
        out_ref[RATIO * FM :, :] = tail.astype(out_ref.dtype)


def attend(where, queries, weights_t, kv, out_type):
    blocks, rows, width = queries.shape
    tokens = kv.shape[0]
    D = HEAD_SIZE
    R = RATIO * rows
    F = RATIO * 2 * FM
    at = pl.BlockSpec((pl.Squeezed(), rows, width), lambda b, p: (b ^ p[2], 0, 0))
    return pl.pallas_call(
        kernel,
        name="attend",
        out_shape=(
            jax.ShapeDtypeStruct(queries.shape, out_type),
            jax.ShapeDtypeStruct((RATIO * FM + TAIL, D), out_type),
        ),
        grid_spec=pltpu.PrefetchScalarGridSpec(
            num_scalar_prefetch=1,
            grid=(blocks,),
            in_specs=[
                at,
                pl.BlockSpec((RATIO * FM, D), lambda b, p: (0, 0)),
                pl.BlockSpec((tokens, 2 * D), lambda b, p: (0, 0)),
            ],
            out_specs=[
                at,
                pl.BlockSpec((RATIO * FM + TAIL, D), lambda b, p: (0, 0)),
            ],
            scratch_shapes=[
                pltpu.VMEM((RATIO * FM, D), f32),
                pltpu.VMEM((8, D), f32),
                pltpu.VMEM((R, D), bf16),
                pltpu.VMEM((R, 2 * D), bf16),
                pltpu.VMEM((R, D), f32),
                pltpu.VMEM((R, 2 * D), f32),
                pltpu.VMEM((F, 2 * D), f32),
                pltpu.VMEM((blocks, F, 2 * D), f32),
                pltpu.VMEM((F, 2 * D), bf16),
                pltpu.VMEM((RATIO * FM, tokens), bf16),
                pltpu.VMEM((R, 2 * FM), bf16),
                pltpu.VMEM((R, 2 * D), f32),
            ],
        ),
        compiler_params=pltpu.CompilerParams(
            dimension_semantics=("arbitrary",), vmem_limit_bytes=58 << 20
        ),
        cost_estimate=pl.CostEstimate(
            flops=blocks * R * tokens * D * 6,
            bytes_accessed=tokens * 4 * D + R * blocks * D * 4,
            transcendentals=blocks * R * tokens,
        ),
    )(where, queries, weights_t, kv)


def exchange(parts, ctx, unit):
    return [
        part if s == 0 else lax.ppermute(part, "ctx", [(i, i ^ (s * unit)) for i in range(ctx)])
        for s, part in enumerate(parts)
    ]


def pairwise(parts):
    while len(parts) > 1:
        parts = [parts[i] + parts[i + 1] for i in range(0, len(parts), 2)]
    return parts[0]


def in_order(parts, number):
    bit = 1
    while bit < len(parts):
        odd = (number & bit) > 0
        parts = [jnp.where(odd, parts[i ^ bit], parts[i]) for i in range(len(parts))]
        bit *= 2
    return parts


def shards(queries, keys, values, feature_weights):
    rows = queries.shape[0]
    heads = feature_weights.shape[0]
    groups = heads // RATIO
    D = HEAD_SIZE
    width = RATIO * D
    ctx = lax.axis_size("ctx")
    place = lax.axis_index("ctx")
    whole = rows * ctx * QUERY_HEADS
    weights_t = jnp.transpose(feature_weights, (0, 2, 1)).reshape(heads * FM, D)
    split = groups > 1 and groups & (groups - 1) == 0 and ctx in (2 * groups, 4 * groups)
    if not split:
        everything = lax.all_gather(jnp.concatenate([keys, values], axis=1), "ctx", axis=0, tiled=True)
        where = jnp.stack([place * rows, 0, 0]).astype(jnp.int32)
        done = []
        for g in range(groups):
            kv = jnp.concatenate(
                [everything[:, g * D : (g + 1) * D], everything[:, (groups + g) * D : (groups + g + 1) * D]], axis=1
            )
            done.append(
                attend(where, queries[None, :, g * width : (g + 1) * width],
                       weights_t[g * RATIO * FM : (g + 1) * RATIO * FM], kv, f32)
            )
        error = jnp.concatenate([d[0][0] for d in done], axis=1)
        cut = RATIO * FM
        loss = lax.psum(sum(jnp.sum(d[1][cut:, 0]) for d in done), ("ctx", "head")) / whole
        gw = lax.psum(jnp.concatenate([d[1][:cut] for d in done], axis=0), "ctx")
        return (error, loss, jnp.transpose(gw.reshape(heads, FM, D), (0, 2, 1)))

    slices = ctx // groups
    number = place % groups
    here = place // groups

    def of_group(a, s, n):
        return lax.dynamic_slice_in_dim(a, (number ^ s) * n, n, 1)

    members = range(groups)
    kv_parts = [jnp.concatenate([of_group(keys, s, D), of_group(values, s, D)], axis=1) for s in members]
    own = jnp.concatenate(in_order(exchange(kv_parts, ctx, 1), number), axis=0)
    q = jnp.stack(exchange([of_group(queries, s, width) for s in members], ctx, 1))
    earlier = [
        lax.ppermute(own, "ctx", [(i, i + s * groups) for i in range(ctx - s * groups)])
        for s in range(1, slices)
    ]
    kv = jnp.concatenate(earlier[::-1] + [own], axis=0)
    run = groups * rows
    where = jnp.stack([(slices - 1) * run, (slices - 1 - here) * run, number]).astype(jnp.int32)
    w = lax.dynamic_slice_in_dim(weights_t, number * RATIO * FM, RATIO * FM, 0)
    error, gw = attend(where, q, w, kv, bf16)
    back = in_order(exchange([error[s] for s in members], ctx, 1), number)
    attn_error = jnp.concatenate(back, axis=1).astype(f32)
    gw = pairwise([a.astype(f32) for a in exchange([gw] * slices, ctx, groups)])
    cut = RATIO * FM
    rest = gw[cut] + gw[cut + 1] + gw[cut + 2]
    tail = []
    for k in range(3):
        tail.append(lax.reduce_precision(rest, 8, 7))
        rest = rest - tail[-1]
    tail = jnp.stack(tail + [jnp.zeros_like(rest)] * (TAIL - 3))
    parts = exchange([jnp.concatenate([gw[:cut], tail]).astype(bf16)] * groups, ctx, 1)
    square = pairwise([jnp.sum(p[cut : cut + 3, 0].astype(f32)) for p in parts])
    count = lax.axis_size("head")
    if count == 2:
        square = square + lax.ppermute(square, "head", [(0, 1), (1, 0)])
    else:
        square = lax.psum(square, "head")
    gw = jnp.concatenate(in_order([p[:cut] for p in parts], number), axis=0).astype(f32)
    return (attn_error, square / whole, jnp.transpose(gw.reshape(heads, FM, D), (0, 2, 1)))


def solution(mesh):
    placed = (P("ctx", "head"), P("ctx", "head"), P("ctx", "head"), P("head", None, None))
    return jax.shard_map(
        shards,
        mesh=mesh,
        in_specs=placed,
        out_specs=(P("ctx", "head"), P(), P("head", None, None)),
        check_vma=False,
    )
```

time: 248 us -> 115 us (0.46)
  waiting for transfers between devices: 107 us -> 20.5 us
  blocking collectives: 86.4 us -> 0 us
  starting transfers between devices: 0.08 us -> 46.8 us
  between operations: 15.8 us -> 5.31 us
  other arithmetic: 5.24 us -> 8.93 us
  local copies, waits for them, and re-layouts: 2.31 us -> 5.19 us
  Pallas kernels: 30.6 us -> 27.9 us
    psum x1 -> x0, blocking collectives: 86.4 us -> none  [shards(): lax.psum(jnp.sum(squares), ('ctx', 'head')) / (whole_rows * QUERY_HEADS)]
    psum x1 -> x0, waiting for transfers between devices: 53.8 us -> none  [shards(): gw = lax.psum(gw, 'ctx')]
    all_gather x1 -> x0, waiting for transfers between devices: 52.8 us -> none  [shards(): lax.all_gather(jnp.concatenate([keys, values], axis=1), 'ctx', axis=0, ti...]
    ppermute x0 -> x19, starting transfers between devices: none -> 46.8 us  [the longest x15 34.6 us: exchange(): lax.ppermute(part, 'ctx', [(i, i ^ s * unit) for i in range(ctx)])]
    ppermute x0 -> x19, waiting for transfers between devices: none -> 20.5 us  [the longest x15 10.7 us: exchange(): lax.ppermute(part, 'ctx', [(i, i ^ s * unit) for i in range(ctx)])]
    pallas_call x1, Pallas kernels: 30.6 us -> 27.9 us  [attend(): pl.pallas_call(kernel, name='attend', out_shape=(jax.ShapeDtypeStruct(que...]
    concatenate x2 -> x6, other arithmetic: 2.8 us -> 0.1 us  [the longest x1 0.04 us: shards(): jnp.concatenate(in_order([p[:cut] for p in parts], number), axis=0)]
  transfers between devices with their start and end apart: 2 -> 19, of which waited for: 2 -> 8; matrix products, arithmetic and copies ran while one was open for 1% -> 10% of each run, Pallas kernels for 0% -> 0%
where the time goes in v2:
time: 115 us
  starting transfers between devices  46.8 us (41%)
  Pallas kernels  27.9 us (24%)
  waiting for transfers between devices  20.5 us (18%)
  other arithmetic  8.93 us (8%)
  between operations  5.31 us (5%)
  local copies, waits for them, and re-layouts  5.19 us (5%)
    ppermute x15, starting transfers between devices, exchange(): lax.ppermute(part, 'ctx', [(i, i ^ s * unit) for i in range(ctx)])  34.6 us
    pallas_call x1, Pallas kernels, attend(): pl.pallas_call(kernel, name='attend', out_shape=(jax.ShapeDtypeStruct(que...  27.9 us
    ppermute x15, waiting for transfers between devices, exchange(): lax.ppermute(part, 'ctx', [(i, i ^ s * unit) for i in range(ctx)])  10.7 us
    ppermute x3, waiting for transfers between devices, shards(): lax.ppermute(own, 'ctx', [(i, i + s * groups) for i in range(ctx - s * gr...  9.74 us
    ppermute x3, starting transfers between devices, shards(): lax.ppermute(own, 'ctx', [(i, i + s * groups) for i in range(ctx - s * gr...  9.36 us
    ppermute x1, starting transfers between devices, shards(): square = square + lax.ppermute(square, 'head', [(0, 1), (1, 0)])  2.85 us
    reduce_sum x4, other arithmetic, shards(): square = pairwise([jnp.sum(p[cut:cut + 3, 0].astype(f32)) for p in parts])  2.41 us
  transfers between devices with their start and end apart: 19, of which 8 were waited for; matrix products, arithmetic and copies ran while one was open for 10% of the time, Pallas kernels for 0%

profile of v2, /device:TPU:0, one launch (start us, length us, event | category | flops | bytes accessed | tf_op | source)
XLA Modules:
  0.0 114.6 jit_solution(12901655885054201742)
XLA Ops:
  0.6 0.0 copy-start
  0.7 1.0 constant_dynamic-slice_fusion
  1.7 2.5 %collective-permute-start.3 = (bf16[128,256]{1,0:T(8,128)(2,1)S(1)}, bf16[128,256]{1,0:T(8,128)(2,1)S(1)}, u32[]{:S(2)}, u32[]{:S(2)}) collective-permute-start(bf16[128,256]{1,0:T(8,128)(2,1)S(1)} %pad_maximum_fusion.3), channel_id=1, source_target_pairs={{0,6},{2,4},{4,2},{6,0},{8,14},{10,12},{12,10},{14,8},{16,22},{18,... | collective-permute-start | bytes 196616 | tf_op jit(solution)/shard_map/ppermute | solution.py:295
  4.1 0.6 collective-permute-start.4
  4.8 0.2 collective-permute-start.5
  5.0 1.3 %dynamic-slice_bitcast_fusion = (bf16[1,128,1024]{2,1,0:T(8,128)(2,1)S(1)}, bf16[128,1024]{1,0:T(8,128)(2,1)S(1)}, bf16[128,1024]{1,0:T(8,128)(2,1)S(1)}, bf16[128,1024]{1,0:T(8,128)(2,1)S(1)}) fusion(bf16[128,4096]{1,0:T(8,128)(2,1)} %param.4, s32[]{:T(128)S(6)} %select_n.160, s32[]{:T(128)S(6)} %select_n.161, s32[]{:T(128)S(6)} %select_n.163, s32[]{:T(128)S(6)} %select_n.162), kind=kLoop, calls=%fused_computation.12 | loop fusion | bytes 2097168 | tf_op jit(solution)/shard_map/stack | solution.py:354
  6.2 1.5 %collective-permute-start.2 = (bf16[128,1024]{1,0:T(8,128)(2,1)S(1)}, bf16[128,1024]{1,0:T(8,128)(2,1)S(1)}, u32[]{:S(2)}, u32[]{:S(2)}) collective-permute-start(bf16[128,1024]{1,0:T(8,128)(2,1)S(1)} %get-tuple-element.18), channel_id=1, source_target_pairs={{0,6},{2,4},{4,2},{6,0},{8,14},{10,12},{12,10},{14,8},{16,22},{18,... | collective-permute-start | bytes 786440 | tf_op jit(solution)/shard_map/ppermute | solution.py:295
  7.8 0.6 collective-permute-start.1
  8.3 0.0 collective-permute-done.3
  8.3 0.0 collective-permute-start
  8.3 0.5 collective-permute-done.4
  8.9 0.0 collective-permute-done.5
  8.9 0.1 broadcast_select_fusion.21
  9.0 5.6 %collective-permute-start.6 = (bf16[512,256]{1,0:T(8,128)(2,1)S(1)}, bf16[512,256]{1,0:T(8,128)(2,1)S(1)}, u32[]{:S(2)}, u32[]{:S(2)}) collective-permute-start(bf16[512,256]{1,0:T(8,128)(2,1)S(1)} %pad_maximum_fusion.2), channel_id=1, source_target_pairs={{0,24},{2,26},{4,28},{6,30},{1,25},{3,27},{5,29},{7,31}} | collective-permute-start | bytes 786440 | tf_op jit(solution)/shard_map/ppermute | solution.py:356
  14.6 0.7 constant_dynamic-slice_fusion.8.w_ref
  15.3 1.3 %collective-permute-start.7 = (bf16[512,256]{1,0:T(8,128)(2,1)S(1)}, bf16[512,256]{1,0:T(8,128)(2,1)S(1)}, u32[]{:S(2)}, u32[]{:S(2)}) collective-permute-start(bf16[512,256]{1,0:T(8,128)(2,1)S(1)} %pad_maximum_fusion.2), channel_id=1, source_target_pairs={{0,16},{2,18},{4,20},{6,22},{8,24},{10,26},{12,28},{14,30},{1,17},... | collective-permute-start | bytes 786440 | tf_op jit(solution)/shard_map/ppermute | solution.py:356
  16.6 0.6 pad_add_fusion.where_ref
  17.1 2.5 %collective-permute-start.8 = (bf16[512,256]{1,0:T(8,128)(2,1)S(1)}, bf16[512,256]{1,0:T(8,128)(2,1)S(1)}, u32[]{:S(2)}, u32[]{:S(2)}) collective-permute-start(bf16[512,256]{1,0:T(8,128)(2,1)S(1)} %pad_maximum_fusion.2), channel_id=1, source_target_pairs={{0,8},{2,10},{4,12},{6,14},{8,16},{10,18},{12,20},{14,22},{16,24},... | collective-permute-start | bytes 786440 | tf_op jit(solution)/shard_map/ppermute | solution.py:356
  19.6 1.0 collective-permute-done.1
  20.6 1.1 pad_maximum_fusion.q_ref
  21.7 5.2 %collective-permute-done.7 = bf16[512,256]{1,0:T(8,128)(2,1)S(1)} collective-permute-done((bf16[512,256]{1,0:T(8,128)(2,1)S(1)}, bf16[512,256]{1,0:T(8,128)(2,1)S(1)}, u32[]{:S(2)}, u32[]{:S(2)}) %collective-permute-start.7) | collective-permute-done | bytes 262176 | tf_op jit(solution)/shard_map/ppermute | solution.py:356
  27.0 4.5 %collective-permute-done.8 = bf16[512,256]{1,0:T(8,128)(2,1)S(1)} collective-permute-done((bf16[512,256]{1,0:T(8,128)(2,1)S(1)}, bf16[512,256]{1,0:T(8,128)(2,1)S(1)}, u32[]{:S(2)}, u32[]{:S(2)}) %collective-permute-start.8) | collective-permute-done | bytes 262176 | tf_op jit(solution)/shard_map/ppermute | solution.py:356
  31.5 0.0 copy-start.1
  31.6 1.0 copy-done.1
  32.5 27.9 %attend.1 = (bf16[4,128,1024]{2,1,0:T(8,128)(2,1)}, bf16[528,128]{1,0:T(8,128)(2,1)}) custom-call(s32[3]{0:T(128)} %pad_add_fusion.where_ref, bf16[4,128,1024]{2,1,0:T(8,128)(2,1)} %pad_maximum_fusion.q_ref, bf16[512,128]{1,0:T(8,128)(2,1)} %constant_dynamic-slice_fusion.8.w_ref, bf16[2048,256]{1,0:T(8,128)(2,1)} %copy-done.1), custom_call_target="tpu_custom_call" | custom-call | flops 6442450944 | bytes 3145728 | tf_op jit(solution)/shard_map/attend/pallas_call | solution.py:248
  60.4 24.9 %collective-permute-start.14 = (bf16[528,128]{1,0:T(8,128)(2,1)}, bf16[528,128]{1,0:T(8,128)(2,1)S(1)}, u32[]{:S(2)}, u32[]{:S(2)}) collective-permute-start(bf16[528,128]{1,0:T(8,128)(2,1)} %get-tuple-element.6), channel_id=1, source_target_pairs={{0,24},{2,26},{4,28},{6,30},{8,16},{10,18},{12,20},{14,22},{16,8},... | collective-permute-start | bytes 405512 | tf_op jit(solution)/shard_map/ppermute | solution.py:295
  85.3 0.6 collective-permute-start.12
  85.8 1.2 %slice_bitcast_fusion = (bf16[128,1024]{1,0:T(8,128)(2,1)S(1)}, bf16[128,1024]{1,0:T(8,128)(2,1)S(1)}, bf16[128,1024]{1,0:T(8,128)(2,1)S(1)}) fusion(bf16[4,128,1024]{2,1,0:T(8,128)(2,1)} %get-tuple-element.5), kind=kLoop, calls=%fused_computation.9 | loop fusion | bytes 1572864 | tf_op jit(solution)/shard_map/squeeze | solution.py:364
  87.0 0.8 collective-permute-start.9
  87.8 1.1 collective-permute-start.10
  88.9 1.1 collective-permute-done.14
  90.0 6.3 %collective-permute-done.13 = bf16[528,128]{1,0:T(8,128)(2,1)S(1)} collective-permute-done((bf16[528,128]{1,0:T(8,128)(2,1)}, bf16[528,128]{1,0:T(8,128)(2,1)S(1)}, u32[]{:S(2)}, u32[]{:S(2)}) %collective-permute-start.13) | collective-permute-done | bytes 135200 | tf_op jit(solution)/shard_map/ppermute | solution.py:295
  96.3 1.0 add_add_fusion
  97.3 0.1 concatenate.48
  97.4 0.1 collective-permute-start.15
  97.4 1.8 %collective-permute-start.16 = (bf16[528,128]{1,0:T(8,128)(2,1)S(1)}, bf16[528,128]{1,0:T(8,128)(2,1)S(1)}, u32[]{:S(2)}, u32[]{:S(2)}) collective-permute-start(bf16[528,128]{1,0:T(8,128)(2,1)S(1)} %concatenate.48), channel_id=1, source_target_pairs={{0,4},{2,6},{4,0},{6,2},{8,12},{10,14},{12,8},{14,10},{16,20},{18,... | collective-permute-start | bytes 405512 | tf_op jit(solution)/shard_map/ppermute | solution.py:295
  99.2 0.6 convert_reduce_fusion.3
  99.9 0.1 collective-permute-start.17
  99.9 1.6 %collective-permute-done.10 = bf16[128,1024]{1,0:T(8,128)(2,1)S(1)} collective-permute-done((bf16[128,1024]{1,0:T(8,128)(2,1)S(1)}, bf16[128,1024]{1,0:T(8,128)(2,1)S(1)}, u32[]{:S(2)}, u32[]{:S(2)}) %collective-permute-start.10) | collective-permute-done | bytes 262176 | tf_op jit(solution)/shard_map/ppermute | solution.py:295
  101.5 1.0 broadcast_select_fusion.5
  102.6 1.5 %maximum_convert_fusion = f32[128,4096]{1,0:T(8,128)} fusion(bf16[128,1024]{1,0:T(8,128)(2,1)S(1)} %get-tuple-element.12, bf16[128,1024]{1,0:T(8,128)(2,1)S(1)} %get-tuple-element.11, bf16[128,1024]{1,0:T(8,128)(2,1)S(1)} %get-tuple-element.10, bf16[128,1024]{1,0:T(8,128)(2,1)S(1)} %get-tuple-element.9), kind=kLoop, calls=%fused_computation.1 | loop fusion | flops 4194304 | bytes 3145728 | tf_op jit(solution)/shard_map/convert_element_type | solution.py:365
  104.1 0.6 convert_reduce_fusion.2
  106.0 0.6 convert_reduce_fusion.1
  106.6 0.2 collective-permute-done.17
  106.8 0.6 convert_reduce_fusion
  108.7 2.9 %collective-permute-start.18 = (f32[]{:T(128)}, f32[]{:T(128)}, u32[]{:S(2)}, u32[]{:S(2)}) collective-permute-start(f32[]{:T(128)} %add.86), channel_id=1, source_target_pairs={{0,1},{1,0},{2,3},{3,2},{4,5},{5,4},{6,7},{7,6},{8,9},{9,8},{10,11... | collective-permute-start | bytes 20 | tf_op jit(solution)/shard_map/ppermute | solution.py:378
  111.6 0.1 broadcast_select_fusion.13
  111.7 1.1 convert_bitcast_fusion
  (31 shorter events, 0.2 us)
Async XLA Ops:
  0.6 14.0 %copy-start = (bf16[32,128,64]{1,2,0:T(8,128)(2,1)S(1)}, bf16[32,128,64]{1,2,0:T(8,128)(2,1)}, u32[]{:S(2)}) copy-start(bf16[32,128,64]{1,2,0:T(8,128)(2,1)} %param.7) | copy-start | bytes 1572868
  1.7 6.7 %collective-permute-start.3 = (bf16[128,256]{1,0:T(8,128)(2,1)S(1)}, bf16[128,256]{1,0:T(8,128)(2,1)S(1)}, u32[]{:S(2)}, u32[]{:S(2)}) collective-permute-start(bf16[128,256]{1,0:T(8,128)(2,1)S(1)} %pad_maximum_fusion.3), channel_id=1, source_target_pairs={{0,6},{2,4},{4,2},{6,0},{8,14},{10,12},{12,10},{14,8},{16,22},{18,... | collective-permute-start | bytes 196616 | tf_op jit(solution)/shard_map/ppermute | solution.py:295
  4.1 4.7 %collective-permute-start.4 = (bf16[128,256]{1,0:T(8,128)(2,1)S(1)}, bf16[128,256]{1,0:T(8,128)(2,1)S(1)}, u32[]{:S(2)}, u32[]{:S(2)}) collective-permute-start(bf16[128,256]{1,0:T(8,128)(2,1)S(1)} %pad_maximum_fusion.4), channel_id=1, source_target_pairs={{0,4},{2,6},{4,0},{6,2},{8,12},{10,14},{12,8},{14,10},{16,20},{18,... | collective-permute-start | bytes 196616 | tf_op jit(solution)/shard_map/ppermute | solution.py:295
  4.8 4.1 %collective-permute-start.5 = (bf16[128,256]{1,0:T(8,128)(2,1)S(1)}, bf16[128,256]{1,0:T(8,128)(2,1)S(1)}, u32[]{:S(2)}, u32[]{:S(2)}) collective-permute-start(bf16[128,256]{1,0:T(8,128)(2,1)S(1)} %pad_maximum_fusion.5), channel_id=1, source_target_pairs={{0,2},{2,0},{4,6},{6,4},{8,10},{10,8},{12,14},{14,12},{16,18},{18,... | collective-permute-start | bytes 196616 | tf_op jit(solution)/shard_map/ppermute | solution.py:295
  6.2 10.9 %collective-permute-start.2 = (bf16[128,1024]{1,0:T(8,128)(2,1)S(1)}, bf16[128,1024]{1,0:T(8,128)(2,1)S(1)}, u32[]{:S(2)}, u32[]{:S(2)}) collective-permute-start(bf16[128,1024]{1,0:T(8,128)(2,1)S(1)} %get-tuple-element.18), channel_id=1, source_target_pairs={{0,6},{2,4},{4,2},{6,0},{8,14},{10,12},{12,10},{14,8},{16,22},{18,... | collective-permute-start | bytes 786440 | tf_op jit(solution)/shard_map/ppermute | solution.py:295
  7.8 12.8 %collective-permute-start.1 = (bf16[128,1024]{1,0:T(8,128)(2,1)S(1)}, bf16[128,1024]{1,0:T(8,128)(2,1)S(1)}, u32[]{:S(2)}, u32[]{:S(2)}) collective-permute-start(bf16[128,1024]{1,0:T(8,128)(2,1)S(1)} %get-tuple-element.19), channel_id=1, source_target_pairs={{0,4},{2,6},{4,0},{6,2},{8,12},{10,14},{12,8},{14,10},{16,20},{18,... | collective-permute-start | bytes 786440 | tf_op jit(solution)/shard_map/ppermute | solution.py:295
  8.3 12.2 %collective-permute-start = (bf16[128,1024]{1,0:T(8,128)(2,1)S(1)}, bf16[128,1024]{1,0:T(8,128)(2,1)S(1)}, u32[]{:S(2)}, u32[]{:S(2)}) collective-permute-start(bf16[128,1024]{1,0:T(8,128)(2,1)S(1)} %get-tuple-element.17), channel_id=1, source_target_pairs={{0,2},{2,0},{4,6},{6,4},{8,10},{10,8},{12,14},{14,12},{16,18},{18,... | collective-permute-start | bytes 786440 | tf_op jit(solution)/shard_map/ppermute | solution.py:295
  9.0 12.7 %collective-permute-start.6 = (bf16[512,256]{1,0:T(8,128)(2,1)S(1)}, bf16[512,256]{1,0:T(8,128)(2,1)S(1)}, u32[]{:S(2)}, u32[]{:S(2)}) collective-permute-start(bf16[512,256]{1,0:T(8,128)(2,1)S(1)} %pad_maximum_fusion.2), channel_id=1, source_target_pairs={{0,24},{2,26},{4,28},{6,30},{1,25},{3,27},{5,29},{7,31}} | collective-permute-start | bytes 786440 | tf_op jit(solution)/shard_map/ppermute | solution.py:356
  15.3 11.7 %collective-permute-start.7 = (bf16[512,256]{1,0:T(8,128)(2,1)S(1)}, bf16[512,256]{1,0:T(8,128)(2,1)S(1)}, u32[]{:S(2)}, u32[]{:S(2)}) collective-permute-start(bf16[512,256]{1,0:T(8,128)(2,1)S(1)} %pad_maximum_fusion.2), channel_id=1, source_target_pairs={{0,16},{2,18},{4,20},{6,22},{8,24},{10,26},{12,28},{14,30},{1,17},... | collective-permute-start | bytes 786440 | tf_op jit(solution)/shard_map/ppermute | solution.py:356
  17.1 14.3 %collective-permute-start.8 = (bf16[512,256]{1,0:T(8,128)(2,1)S(1)}, bf16[512,256]{1,0:T(8,128)(2,1)S(1)}, u32[]{:S(2)}, u32[]{:S(2)}) collective-permute-start(bf16[512,256]{1,0:T(8,128)(2,1)S(1)} %pad_maximum_fusion.2), channel_id=1, source_target_pairs={{0,8},{2,10},{4,12},{6,14},{8,16},{10,18},{12,20},{14,22},{16,24},... | collective-permute-start | bytes 786440 | tf_op jit(solution)/shard_map/ppermute | solution.py:356
  31.5 1.0 copy-start.1
  60.4 29.6 %collective-permute-start.14 = (bf16[528,128]{1,0:T(8,128)(2,1)}, bf16[528,128]{1,0:T(8,128)(2,1)S(1)}, u32[]{:S(2)}, u32[]{:S(2)}) collective-permute-start(bf16[528,128]{1,0:T(8,128)(2,1)} %get-tuple-element.6), channel_id=1, source_target_pairs={{0,24},{2,26},{4,28},{6,30},{8,16},{10,18},{12,20},{14,22},{16,8},... | collective-permute-start | bytes 405512 | tf_op jit(solution)/shard_map/ppermute | solution.py:295
  85.3 11.0 %collective-permute-start.13 = (bf16[528,128]{1,0:T(8,128)(2,1)}, bf16[528,128]{1,0:T(8,128)(2,1)S(1)}, u32[]{:S(2)}, u32[]{:S(2)}) collective-permute-start(bf16[528,128]{1,0:T(8,128)(2,1)} %get-tuple-element.6), channel_id=1, source_target_pairs={{0,16},{2,18},{4,20},{6,22},{8,24},{10,26},{12,28},{14,30},{16,0},... | collective-permute-start | bytes 405512 | tf_op jit(solution)/shard_map/ppermute | solution.py:295
  85.3 11.0 %collective-permute-start.12 = (bf16[528,128]{1,0:T(8,128)(2,1)}, bf16[528,128]{1,0:T(8,128)(2,1)S(1)}, u32[]{:S(2)}, u32[]{:S(2)}) collective-permute-start(bf16[528,128]{1,0:T(8,128)(2,1)} %get-tuple-element.6), channel_id=1, source_target_pairs={{0,8},{2,10},{4,12},{6,14},{8,0},{10,2},{12,4},{14,6},{16,24},{18,... | collective-permute-start | bytes 405512 | tf_op jit(solution)/shard_map/ppermute | solution.py:295
  87.0 12.9 %collective-permute-start.9 = (bf16[128,1024]{1,0:T(8,128)(2,1)S(1)}, bf16[128,1024]{1,0:T(8,128)(2,1)S(1)}, u32[]{:S(2)}, u32[]{:S(2)}) collective-permute-start(bf16[128,1024]{1,0:T(8,128)(2,1)S(1)} %get-tuple-element.15), channel_id=1, source_target_pairs={{0,6},{2,4},{4,2},{6,0},{8,14},{10,12},{12,10},{14,8},{16,22},{18,... | collective-permute-start | bytes 786440 | tf_op jit(solution)/shard_map/ppermute | solution.py:295
  87.8 13.8 %collective-permute-start.10 = (bf16[128,1024]{1,0:T(8,128)(2,1)S(1)}, bf16[128,1024]{1,0:T(8,128)(2,1)S(1)}, u32[]{:S(2)}, u32[]{:S(2)}) collective-permute-start(bf16[128,1024]{1,0:T(8,128)(2,1)S(1)} %get-tuple-element.14), channel_id=1, source_target_pairs={{0,4},{2,6},{4,0},{6,2},{8,12},{10,14},{12,8},{14,10},{16,20},{18,... | collective-permute-start | bytes 786440 | tf_op jit(solution)/shard_map/ppermute | solution.py:295
  90.0 11.6 %collective-permute-start.11 = (bf16[128,1024]{1,0:T(8,128)(2,1)S(1)}, bf16[128,1024]{1,0:T(8,128)(2,1)S(1)}, u32[]{:S(2)}, u32[]{:S(2)}) collective-permute-start(bf16[128,1024]{1,0:T(8,128)(2,1)S(1)} %get-tuple-element.13), channel_id=1, source_target_pairs={{0,2},{2,0},{4,6},{6,4},{8,10},{10,8},{12,14},{14,12},{16,18},{18,... | collective-permute-start | bytes 786440 | tf_op jit(solution)/shard_map/ppermute | solution.py:295
  97.4 6.7 %collective-permute-start.15 = (bf16[528,128]{1,0:T(8,128)(2,1)S(1)}, bf16[528,128]{1,0:T(8,128)(2,1)S(1)}, u32[]{:S(2)}, u32[]{:S(2)}) collective-permute-start(bf16[528,128]{1,0:T(8,128)(2,1)S(1)} %concatenate.48), channel_id=1, source_target_pairs={{0,2},{2,0},{4,6},{6,4},{8,10},{10,8},{12,14},{14,12},{16,18},{18,... | collective-permute-start | bytes 405512 | tf_op jit(solution)/shard_map/ppermute | solution.py:295
  97.4 8.6 %collective-permute-start.16 = (bf16[528,128]{1,0:T(8,128)(2,1)S(1)}, bf16[528,128]{1,0:T(8,128)(2,1)S(1)}, u32[]{:S(2)}, u32[]{:S(2)}) collective-permute-start(bf16[528,128]{1,0:T(8,128)(2,1)S(1)} %concatenate.48), channel_id=1, source_target_pairs={{0,4},{2,6},{4,0},{6,2},{8,12},{10,14},{12,8},{14,10},{16,20},{18,... | collective-permute-start | bytes 405512 | tf_op jit(solution)/shard_map/ppermute | solution.py:295
  99.9 7.0 %collective-permute-start.17 = (bf16[528,128]{1,0:T(8,128)(2,1)S(1)}, bf16[528,128]{1,0:T(8,128)(2,1)S(1)}, u32[]{:S(2)}, u32[]{:S(2)}) collective-permute-start(bf16[528,128]{1,0:T(8,128)(2,1)S(1)} %concatenate.48), channel_id=1, source_target_pairs={{0,6},{2,4},{4,2},{6,0},{8,14},{10,12},{12,10},{14,8},{16,22},{18,... | collective-permute-start | bytes 405512 | tf_op jit(solution)/shard_map/ppermute | solution.py:295
  108.7 4.0 %collective-permute-start.18 = (f32[]{:T(128)}, f32[]{:T(128)}, u32[]{:S(2)}, u32[]{:S(2)}) collective-permute-start(f32[]{:T(128)} %add.86), channel_id=1, source_target_pairs={{0,1},{1,0},{2,3},{3,2},{4,5},{5,4},{6,7},{7,6},{8,9},{9,8},{10,11... | collective-permute-start | bytes 20 | tf_op jit(solution)/shard_map/ppermute | solution.py:378

commit v3 on v2

--- a/solution.py
+++ b/solution.py
@@ -52,12 +52,18 @@
     return jnp.concatenate([v, jnp.ones_like(v) if other is None else other], axis=1)
 
 
-def kernel(where_ref, q_ref, w_ref, kv_ref, err_ref, out_ref,
-           gw_ref, square, qs, qc, m_ref, acc, state, lsum, lx, xs, phiq, den):
-    rows = q_ref.shape[0]
+def kernel(blocks, pieces, where_ref, *refs):
+    q_refs, (w_ref, *kv_refs), err_refs, (out_ref, *scratch) = (
+        refs[:blocks],
+        refs[blocks : blocks + 1 + pieces],
+        refs[blocks + 1 + pieces : 2 * blocks + 1 + pieces],
+        refs[2 * blocks + 1 + pieces :],
+    )
+    (kv_ref, errs, gw_ref, square, qs, qc, m_ref, acc, state, lsum, lx, xs, phiq, den) = scratch
+    rows = q_refs[0].shape[0]
     D = HEAD_SIZE
     block = pl.program_id(0)
-    blocks = lsum.shape[0]
+    piece = where_ref[2] ^ block
     low = pl.multiple_of(where_ref[1], rows)
 
     def reach(b):
@@ -71,12 +77,23 @@
     hf = [slice(h * 2 * FM, (h + 1) * 2 * FM) for h in heads]
     hw = [slice(h * FM, (h + 1) * FM) for h in heads]
 
-    for h in heads:
-        q = q_ref[:, h * D : (h + 1) * D]
-        qs[hr[h], :] = q
-        scaled = q.astype(f32) * (SCALE * LOG2E)
-        high = scaled.astype(bf16)
-        qc[hr[h], :] = widened(high, (scaled - high.astype(f32)).astype(bf16))
+    for k, q_ref in enumerate(q_refs):
+
+        @pl.when(piece == k)
+        def _(q_ref=q_ref):
+            for h in heads:
+                q = q_ref[:, h * D : (h + 1) * D]
+                qs[hr[h], :] = q
+                scaled = q.astype(f32) * (SCALE * LOG2E)
+                high = scaled.astype(bf16)
+                qc[hr[h], :] = widened(high, (scaled - high.astype(f32)).astype(bf16))
+
+    @pl.when(block == 0)
+    def _():
+        for k, ref in enumerate(kv_refs):
+            n = ref.shape[0]
+            kv_ref[k * n : (k + 1) * n, :] = ref[...]
+
     w = w_ref[...]
 
     kd = kv_ref[pl.ds(dbase, span), :D]
@@ -90,55 +107,68 @@
     xd = dot(w, kd, 1, 1).astype(bf16)
     phikd = key_features(xd, RATIO)
     s = dot(qc[...], widened(kd, kd), 1, 1)
-    ps, mixes = [], []
-    for h in heads:
-        sh = s[hr[h]]
-        sc = jnp.where(causal, sh, big_negative)
-        top = jnp.max(sc, axis=1, keepdims=True)
-        m_ref[hr[h], :] = jnp.broadcast_to(top, (rows, D))
-        ps.append(jnp.exp2(sc - top).astype(bf16))
-        sw = jnp.where(window, sh, big_negative)
-        local = jnp.exp2(sw - jnp.max(sw, axis=1, keepdims=True))
-        q = qs[hr[h], :]
-        x = dot(q, w[hw[h]], 1, 1).astype(bf16)
+    fqs = []
+    for h in heads:
+        x = dot(qs[hr[h], :], w[hw[h]], 1, 1).astype(bf16)
         e = jnp.exp(-jnp.abs(x))
         one = jnp.ones_like(x)
         fq = jnp.concatenate([jnp.where(x > 0, one + x, e), jnp.where(x > 0, e, one - x)], axis=1)
-        phiq[hr[h], :] = fq * jnp.asarray(SIGMA, bf16)
-        lin = dot(phiq[hr[h], :], phikd[hf[h]], 1, 0)
-        mixes.append(jnp.where(far, lin, local).astype(bf16))
+        fqs.append(fq * jnp.asarray(SIGMA, bf16))
+        phiq[hr[h], :] = fqs[h]
+    lins = [dot(fqs[h], phikd[hf[h]], 1, 0).astype(bf16) for h in heads]
+    scs = [jnp.where(causal, s[hr[h]], big_negative) for h in heads]
+    tops = [jnp.max(sc, axis=1, keepdims=True) for sc in scs]
+    sws = [jnp.where(window, s[hr[h]], big_negative) for h in heads]
+    peaks = [jnp.max(sw, axis=1, keepdims=True) for sw in sws]
+    for h in heads:
+        m_ref[hr[h], :] = jnp.broadcast_to(tops[h], (rows, D))
+    ps = [jnp.exp2(scs[h] - tops[h]).astype(bf16) for h in heads]
+    mixes = [jnp.where(far, lins[h], jnp.exp2(sws[h] - peaks[h]).astype(bf16)) for h in heads]
     acc[...] = dot(jnp.concatenate(ps, axis=0), vx, 1, 0)
     den[...] = dot(jnp.concatenate(mixes, axis=0), vx, 1, 0)
 
     def teacher_step(j0, n):
         kc = kv_ref[pl.ds(j0, n), :D]
+        kk = widened(kc, kc)
         vc = widened(kv_ref[pl.ds(j0, n), D:])
-        s = dot(qc[...], widened(kc, kc), 1, 1)
-        old = m_ref[...]
-        new = jnp.maximum(old, jnp.max(s, axis=1, keepdims=True))
-        m_ref[...] = new
-        a = jnp.exp2(old - new)
-        p = jnp.exp2(s - jnp.concatenate([new] * (n // D), axis=1)).astype(bf16)
-        acc[...] = acc[...] * jnp.concatenate([a, a], axis=1) + dot(p, vc, 1, 0)
+        size = RATIO * rows // 4
+        cuts = [slice(i * size, (i + 1) * size) for i in range(4)]
+        scores = [dot(qc[c, :], kk, 1, 1) for c in cuts]
+        for c, s in zip(cuts, scores):
+            old = m_ref[c, :]
+            new = jnp.maximum(old, jnp.max(s, axis=1, keepdims=True))
+            m_ref[c, :] = new
+            a = jnp.exp2(old - new)
+            p = jnp.exp2(s - jnp.concatenate([new] * (n // D), axis=1)).astype(bf16)
+            acc[c, :] = acc[c, :] * jnp.concatenate([a, a], axis=1) + dot(p, vc, 1, 0)
 
     def state_step(j0, n):
-        x = dot(w, kv_ref[pl.ds(j0, n), :D], 1, 1).astype(bf16)
-        xs[:, pl.ds(j0, n)] = x
-        state[...] += dot(key_features(x, RATIO), widened(kv_ref[pl.ds(j0, n), D:]), 1, 0)
+        kc = kv_ref[pl.ds(j0, n), :D]
+        vc = widened(kv_ref[pl.ds(j0, n), D:])
+        size = RATIO // 2
+        xps = [dot(w[i * size * FM : (i + 1) * size * FM], kc, 1, 1).astype(bf16) for i in range(2)]
+        for i, x in enumerate(xps):
+            xs[i * size * FM : (i + 1) * size * FM, pl.ds(j0, n)] = x
+            c = slice(i * size * 2 * FM, (i + 1) * size * 2 * FM)
+            state[c, :] += dot(key_features(x, size), vc, 1, 0)
 
     def sweep(step, stop):
-        count = (stop - low) // (4 * rows)
+        count = (stop - low) // (8 * rows)
 
         def body(t, c):
-            step(pl.multiple_of(low + t * 4 * rows, rows), 4 * rows)
+            step(pl.multiple_of(low + t * 8 * rows, rows), 8 * rows)
             return c
 
         lax.fori_loop(0, count, body, 0)
-        left = (stop - low) % (4 * rows)
-
-        @pl.when(left >= 2 * rows)
+        left = (stop - low) % (8 * rows)
+
+        @pl.when(left >= 4 * rows)
         def _():
-            step(pl.multiple_of(low + count * 4 * rows, rows), 2 * rows)
+            step(pl.multiple_of(low + count * 8 * rows, rows), 4 * rows)
+
+        @pl.when(left % (4 * rows) >= 2 * rows)
+        def _():
+            step(pl.multiple_of(stop - left % (4 * rows), rows), 2 * rows)
 
         @pl.when(left % (2 * rows) > 0)
         def _():
@@ -160,19 +190,22 @@
     lane = lax.broadcasted_iota(jnp.int32, (rows, D), 1)
     lanef = lax.broadcasted_iota(jnp.int32, (2 * FM, D), 1)
     total = jnp.zeros((8, D), f32)
-    gxs, sxs = [], []
+    gxs, sxs, firsts = [], [], []
     for h in heads:
         st = state[hf[h], :]
         sb = st[:, :D].astype(bf16)
         n = st[:, D:]
         n_hi = n.astype(bf16)
         n_lo = n - n_hi.astype(f32)
-        nd = den[hr[h], :] + dot(phiq[hr[h], :], widened(sb, n_hi), 1, 0)
+        firsts.append(dot(phiq[hr[h], :], widened(sb, n_hi), 1, 0))
+        sxs.append(widened(sb, jnp.where(lanef == 2, n_lo, n).astype(bf16)))
+    for h in heads:
+        nd = den[hr[h], :] + firsts[h]
         inverse = 1.0 / nd[:, D:]
         student = nd[:, :D] * inverse
         teacher = acc[hr[h], :D] / acc[hr[h], D:]
         e = student - teacher
-        err_ref[:, h * D : (h + 1) * D] = e.astype(err_ref.dtype)
+        errs[:, h * D : (h + 1) * D] = e.astype(errs.dtype)
         e2 = e * e
         for b in range(rows // 8):
             total = total + e2[b * 8 : (b + 1) * 8]
@@ -181,31 +214,38 @@
         gd_hi = gd.astype(bf16).astype(f32)
         gdx = jnp.where(lane == 1, gd - gd_hi, jnp.where(lane <= 2, gd_hi, 0.0)).astype(bf16)
         gxs.append(widened(go, gdx))
-        sxs.append(widened(sb, jnp.where(lanef == 2, n_lo, n).astype(bf16)))
     square[...] += total
+    for k, err_ref in enumerate(err_refs):
+
+        @pl.when(piece == k)
+        def _(err_ref=err_ref):
+            err_ref[...] = errs[...]
+
     gx = jnp.concatenate(gxs, axis=0)
     laned = lax.broadcasted_iota(jnp.int32, (span, D), 1)
     vg = widened(vd, jnp.where(laned == 2, 0.0, 1.0).astype(bf16))
     glin = dot(gx, vg, 1, 1)
-    gouts = []
-    for h in heads:
-        q = qs[hr[h], :]
-        gl = jnp.where(far, glin[hr[h]], 0.0).astype(bf16)
-        xq = dot(w[hw[h]], q, 1, 1).astype(bf16)
-        fqt = key_features(xq, 1) * jnp.asarray(SIGMA, bf16)
-        gq = dot(sxs[h], gxs[h], 1, 1) + dot(phikd[hf[h]], gl, 1, 1)
-        y = (key_slopes(xq, gq, 1) * SIGMA).astype(bf16)
-        gw_ref[hw[h], :] += dot(y, q, 1, 0)
-        lsum[block, hf[h], :] = dot(fqt, gxs[h], 1, 0)
-        gouts.append(dot(fqt, gl, 1, 0))
+    xqs = [dot(w[hw[h]], qs[hr[h], :], 1, 1).astype(bf16) for h in heads]
+    fqts = [key_features(x, 1) * jnp.asarray(SIGMA, bf16) for x in xqs]
+    gls = [jnp.where(far, glin[hr[h]], 0.0).astype(bf16) for h in heads]
+    gouts = [dot(fqts[h], gls[h], 1, 0) for h in heads]
+    gqs = [dot(sxs[h], gxs[h], 1, 1) + dot(phikd[hf[h]], gls[h], 1, 1) for h in heads]
+    for h in heads:
+        lsum[block, hf[h], :] = dot(fqts[h], gxs[h], 1, 0)
+    ys = [(key_slopes(xqs[h], gqs[h], 1) * SIGMA).astype(bf16) for h in heads]
+    for h in heads:
+        gw_ref[hw[h], :] += dot(ys[h], qs[hr[h], :], 1, 0)
     gp = key_slopes(xd, jnp.concatenate(gouts, axis=0), RATIO).astype(bf16)
     gw_ref[...] += dot(gp, kd, 1, 0)
 
     def back_step(j0, n):
         kc = kv_ref[pl.ds(j0, n), :D]
-        g = dot(lx[...], widened(kv_ref[pl.ds(j0, n), D:]), 1, 1)
-        gp = key_slopes(xs[:, pl.ds(j0, n)], g, RATIO).astype(bf16)
-        gw_ref[...] += dot(gp, kc, 1, 0)
+        vc = widened(kv_ref[pl.ds(j0, n), D:])
+        size = RATIO // 2
+        gs = [dot(lx[i * size * 2 * FM : (i + 1) * size * 2 * FM, :], vc, 1, 1) for i in range(2)]
+        for i, g in enumerate(gs):
+            c = slice(i * size * FM, (i + 1) * size * FM)
+            gw_ref[c, :] += dot(key_slopes(xs[c, pl.ds(j0, n)], g, size).astype(bf16), kc, 1, 0)
 
     @pl.when(block == blocks - 1)
     def _():
@@ -239,32 +279,31 @@
 
 
 def attend(where, queries, weights_t, kv, out_type):
-    blocks, rows, width = queries.shape
-    tokens = kv.shape[0]
+    blocks, pieces = len(queries), len(kv)
+    rows, width = queries[0].shape
+    tokens = sum(a.shape[0] for a in kv)
     D = HEAD_SIZE
     R = RATIO * rows
     F = RATIO * 2 * FM
-    at = pl.BlockSpec((pl.Squeezed(), rows, width), lambda b, p: (b ^ p[2], 0, 0))
-    return pl.pallas_call(
-        kernel,
+
+    def all_of(shape):
+        return pl.BlockSpec(shape, lambda b, p: (0, 0), pipeline_mode=pl.Buffered(1))
+
+    *error, gw = pl.pallas_call(
+        functools.partial(kernel, blocks, pieces),
         name="attend",
-        out_shape=(
-            jax.ShapeDtypeStruct(queries.shape, out_type),
-            jax.ShapeDtypeStruct((RATIO * FM + TAIL, D), out_type),
-        ),
+        out_shape=[jax.ShapeDtypeStruct((rows, width), out_type)] * blocks
+        + [jax.ShapeDtypeStruct((RATIO * FM + TAIL, D), out_type)],
         grid_spec=pltpu.PrefetchScalarGridSpec(
             num_scalar_prefetch=1,
             grid=(blocks,),
-            in_specs=[
-                at,
-                pl.BlockSpec((RATIO * FM, D), lambda b, p: (0, 0)),
-                pl.BlockSpec((tokens, 2 * D), lambda b, p: (0, 0)),
-            ],
-            out_specs=[
-                at,
-                pl.BlockSpec((RATIO * FM + TAIL, D), lambda b, p: (0, 0)),
-            ],
+            in_specs=[all_of((rows, width))] * blocks
+            + [all_of((RATIO * FM, D))]
+            + [all_of(a.shape) for a in kv],
+            out_specs=[all_of((rows, width))] * blocks + [all_of((RATIO * FM + TAIL, D))],
             scratch_shapes=[
+                pltpu.VMEM((tokens, 2 * D), bf16),
+                pltpu.VMEM((rows, width), out_type),
                 pltpu.VMEM((RATIO * FM, D), f32),
                 pltpu.VMEM((8, D), f32),
                 pltpu.VMEM((R, D), bf16),
@@ -280,14 +319,15 @@
             ],
         ),
         compiler_params=pltpu.CompilerParams(
-            dimension_semantics=("arbitrary",), vmem_limit_bytes=58 << 20
+            dimension_semantics=("arbitrary",), vmem_limit_bytes=56 << 20
         ),
         cost_estimate=pl.CostEstimate(
             flops=blocks * R * tokens * D * 6,
             bytes_accessed=tokens * 4 * D + R * blocks * D * 4,
             transcendentals=blocks * R * tokens,
         ),
-    )(where, queries, weights_t, kv)
+    )(where, *queries, weights_t, *kv)
+    return error, gw
 
 
 def exchange(parts, ctx, unit):
@@ -332,8 +372,8 @@
                 [everything[:, g * D : (g + 1) * D], everything[:, (groups + g) * D : (groups + g + 1) * D]], axis=1
             )
             done.append(
-                attend(where, queries[None, :, g * width : (g + 1) * width],
-                       weights_t[g * RATIO * FM : (g + 1) * RATIO * FM], kv, f32)
+                attend(where, [queries[:, g * width : (g + 1) * width]],
+                       weights_t[g * RATIO * FM : (g + 1) * RATIO * FM], [kv], f32)
             )
         error = jnp.concatenate([d[0][0] for d in done], axis=1)
         cut = RATIO * FM
@@ -351,17 +391,18 @@
     members = range(groups)
     kv_parts = [jnp.concatenate([of_group(keys, s, D), of_group(values, s, D)], axis=1) for s in members]
     own = jnp.concatenate(in_order(exchange(kv_parts, ctx, 1), number), axis=0)
-    q = jnp.stack(exchange([of_group(queries, s, width) for s in members], ctx, 1))
     earlier = [
         lax.ppermute(own, "ctx", [(i, i + s * groups) for i in range(ctx - s * groups)])
         for s in range(1, slices)
     ]
-    kv = jnp.concatenate(earlier[::-1] + [own], axis=0)
+    queries, own = lax.optimization_barrier((queries, own))
+    q = exchange([of_group(queries, s, width) for s in members], ctx, 1)
+    kv = earlier[::-1] + [own]
     run = groups * rows
     where = jnp.stack([(slices - 1) * run, (slices - 1 - here) * run, number]).astype(jnp.int32)
     w = lax.dynamic_slice_in_dim(weights_t, number * RATIO * FM, RATIO * FM, 0)
     error, gw = attend(where, q, w, kv, bf16)
-    back = in_order(exchange([error[s] for s in members], ctx, 1), number)
+    back = in_order(exchange(error, ctx, 1), number)
     attn_error = jnp.concatenate(back, axis=1).astype(f32)
     gw = pairwise([a.astype(f32) for a in exchange([gw] * slices, ctx, groups)])
     cut = RATIO * FM
@@ -372,12 +413,14 @@
         rest = rest - tail[-1]
     tail = jnp.stack(tail + [jnp.zeros_like(rest)] * (TAIL - 3))
     parts = exchange([jnp.concatenate([gw[:cut], tail]).astype(bf16)] * groups, ctx, 1)
-    square = pairwise([jnp.sum(p[cut : cut + 3, 0].astype(f32)) for p in parts])
+    tails = [p[cut : cut + 3].astype(f32) for p in parts]
+    square = pairwise([a[0] + a[1] + a[2] for a in tails])
     count = lax.axis_size("head")
     if count == 2:
         square = square + lax.ppermute(square, "head", [(0, 1), (1, 0)])
     else:
         square = lax.psum(square, "head")
+    square = square[0]
     gw = jnp.concatenate(in_order([p[:cut] for p in parts], number), axis=0).astype(f32)
     return (attn_error, square / whole, jnp.transpose(gw.reshape(heads, FM, D), (0, 2, 1)))
 

time: 115 us -> 101 us (0.88)
  waiting for transfers between devices: 20.5 us -> 29.6 us
  Pallas kernels: 27.9 us -> 20.6 us
  starting transfers between devices: 46.8 us -> 39.8 us
  other arithmetic: 8.93 us -> 5.55 us
  between operations: 5.31 us -> 2.09 us
  local copies, waits for them, and re-layouts: 5.19 us -> 3.28 us
    ppermute x15, waiting for transfers between devices: 10.7 us -> 24.7 us  [exchange(): lax.ppermute(part, 'ctx', [(i, i ^ s * unit) for i in range(ctx)])]
    pallas_call x1, Pallas kernels: 27.9 us -> 20.6 us  [attend(): pl.pallas_call(functools.partial(kernel, blocks, pieces), name='attend',...]
    ppermute x15, starting transfers between devices: 34.6 us -> 28.6 us  [exchange(): lax.ppermute(part, 'ctx', [(i, i ^ s * unit) for i in range(ctx)])]
    ppermute x3, waiting for transfers between devices: 9.74 us -> 4.09 us  [shards(): lax.ppermute(own, 'ctx', [(i, i + s * groups) for i in range(ctx - s * gr...]
    reduce_sum x4 -> x0, other arithmetic: 2.41 us -> none  [shards(): square = pairwise([jnp.sum(p[cut:cut + 3, 0].astype(f32)) for p in parts])]
    ppermute x1, starting transfers between devices: 2.85 us -> 1.56 us  [shards(): square = square + lax.ppermute(square, 'head', [(0, 1), (1, 0)])]
    another operation x1 -> x0, local copies, waits for them, and re-layouts: 1.26 us -> none  [shards(): jnp.stack(exchange([of_group(queries, s, width) for s in members], ctx, 1))]
    squeeze x1 -> x0, local copies, waits for them, and re-layouts: 1.16 us -> none  [shards(): back = in_order(exchange([error[s] for s in members], ctx, 1), number)]
  transfers between devices with their start and end apart: 19 -> 19, of which waited for: 8 -> 10; matrix products, arithmetic and copies ran while one was open for 10% -> 6% of each run, Pallas kernels for 0% -> 0%
where the time goes in v3:
time: 101 us
  starting transfers between devices  39.8 us (39%)
  waiting for transfers between devices  29.6 us (29%)
  Pallas kernels  20.6 us (20%)
  other arithmetic  5.55 us (5%)
  local copies, waits for them, and re-layouts  3.28 us (3%)
  between operations  2.09 us (2%)
    ppermute x15, starting transfers between devices, exchange(): lax.ppermute(part, 'ctx', [(i, i ^ s * unit) for i in range(ctx)])  28.6 us
    ppermute x15, waiting for transfers between devices, exchange(): lax.ppermute(part, 'ctx', [(i, i ^ s * unit) for i in range(ctx)])  24.7 us
    pallas_call x1, Pallas kernels, attend(): pl.pallas_call(functools.partial(kernel, blocks, pieces), name='attend',...  20.6 us
    ppermute x3, starting transfers between devices, shards(): lax.ppermute(own, 'ctx', [(i, i + s * groups) for i in range(ctx - s * gr...  9.59 us
    ppermute x3, waiting for transfers between devices, shards(): lax.ppermute(own, 'ctx', [(i, i + s * groups) for i in range(ctx - s * gr...  4.09 us
  transfers between devices with their start and end apart: 19, of which 10 were waited for; matrix products, arithmetic and copies ran while one was open for 6% of the time, Pallas kernels for 0%

profile of v3, /device:TPU:0, one launch (start us, length us, event | category | flops | bytes accessed | tf_op | source)
XLA Modules:
  0.0 100.9 jit_solution(16853501636581276815)
XLA Ops:
  0.6 0.0 copy-start
  0.7 1.0 %constant_dynamic-slice_fusion.5 = (bf16[128,128]{1,0:T(8,128)(2,1)S(1)}, bf16[128,128]{1,0:T(8,128)(2,1)S(1)}, bf16[128,128]{1,0:T(8,128)(2,1)S(1)}, bf16[128,1...) fusion(bf16[128,512]{1,0:T(8,128)(2,1)} %param.6, ...), kind=kLoop, calls=%fused_computation.39 | loop fusion | bytes 524304 | tf_op jit(solution)/shard_map/dynamic_slice | solution.py:389
  1.7 2.5 %collective-permute-start = (bf16[128,256]{1,0:T(8,128)(2,1)S(1)}, bf16[128,256]{1,0:T(8,128)(2,1)S(1)}, u32[]{:S(2)}, u32[]{:S(2)}) collective-permute-start(bf16[128,256]{1,0:T(8,128)(2,1)S(1)} %pad_maximum_fusion.2), channel_id=1, source_target_pairs={{0,6},{2,4},{4,2},{6,0},{8,14},{10,12},{12,10},{14,8},{16,22},{18,... | collective-permute-start | bytes 196616 | tf_op jit(solution)/shard_map/ppermute | solution.py:335
  4.2 0.6 collective-permute-start.1
  4.9 0.2 collective-permute-start.2
  5.0 1.6 %collective-permute-done = bf16[128,256]{1,0:T(8,128)(2,1)S(1)} collective-permute-done((bf16[128,256]{1,0:T(8,128)(2,1)S(1)}, bf16[128,256]{1,0:T(8,128)(2,1)S(1)}, u32[]{:S(2)}, u32[]{:S(2)}) %collective-permute-start) | collective-permute-done | bytes 65568 | tf_op jit(solution)/shard_map/ppermute | solution.py:335
  6.7 2.3 %collective-permute-done.1 = bf16[128,256]{1,0:T(8,128)(2,1)S(1)} collective-permute-done((bf16[128,256]{1,0:T(8,128)(2,1)S(1)}, bf16[128,256]{1,0:T(8,128)(2,1)S(1)}, u32[]{:S(2)}, u32[]{:S(2)}) %collective-permute-start.1) | collective-permute-done | bytes 65568 | tf_op jit(solution)/shard_map/ppermute | solution.py:335
  8.9 0.0 collective-permute-done.2
  9.0 0.1 broadcast_select_fusion.23
  9.1 0.8 constant_dynamic-slice_fusion.1
  9.9 0.0 collective-permute-start.3
  9.9 5.6 %collective-permute-start.6 = (bf16[512,256]{1,0:T(8,128)(2,1)S(1)}, bf16[512,256]{1,0:T(8,128)(2,1)S(1)}, u32[]{:S(2)}, u32[]{:S(2)}) collective-permute-start(bf16[512,256]{1,0:T(8,128)(2,1)S(1)} %pad_maximum_fusion.1.refs_8_), channel_id=1, source_target_pairs={{0,24},{2,26},{4,28},{6,30},{1,25},{3,27},{5,29},{7,31}} | collective-permute-start | bytes 786440 | tf_op jit(solution)/shard_map/ppermute | solution.py:395
  15.5 1.7 %collective-permute-start.4 = (bf16[128,1024]{1,0:T(8,128)(2,1)S(1)}, bf16[128,1024]{1,0:T(8,128)(2,1)S(1)}, u32[]{:S(2)}, u32[]{:S(2)}) collective-permute-start(bf16[128,1024]{1,0:T(8,128)(2,1)S(1)} %get-tuple-element.24), channel_id=1, source_target_pairs={{0,4},{2,6},{4,0},{6,2},{8,12},{10,14},{12,8},{14,10},{16,20},{18,... | collective-permute-start | bytes 786440 | tf_op jit(solution)/shard_map/ppermute | solution.py:335
  17.2 0.0 collective-permute-start.5
  17.2 1.3 %collective-permute-start.7 = (bf16[512,256]{1,0:T(8,128)(2,1)S(1)}, bf16[512,256]{1,0:T(8,128)(2,1)S(1)}, u32[]{:S(2)}, u32[]{:S(2)}) collective-permute-start(bf16[512,256]{1,0:T(8,128)(2,1)S(1)} %pad_maximum_fusion.1.refs_8_), channel_id=1, source_target_pairs={{0,16},{2,18},{4,20},{6,22},{8,24},{10,26},{12,28},{14,30},{1,17},... | collective-permute-start | bytes 786440 | tf_op jit(solution)/shard_map/ppermute | solution.py:395
  18.5 0.0 collective-permute-done.3.refs_1_
  18.5 0.0 copy-start.3
  18.5 2.7 %collective-permute-start.8 = (bf16[512,256]{1,0:T(8,128)(2,1)S(1)}, bf16[512,256]{1,0:T(8,128)(2,1)S(1)}, u32[]{:S(2)}, u32[]{:S(2)}) collective-permute-start(bf16[512,256]{1,0:T(8,128)(2,1)S(1)} %pad_maximum_fusion.1.refs_8_), channel_id=1, source_target_pairs={{0,8},{2,10},{4,12},{6,14},{8,16},{10,18},{12,20},{14,22},{16,24},... | collective-permute-start | bytes 786440 | tf_op jit(solution)/shard_map/ppermute | solution.py:395
  21.2 0.7 pad_add_fusion.where_ref
  21.9 0.7 constant_dynamic-slice_fusion.refs_4_
  22.6 2.1 %collective-permute-done.4.refs_2_ = bf16[128,1024]{1,0:T(8,128)(2,1)S(1)} collective-permute-done((bf16[128,1024]{1,0:T(8,128)(2,1)S(1)}, bf16[128,1024]{1,0:T(8,128)(2,1)S(1)}, u32[]{:S(2)}, u32[]{:S(2)}) %collective-permute-start.4) | collective-permute-done | bytes 262176 | tf_op jit(solution)/shard_map/ppermute | solution.py:335
  24.7 4.2 %collective-permute-done.5.refs_3_ = bf16[128,1024]{1,0:T(8,128)(2,1)S(1)} collective-permute-done((bf16[128,1024]{1,0:T(8,128)(2,1)S(1)}, bf16[128,1024]{1,0:T(8,128)(2,1)S(1)}, u32[]{:S(2)}, u32[]{:S(2)}) %collective-permute-start.5) | collective-permute-done | bytes 262176 | tf_op jit(solution)/shard_map/ppermute | solution.py:335
  28.9 0.0 collective-permute-done.6.refs_5_
  28.9 4.1 %collective-permute-done.8.refs_7_ = bf16[512,256]{1,0:T(8,128)(2,1)S(1)} collective-permute-done((bf16[512,256]{1,0:T(8,128)(2,1)S(1)}, bf16[512,256]{1,0:T(8,128)(2,1)S(1)}, u32[]{:S(2)}, u32[]{:S(2)}) %collective-permute-start.8) | collective-permute-done | bytes 262176 | tf_op jit(solution)/shard_map/ppermute | solution.py:395
  33.1 0.7 copy-done.8
  33.7 20.6 %attend.1 = (bf16[128,1024]{1,0:T(8,128)(2,1)}, bf16[128,1024]{1,0:T(8,128)(2,1)}, bf16[128,1024]{1,0:T(8,128)(2,1)}, bf16[128,1024]{1,0:T(8,128)(2,1)}, bf16[528,128]{1,0:T(8,128)(2,1)}) custom-call(s32[3]{0:T(128)} %pad_add_fusion.where_ref, bf16[128,1024]{1,0:T(8,128)(2,1)} %get-tuple-element.26.refs_0_, bf16[128,1024]{1,0:T(8,128)(2,1)} %copy-done.3, ...), custom_call_target="tpu_custom_call" | custom-call | flops 6442450944 | bytes 3145728 | tf_op jit(solution)/shard_map/attend/pallas_call | solution.py:292
  54.3 19.2 %collective-permute-start.14 = (bf16[528,128]{1,0:T(8,128)(2,1)}, bf16[528,128]{1,0:T(8,128)(2,1)S(1)}, u32[]{:S(2)}, u32[]{:S(2)}) collective-permute-start(bf16[528,128]{1,0:T(8,128)(2,1)} %get-tuple-element.16), channel_id=1, source_target_pairs={{0,24},{2,26},{4,28},{6,30},{8,16},{10,18},{12,20},{14,22},{16,8},... | collective-permute-start | bytes 405512 | tf_op jit(solution)/shard_map/ppermute | solution.py:335
  73.5 0.4 collective-permute-start.13
  73.8 0.5 collective-permute-start.12
  74.4 0.6 collective-permute-start.9
  75.0 0.9 collective-permute-start.10
  75.9 1.8 %collective-permute-done.14 = bf16[528,128]{1,0:T(8,128)(2,1)S(1)} collective-permute-done((bf16[528,128]{1,0:T(8,128)(2,1)}, bf16[528,128]{1,0:T(8,128)(2,1)S(1)}, u32[]{:S(2)}, u32[]{:S(2)}) %collective-permute-start.14) | collective-permute-done | bytes 135200 | tf_op jit(solution)/shard_map/ppermute | solution.py:335
  77.8 8.3 %collective-permute-done.13 = bf16[528,128]{1,0:T(8,128)(2,1)S(1)} collective-permute-done((bf16[528,128]{1,0:T(8,128)(2,1)}, bf16[528,128]{1,0:T(8,128)(2,1)S(1)}, u32[]{:S(2)}, u32[]{:S(2)}) %collective-permute-start.13) | collective-permute-done | bytes 135200 | tf_op jit(solution)/shard_map/ppermute | solution.py:335
  86.1 1.0 add_add_fusion
  87.1 0.1 concatenate.43
  87.2 1.3 %collective-permute-start.17 = (bf16[528,128]{1,0:T(8,128)(2,1)S(1)}, bf16[528,128]{1,0:T(8,128)(2,1)S(1)}, u32[]{:S(2)}, u32[]{:S(2)}) collective-permute-start(bf16[528,128]{1,0:T(8,128)(2,1)S(1)} %concatenate.43), channel_id=1, source_target_pairs={{0,6},{2,4},{4,2},{6,0},{8,14},{10,12},{12,10},{14,8},{16,22},{18,... | collective-permute-start | bytes 405512 | tf_op jit(solution)/shard_map/ppermute | solution.py:335
  88.5 0.5 collective-permute-start.16
  89.0 0.2 collective-permute-start.15
  89.2 0.0 collective-permute-done.10
  89.2 0.0 collective-permute-done.11
  89.2 1.0 %broadcast_select_fusion.7 = (bf16[128,1024]{1,0:T(8,128)(2,1)S(1)}, bf16[128,1024]{1,0:T(8,128)(2,1)S(1)}, bf16[128,1024]{1,0:T(8,128)(2,1)S(1)}, bf16[128,1024]{1,0:T(8,128)(2,1)S(1)}) fusion(pred[]{:T(512)S(6)} %gt.4, bf16[128,1024]{1,0:T(8,128)(2,1)S(1)} %collective-permute-done.9, bf16[128,1024]{1,0:T(8,128)(2,1)S(1)} %collective-permute-done.10, ...), kind=kLoop, calls=%fused_computation.13 | loop fusion | flops 1048576 | bytes 2097154 | tf_op jit(solution)/shard_map/jit(_where)/select_n | solution.py:350
  90.3 1.5 %maximum_convert_fusion = f32[128,4096]{1,0:T(8,128)} fusion(bf16[128,1024]{1,0:T(8,128)(2,1)S(1)} %get-tuple-element.22, bf16[128,1024]{1,0:T(8,128)(2,1)S(1)} %get-tuple-element.21, bf16[128,1024]{1,0:T(8,128)(2,1)S(1)} %get-tuple-element.20, bf16[128,1024]{1,0:T(8,128)(2,1)S(1)} %get-tuple-element.19), kind=kLoop, calls=%fused_computation | loop fusion | flops 4194304 | bytes 3145728 | tf_op jit(solution)/shard_map/convert_element_type | solution.py:406
  91.8 1.1 %collective-permute-done.17 = bf16[528,128]{1,0:T(8,128)(2,1)S(1)} collective-permute-done((bf16[528,128]{1,0:T(8,128)(2,1)S(1)}, bf16[528,128]{1,0:T(8,128)(2,1)S(1)}, u32[]{:S(2)}, u32[]{:S(2)}) %collective-permute-start.17) | collective-permute-done | bytes 135200 | tf_op jit(solution)/shard_map/ppermute | solution.py:335
  92.9 3.1 %collective-permute-done.16 = bf16[528,128]{1,0:T(8,128)(2,1)S(1)} collective-permute-done((bf16[528,128]{1,0:T(8,128)(2,1)S(1)}, bf16[528,128]{1,0:T(8,128)(2,1)S(1)}, u32[]{:S(2)}, u32[]{:S(2)}) %collective-permute-start.16) | collective-permute-done | bytes 135200 | tf_op jit(solution)/shard_map/ppermute | solution.py:335
  96.1 1.6 %collective-permute-start.18 = (f32[128]{0:T(128)S(1)}, f32[128]{0:T(128)S(1)}, u32[]{:S(2)}, u32[]{:S(2)}) collective-permute-start(f32[128]{0:T(128)S(1)} %add_bitcast_fusion), channel_id=1, source_target_pairs={{0,1},{1,0},{2,3},{3,2},{4,5},{5,4},{6,7},{7,6},{8,9},{9,8},{10,11... | collective-permute-start | bytes 1544 | tf_op jit(solution)/shard_map/ppermute | solution.py:420
  97.6 0.1 broadcast_select_fusion.15
  97.8 1.1 %convert_bitcast_fusion = f32[32,128,64]{1,2,0:T(8,128)} fusion(bf16[32,64,128]{2,1,0:T(8,128)(2,1)S(1)} %bitcast.14), kind=kLoop, calls=%fused_computation.1 | loop fusion | flops 262144 | bytes 1572864 | tf_op jit(solution)/shard_map/transpose | solution.py:425
  98.8 0.8 collective-permute-done.18
  (37 shorter events, 0.2 us)
Async XLA Ops:
  0.6 21.3 %copy-start = (bf16[32,128,64]{1,2,0:T(8,128)(2,1)S(1)}, bf16[32,128,64]{1,2,0:T(8,128)(2,1)}, u32[]{:S(2)}) copy-start(bf16[32,128,64]{1,2,0:T(8,128)(2,1)} %param.7) | copy-start | bytes 1572868
  0.6 8.4 %copy-start.1 = (bf16[128,4096]{1,0:T(8,128)(2,1)S(1)}, bf16[128,4096]{1,0:T(8,128)(2,1)}, u32[]{:S(2)}) copy-start(bf16[128,4096]{1,0:T(8,128)(2,1)} %param.4) | copy-start | bytes 3145732
  1.7 5.0 %collective-permute-start = (bf16[128,256]{1,0:T(8,128)(2,1)S(1)}, bf16[128,256]{1,0:T(8,128)(2,1)S(1)}, u32[]{:S(2)}, u32[]{:S(2)}) collective-permute-start(bf16[128,256]{1,0:T(8,128)(2,1)S(1)} %pad_maximum_fusion.2), channel_id=1, source_target_pairs={{0,6},{2,4},{4,2},{6,0},{8,14},{10,12},{12,10},{14,8},{16,22},{18,... | collective-permute-start | bytes 196616 | tf_op jit(solution)/shard_map/ppermute | solution.py:335
  4.2 4.7 %collective-permute-start.1 = (bf16[128,256]{1,0:T(8,128)(2,1)S(1)}, bf16[128,256]{1,0:T(8,128)(2,1)S(1)}, u32[]{:S(2)}, u32[]{:S(2)}) collective-permute-start(bf16[128,256]{1,0:T(8,128)(2,1)S(1)} %pad_maximum_fusion.3), channel_id=1, source_target_pairs={{0,4},{2,6},{4,0},{6,2},{8,12},{10,14},{12,8},{14,10},{16,20},{18,... | collective-permute-start | bytes 196616 | tf_op jit(solution)/shard_map/ppermute | solution.py:335
  4.9 4.1 %collective-permute-start.2 = (bf16[128,256]{1,0:T(8,128)(2,1)S(1)}, bf16[128,256]{1,0:T(8,128)(2,1)S(1)}, u32[]{:S(2)}, u32[]{:S(2)}) collective-permute-start(bf16[128,256]{1,0:T(8,128)(2,1)S(1)} %pad_maximum_fusion.4), channel_id=1, source_target_pairs={{0,2},{2,0},{4,6},{6,4},{8,10},{10,8},{12,14},{14,12},{16,18},{18,... | collective-permute-start | bytes 196616 | tf_op jit(solution)/shard_map/ppermute | solution.py:335
  9.1 24.0 %copy-start.2 = (bf16[512,256]{1,0:T(8,128)(2,1)}, bf16[512,256]{1,0:T(8,128)(2,1)S(1)}, u32[]{:S(2)}) copy-start(bf16[512,256]{1,0:T(8,128)(2,1)S(1)} %pad_maximum_fusion.1.refs_8_) | copy-start | bytes 786436
  9.9 8.6 %collective-permute-start.3 = (bf16[128,1024]{1,0:T(8,128)(2,1)S(1)}, bf16[128,1024]{1,0:T(8,128)(2,1)S(1)}, u32[]{:S(2)}, u32[]{:S(2)}) collective-permute-start(bf16[128,1024]{1,0:T(8,128)(2,1)S(1)} %get-tuple-element.25), channel_id=1, source_target_pairs={{0,2},{2,0},{4,6},{6,4},{8,10},{10,8},{12,14},{14,12},{16,18},{18,... | collective-permute-start | bytes 786440 | tf_op jit(solution)/shard_map/ppermute | solution.py:335
  9.9 19.0 %collective-permute-start.6 = (bf16[512,256]{1,0:T(8,128)(2,1)S(1)}, bf16[512,256]{1,0:T(8,128)(2,1)S(1)}, u32[]{:S(2)}, u32[]{:S(2)}) collective-permute-start(bf16[512,256]{1,0:T(8,128)(2,1)S(1)} %pad_maximum_fusion.1.refs_8_), channel_id=1, source_target_pairs={{0,24},{2,26},{4,28},{6,30},{1,25},{3,27},{5,29},{7,31}} | collective-permute-start | bytes 786440 | tf_op jit(solution)/shard_map/ppermute | solution.py:395
  15.5 9.2 %collective-permute-start.4 = (bf16[128,1024]{1,0:T(8,128)(2,1)S(1)}, bf16[128,1024]{1,0:T(8,128)(2,1)S(1)}, u32[]{:S(2)}, u32[]{:S(2)}) collective-permute-start(bf16[128,1024]{1,0:T(8,128)(2,1)S(1)} %get-tuple-element.24), channel_id=1, source_target_pairs={{0,4},{2,6},{4,0},{6,2},{8,12},{10,14},{12,8},{14,10},{16,20},{18,... | collective-permute-start | bytes 786440 | tf_op jit(solution)/shard_map/ppermute | solution.py:335
  17.2 11.7 %collective-permute-start.5 = (bf16[128,1024]{1,0:T(8,128)(2,1)S(1)}, bf16[128,1024]{1,0:T(8,128)(2,1)S(1)}, u32[]{:S(2)}, u32[]{:S(2)}) collective-permute-start(bf16[128,1024]{1,0:T(8,128)(2,1)S(1)} %get-tuple-element.23), channel_id=1, source_target_pairs={{0,6},{2,4},{4,2},{6,0},{8,14},{10,12},{12,10},{14,8},{16,22},{18,... | collective-permute-start | bytes 786440 | tf_op jit(solution)/shard_map/ppermute | solution.py:335
  17.2 11.7 %collective-permute-start.7 = (bf16[512,256]{1,0:T(8,128)(2,1)S(1)}, bf16[512,256]{1,0:T(8,128)(2,1)S(1)}, u32[]{:S(2)}, u32[]{:S(2)}) collective-permute-start(bf16[512,256]{1,0:T(8,128)(2,1)S(1)} %pad_maximum_fusion.1.refs_8_), channel_id=1, source_target_pairs={{0,16},{2,18},{4,20},{6,22},{8,24},{10,26},{12,28},{14,30},{1,17},... | collective-permute-start | bytes 786440 | tf_op jit(solution)/shard_map/ppermute | solution.py:395
  18.5 14.5 %copy-start.3 = (bf16[128,1024]{1,0:T(8,128)(2,1)}, bf16[128,1024]{1,0:T(8,128)(2,1)S(1)}, u32[]{:S(2)}) copy-start(bf16[128,1024]{1,0:T(8,128)(2,1)S(1)} %collective-permute-done.3.refs_1_) | copy-start | bytes 786436
  18.5 14.5 %collective-permute-start.8 = (bf16[512,256]{1,0:T(8,128)(2,1)S(1)}, bf16[512,256]{1,0:T(8,128)(2,1)S(1)}, u32[]{:S(2)}, u32[]{:S(2)}) collective-permute-start(bf16[512,256]{1,0:T(8,128)(2,1)S(1)} %pad_maximum_fusion.1.refs_8_), channel_id=1, source_target_pairs={{0,8},{2,10},{4,12},{6,14},{8,16},{10,18},{12,20},{14,22},{16,24},... | collective-permute-start | bytes 786440 | tf_op jit(solution)/shard_map/ppermute | solution.py:395
  24.7 8.3 %copy-start.5 = (bf16[128,1024]{1,0:T(8,128)(2,1)}, bf16[128,1024]{1,0:T(8,128)(2,1)S(1)}, u32[]{:S(2)}) copy-start(bf16[128,1024]{1,0:T(8,128)(2,1)S(1)} %collective-permute-done.4.refs_2_) | copy-start | bytes 786436
  28.9 4.1 %copy-start.6 = (bf16[128,1024]{1,0:T(8,128)(2,1)}, bf16[128,1024]{1,0:T(8,128)(2,1)S(1)}, u32[]{:S(2)}) copy-start(bf16[128,1024]{1,0:T(8,128)(2,1)S(1)} %collective-permute-done.5.refs_3_) | copy-start | bytes 786436
  28.9 4.1 %copy-start.4 = (bf16[512,256]{1,0:T(8,128)(2,1)}, bf16[512,256]{1,0:T(8,128)(2,1)S(1)}, u32[]{:S(2)}) copy-start(bf16[512,256]{1,0:T(8,128)(2,1)S(1)} %collective-permute-done.6.refs_5_) | copy-start | bytes 786436
  28.9 4.1 %copy-start.7 = (bf16[512,256]{1,0:T(8,128)(2,1)}, bf16[512,256]{1,0:T(8,128)(2,1)S(1)}, u32[]{:S(2)}) copy-start(bf16[512,256]{1,0:T(8,128)(2,1)S(1)} %collective-permute-done.7.refs_6_) | copy-start | bytes 786436
  33.0 0.7 copy-start.8
  54.3 23.5 %collective-permute-start.14 = (bf16[528,128]{1,0:T(8,128)(2,1)}, bf16[528,128]{1,0:T(8,128)(2,1)S(1)}, u32[]{:S(2)}, u32[]{:S(2)}) collective-permute-start(bf16[528,128]{1,0:T(8,128)(2,1)} %get-tuple-element.16), channel_id=1, source_target_pairs={{0,24},{2,26},{4,28},{6,30},{8,16},{10,18},{12,20},{14,22},{16,8},... | collective-permute-start | bytes 405512 | tf_op jit(solution)/shard_map/ppermute | solution.py:335
  73.5 12.6 %collective-permute-start.13 = (bf16[528,128]{1,0:T(8,128)(2,1)}, bf16[528,128]{1,0:T(8,128)(2,1)S(1)}, u32[]{:S(2)}, u32[]{:S(2)}) collective-permute-start(bf16[528,128]{1,0:T(8,128)(2,1)} %get-tuple-element.16), channel_id=1, source_target_pairs={{0,16},{2,18},{4,20},{6,22},{8,24},{10,26},{12,28},{14,30},{16,0},... | collective-permute-start | bytes 405512 | tf_op jit(solution)/shard_map/ppermute | solution.py:335
  73.8 12.2 %collective-permute-start.12 = (bf16[528,128]{1,0:T(8,128)(2,1)}, bf16[528,128]{1,0:T(8,128)(2,1)S(1)}, u32[]{:S(2)}, u32[]{:S(2)}) collective-permute-start(bf16[528,128]{1,0:T(8,128)(2,1)} %get-tuple-element.16), channel_id=1, source_target_pairs={{0,8},{2,10},{4,12},{6,14},{8,0},{10,2},{12,4},{14,6},{16,24},{18,... | collective-permute-start | bytes 405512 | tf_op jit(solution)/shard_map/ppermute | solution.py:335
  74.4 14.6 %collective-permute-start.9 = (bf16[128,1024]{1,0:T(8,128)(2,1)}, bf16[128,1024]{1,0:T(8,128)(2,1)S(1)}, u32[]{:S(2)}, u32[]{:S(2)}) collective-permute-start(bf16[128,1024]{1,0:T(8,128)(2,1)} %get-tuple-element.12), channel_id=1, source_target_pairs={{0,6},{2,4},{4,2},{6,0},{8,14},{10,12},{12,10},{14,8},{16,22},{18,... | collective-permute-start | bytes 786440 | tf_op jit(solution)/shard_map/ppermute | solution.py:335
  75.0 14.2 %collective-permute-start.10 = (bf16[128,1024]{1,0:T(8,128)(2,1)}, bf16[128,1024]{1,0:T(8,128)(2,1)S(1)}, u32[]{:S(2)}, u32[]{:S(2)}) collective-permute-start(bf16[128,1024]{1,0:T(8,128)(2,1)} %get-tuple-element.13), channel_id=1, source_target_pairs={{0,4},{2,6},{4,0},{6,2},{8,12},{10,14},{12,8},{14,10},{16,20},{18,... | collective-permute-start | bytes 786440 | tf_op jit(solution)/shard_map/ppermute | solution.py:335
  77.8 11.5 %collective-permute-start.11 = (bf16[128,1024]{1,0:T(8,128)(2,1)}, bf16[128,1024]{1,0:T(8,128)(2,1)S(1)}, u32[]{:S(2)}, u32[]{:S(2)}) collective-permute-start(bf16[128,1024]{1,0:T(8,128)(2,1)} %get-tuple-element.14), channel_id=1, source_target_pairs={{0,2},{2,0},{4,6},{6,4},{8,10},{10,8},{12,14},{14,12},{16,18},{18,... | collective-permute-start | bytes 786440 | tf_op jit(solution)/shard_map/ppermute | solution.py:335
  87.2 5.7 %collective-permute-start.17 = (bf16[528,128]{1,0:T(8,128)(2,1)S(1)}, bf16[528,128]{1,0:T(8,128)(2,1)S(1)}, u32[]{:S(2)}, u32[]{:S(2)}) collective-permute-start(bf16[528,128]{1,0:T(8,128)(2,1)S(1)} %concatenate.43), channel_id=1, source_target_pairs={{0,6},{2,4},{4,2},{6,0},{8,14},{10,12},{12,10},{14,8},{16,22},{18,... | collective-permute-start | bytes 405512 | tf_op jit(solution)/shard_map/ppermute | solution.py:335
  88.5 7.6 %collective-permute-start.16 = (bf16[528,128]{1,0:T(8,128)(2,1)S(1)}, bf16[528,128]{1,0:T(8,128)(2,1)S(1)}, u32[]{:S(2)}, u32[]{:S(2)}) collective-permute-start(bf16[528,128]{1,0:T(8,128)(2,1)S(1)} %concatenate.43), channel_id=1, source_target_pairs={{0,4},{2,6},{4,0},{6,2},{8,12},{10,14},{12,8},{14,10},{16,20},{18,... | collective-permute-start | bytes 405512 | tf_op jit(solution)/shard_map/ppermute | solution.py:335
  89.0 7.1 %collective-permute-start.15 = (bf16[528,128]{1,0:T(8,128)(2,1)S(1)}, bf16[528,128]{1,0:T(8,128)(2,1)S(1)}, u32[]{:S(2)}, u32[]{:S(2)}) collective-permute-start(bf16[528,128]{1,0:T(8,128)(2,1)S(1)} %concatenate.43), channel_id=1, source_target_pairs={{0,2},{2,0},{4,6},{6,4},{8,10},{10,8},{12,14},{14,12},{16,18},{18,... | collective-permute-start | bytes 405512 | tf_op jit(solution)/shard_map/ppermute | solution.py:335
  96.1 3.6 %collective-permute-start.18 = (f32[128]{0:T(128)S(1)}, f32[128]{0:T(128)S(1)}, u32[]{:S(2)}, u32[]{:S(2)}) collective-permute-start(f32[128]{0:T(128)S(1)} %add_bitcast_fusion), channel_id=1, source_target_pairs={{0,1},{1,0},{2,3},{3,2},{4,5},{5,4},{6,7},{7,6},{8,9},{9,8},{10,11... | collective-permute-start | bytes 1544 | tf_op jit(solution)/shard_map/ppermute | solution.py:420

commit v4 on v3

--- a/solution.py
+++ b/solution.py
@@ -52,14 +52,13 @@
     return jnp.concatenate([v, jnp.ones_like(v) if other is None else other], axis=1)
 
 
-def kernel(blocks, pieces, where_ref, *refs):
-    q_refs, (w_ref, *kv_refs), err_refs, (out_ref, *scratch) = (
+def near_kernel(blocks, pieces, most, where_ref, *refs):
+    q_refs, (w_ref, *kv_refs), (m_ref, acc, den, phiq), (kv_ref, qs, qc) = (
         refs[:blocks],
         refs[blocks : blocks + 1 + pieces],
-        refs[blocks + 1 + pieces : 2 * blocks + 1 + pieces],
-        refs[2 * blocks + 1 + pieces :],
+        refs[blocks + 1 + pieces : blocks + 5 + pieces],
+        refs[blocks + 5 + pieces :],
     )
-    (kv_ref, errs, gw_ref, square, qs, qc, m_ref, acc, state, lsum, lx, xs, phiq, den) = scratch
     rows = q_refs[0].shape[0]
     D = HEAD_SIZE
     block = pl.program_id(0)
@@ -90,9 +89,10 @@
 
     @pl.when(block == 0)
     def _():
-        for k, ref in enumerate(kv_refs):
-            n = ref.shape[0]
-            kv_ref[k * n : (k + 1) * n, :] = ref[...]
+        first = 0
+        for ref in kv_refs:
+            kv_ref[first : first + ref.shape[0], :] = ref[...]
+            first += ref.shape[0]
 
     w = w_ref[...]
 
@@ -142,6 +142,99 @@
             p = jnp.exp2(s - jnp.concatenate([new] * (n // D), axis=1)).astype(bf16)
             acc[c, :] = acc[c, :] * jnp.concatenate([a, a], axis=1) + dot(p, vc, 1, 0)
 
+    def sweep(step, stop):
+        def body(t, c):
+            step(pl.multiple_of(low + t * most * rows, rows), most * rows)
+            return c
+
+        lax.fori_loop(0, (stop - low) // (most * rows), body, 0)
+        size = most // 2
+        while size:
+            left = (stop - low) % (2 * size * rows)
+
+            @pl.when(left >= size * rows)
+            def _(size=size, left=left):
+                step(pl.multiple_of(stop - left, rows), size * rows)
+
+            size //= 2
+
+    sweep(teacher_step, dbase)
+
+
+def far_kernel(blocks, pieces, most, where_ref, *refs):
+    n_in = blocks + 5 + pieces
+    q_refs, (w_ref, m_in, acc_in, den, phiq, *kv_refs), err_refs, (out_ref, *scratch) = (
+        refs[:blocks],
+        refs[blocks:n_in],
+        refs[n_in : n_in + blocks],
+        refs[n_in + blocks :],
+    )
+    (kv_ref, errs, gw_ref, square, qs, qc, m_ref, acc, state, lsum, lx, xs) = scratch
+    rows = q_refs[0].shape[0]
+    D = HEAD_SIZE
+    block = pl.program_id(0)
+    piece = where_ref[2] ^ block
+    low = pl.multiple_of(where_ref[1], rows)
+
+    def reach(b):
+        return pl.multiple_of(jnp.maximum(where_ref[0] + (b - 1) * rows, low), rows)
+
+    start = where_ref[0] + block * rows
+    dbase = reach(block)
+    span = 2 * rows
+    heads = range(RATIO)
+    hr = [slice(h * rows, (h + 1) * rows) for h in heads]
+    hf = [slice(h * 2 * FM, (h + 1) * 2 * FM) for h in heads]
+    hw = [slice(h * FM, (h + 1) * FM) for h in heads]
+
+    for k, q_ref in enumerate(q_refs):
+
+        @pl.when(piece == k)
+        def _(q_ref=q_ref):
+            for h in heads:
+                q = q_ref[:, h * D : (h + 1) * D]
+                qs[hr[h], :] = q
+                scaled = q.astype(f32) * (SCALE * LOG2E)
+                high = scaled.astype(bf16)
+                qc[hr[h], :] = widened(high, (scaled - high.astype(f32)).astype(bf16))
+
+    @pl.when(block == 0)
+    def _():
+        first = 0
+        for ref in kv_refs:
+            kv_ref[first : first + ref.shape[0], :] = ref[...]
+            first += ref.shape[0]
+
+    w = w_ref[...]
+    m_ref[...] = m_in[...]
+    acc[...] = acc_in[...]
+
+    kd = kv_ref[pl.ds(dbase, span), :D]
+    vd = kv_ref[pl.ds(dbase, span), D:]
+    vx = widened(vd)
+    i_pos = start + lax.broadcasted_iota(jnp.int32, (rows, span), 0)
+    j_pos = dbase + lax.broadcasted_iota(jnp.int32, (rows, span), 1)
+    causal = j_pos <= i_pos
+    far = j_pos < i_pos - WIN
+    window = jnp.logical_and(causal, jnp.logical_not(far))
+    xd = dot(w, kd, 1, 1).astype(bf16)
+    phikd = key_features(xd, RATIO)
+
+    def teacher_step(j0, n):
+        kc = kv_ref[pl.ds(j0, n), :D]
+        kk = widened(kc, kc)
+        vc = widened(kv_ref[pl.ds(j0, n), D:])
+        size = RATIO * rows // 4
+        cuts = [slice(i * size, (i + 1) * size) for i in range(4)]
+        scores = [dot(qc[c, :], kk, 1, 1) for c in cuts]
+        for c, s in zip(cuts, scores):
+            old = m_ref[c, :]
+            new = jnp.maximum(old, jnp.max(s, axis=1, keepdims=True))
+            m_ref[c, :] = new
+            a = jnp.exp2(old - new)
+            p = jnp.exp2(s - jnp.concatenate([new] * (n // D), axis=1)).astype(bf16)
+            acc[c, :] = acc[c, :] * jnp.concatenate([a, a], axis=1) + dot(p, vc, 1, 0)
+
     def state_step(j0, n):
         kc = kv_ref[pl.ds(j0, n), :D]
         vc = widened(kv_ref[pl.ds(j0, n), D:])
@@ -153,28 +246,22 @@
             state[c, :] += dot(key_features(x, size), vc, 1, 0)
 
     def sweep(step, stop):
-        count = (stop - low) // (8 * rows)
-
         def body(t, c):
-            step(pl.multiple_of(low + t * 8 * rows, rows), 8 * rows)
+            step(pl.multiple_of(low + t * most * rows, rows), most * rows)
             return c
 
-        lax.fori_loop(0, count, body, 0)
-        left = (stop - low) % (8 * rows)
-
-        @pl.when(left >= 4 * rows)
-        def _():
-            step(pl.multiple_of(low + count * 8 * rows, rows), 4 * rows)
-
-        @pl.when(left % (4 * rows) >= 2 * rows)
-        def _():
-            step(pl.multiple_of(stop - left % (4 * rows), rows), 2 * rows)
-
-        @pl.when(left % (2 * rows) > 0)
-        def _():
-            step(pl.multiple_of(stop - rows, rows), rows)
-
-    sweep(teacher_step, dbase)
+        lax.fori_loop(0, (stop - low) // (most * rows), body, 0)
+        size = most // 2
+        while size:
+            left = (stop - low) % (2 * size * rows)
+
+            @pl.when(left >= size * rows)
+            def _(size=size, left=left):
+                step(pl.multiple_of(stop - left, rows), size * rows)
+
+            size //= 2
+
+    sweep(teacher_step, reach(0))
 
     @pl.when(block == 0)
     def _():
@@ -278,10 +365,9 @@
         out_ref[RATIO * FM :, :] = tail.astype(out_ref.dtype)
 
 
-def attend(where, queries, weights_t, kv, out_type):
-    blocks, pieces = len(queries), len(kv)
+def attend(near, where, queries, weights_t, kv_near, kv, out_type):
+    blocks = len(queries)
     rows, width = queries[0].shape
-    tokens = sum(a.shape[0] for a in kv)
     D = HEAD_SIZE
     R = RATIO * rows
     F = RATIO * 2 * FM
@@ -289,44 +375,72 @@
     def all_of(shape):
         return pl.BlockSpec(shape, lambda b, p: (0, 0), pipeline_mode=pl.Buffered(1))
 
-    *error, gw = pl.pallas_call(
-        functools.partial(kernel, blocks, pieces),
-        name="attend",
-        out_shape=[jax.ShapeDtypeStruct((rows, width), out_type)] * blocks
+    def each(a):
+        return pl.BlockSpec((pl.Squeezed(), *a.shape[1:]), lambda b, p: (b, 0, 0))
+
+    def call(body, name, place, pieces, more, out_shape, out_specs, scratch, keys, most):
+        return pl.pallas_call(
+            functools.partial(body, blocks, len(pieces), most),
+            name=name,
+            out_shape=out_shape,
+            grid_spec=pltpu.PrefetchScalarGridSpec(
+                num_scalar_prefetch=1,
+                grid=(blocks,),
+                in_specs=[all_of((rows, width))] * blocks
+                + [all_of((RATIO * FM, D))]
+                + [each(a) for a in more]
+                + [all_of(a.shape) for a in pieces],
+                out_specs=out_specs,
+                scratch_shapes=scratch,
+            ),
+            compiler_params=pltpu.CompilerParams(
+                dimension_semantics=("arbitrary",), vmem_limit_bytes=56 << 20
+            ),
+            cost_estimate=pl.CostEstimate(
+                flops=blocks * R * keys * D * 6,
+                bytes_accessed=keys * 4 * D + R * blocks * D * 4,
+                transcendentals=blocks * R * keys,
+            ),
+        )(place, *queries, weights_t, *more, *pieces)
+
+    sums = [
+        jax.ShapeDtypeStruct((blocks, R, D), f32),
+        jax.ShapeDtypeStruct((blocks, R, 2 * D), f32),
+        jax.ShapeDtypeStruct((blocks, R, 2 * D), f32),
+        jax.ShapeDtypeStruct((blocks, R, 2 * FM), bf16),
+    ]
+    tokens = sum(a.shape[0] for a in kv_near)
+    sums = call(
+        near_kernel, "near", near, kv_near, [], sums, [each(a) for a in sums],
+        [
+            pltpu.VMEM((tokens, 2 * D), bf16),
+            pltpu.VMEM((R, D), bf16),
+            pltpu.VMEM((R, 2 * D), bf16),
+        ],
+        tokens, 2 if blocks > 2 else 1,
+    )
+    tokens = sum(a.shape[0] for a in kv)
+    *error, gw = call(
+        far_kernel, "far", where, kv, sums,
+        [jax.ShapeDtypeStruct((rows, width), out_type)] * blocks
         + [jax.ShapeDtypeStruct((RATIO * FM + TAIL, D), out_type)],
-        grid_spec=pltpu.PrefetchScalarGridSpec(
-            num_scalar_prefetch=1,
-            grid=(blocks,),
-            in_specs=[all_of((rows, width))] * blocks
-            + [all_of((RATIO * FM, D))]
-            + [all_of(a.shape) for a in kv],
-            out_specs=[all_of((rows, width))] * blocks + [all_of((RATIO * FM + TAIL, D))],
-            scratch_shapes=[
-                pltpu.VMEM((tokens, 2 * D), bf16),
-                pltpu.VMEM((rows, width), out_type),
-                pltpu.VMEM((RATIO * FM, D), f32),
-                pltpu.VMEM((8, D), f32),
-                pltpu.VMEM((R, D), bf16),
-                pltpu.VMEM((R, 2 * D), bf16),
-                pltpu.VMEM((R, D), f32),
-                pltpu.VMEM((R, 2 * D), f32),
-                pltpu.VMEM((F, 2 * D), f32),
-                pltpu.VMEM((blocks, F, 2 * D), f32),
-                pltpu.VMEM((F, 2 * D), bf16),
-                pltpu.VMEM((RATIO * FM, tokens), bf16),
-                pltpu.VMEM((R, 2 * FM), bf16),
-                pltpu.VMEM((R, 2 * D), f32),
-            ],
-        ),
-        compiler_params=pltpu.CompilerParams(
-            dimension_semantics=("arbitrary",), vmem_limit_bytes=56 << 20
-        ),
-        cost_estimate=pl.CostEstimate(
-            flops=blocks * R * tokens * D * 6,
-            bytes_accessed=tokens * 4 * D + R * blocks * D * 4,
-            transcendentals=blocks * R * tokens,
-        ),
-    )(where, *queries, weights_t, *kv)
+        [all_of((rows, width))] * blocks + [all_of((RATIO * FM + TAIL, D))],
+        [
+            pltpu.VMEM((tokens, 2 * D), bf16),
+            pltpu.VMEM((rows, width), out_type),
+            pltpu.VMEM((RATIO * FM, D), f32),
+            pltpu.VMEM((8, D), f32),
+            pltpu.VMEM((R, D), bf16),
+            pltpu.VMEM((R, 2 * D), bf16),
+            pltpu.VMEM((R, D), f32),
+            pltpu.VMEM((R, 2 * D), f32),
+            pltpu.VMEM((F, 2 * D), f32),
+            pltpu.VMEM((blocks, F, 2 * D), f32),
+            pltpu.VMEM((F, 2 * D), bf16),
+            pltpu.VMEM((RATIO * FM, tokens), bf16),
+        ],
+        tokens, 8,
+    )
     return error, gw
 
 
@@ -366,14 +480,17 @@
     if not split:
         everything = lax.all_gather(jnp.concatenate([keys, values], axis=1), "ctx", axis=0, tiled=True)
         where = jnp.stack([place * rows, 0, 0]).astype(jnp.int32)
+        near = jnp.stack([rows, jnp.where(place > 0, 0, rows), 0]).astype(jnp.int32)
         done = []
         for g in range(groups):
             kv = jnp.concatenate(
                 [everything[:, g * D : (g + 1) * D], everything[:, (groups + g) * D : (groups + g + 1) * D]], axis=1
             )
+            mine = jnp.concatenate([keys[:, g * D : (g + 1) * D], values[:, g * D : (g + 1) * D]], axis=1)
+            before = lax.dynamic_slice_in_dim(kv, jnp.maximum(place - 1, 0) * rows, rows, 0)
             done.append(
-                attend(where, [queries[:, g * width : (g + 1) * width]],
-                       weights_t[g * RATIO * FM : (g + 1) * RATIO * FM], [kv], f32)
+                attend(near, where, [queries[:, g * width : (g + 1) * width]],
+                       weights_t[g * RATIO * FM : (g + 1) * RATIO * FM], [before, mine, before], [kv], f32)
             )
         error = jnp.concatenate([d[0][0] for d in done], axis=1)
         cut = RATIO * FM
@@ -391,17 +508,18 @@
     members = range(groups)
     kv_parts = [jnp.concatenate([of_group(keys, s, D), of_group(values, s, D)], axis=1) for s in members]
     own = jnp.concatenate(in_order(exchange(kv_parts, ctx, 1), number), axis=0)
+    before = lax.ppermute(own[-rows:], "ctx", [(i, i + groups) for i in range(ctx - groups)])
+    q = exchange([of_group(queries, s, width) for s in members], ctx, 1)
     earlier = [
         lax.ppermute(own, "ctx", [(i, i + s * groups) for i in range(ctx - s * groups)])
         for s in range(1, slices)
     ]
-    queries, own = lax.optimization_barrier((queries, own))
-    q = exchange([of_group(queries, s, width) for s in members], ctx, 1)
     kv = earlier[::-1] + [own]
     run = groups * rows
     where = jnp.stack([(slices - 1) * run, (slices - 1 - here) * run, number]).astype(jnp.int32)
+    near = jnp.stack([rows, jnp.where(here > 0, 0, rows), number]).astype(jnp.int32)
     w = lax.dynamic_slice_in_dim(weights_t, number * RATIO * FM, RATIO * FM, 0)
-    error, gw = attend(where, q, w, kv, bf16)
+    error, gw = attend(near, where, q, w, [before, own], kv, bf16)
     back = in_order(exchange(error, ctx, 1), number)
     attn_error = jnp.concatenate(back, axis=1).astype(f32)
     gw = pairwise([a.astype(f32) for a in exchange([gw] * slices, ctx, groups)])

time: 101 us -> 101 us (level)
  waiting for transfers between devices: 29.6 us -> 13.5 us
  Pallas kernels: 20.6 us -> 27.8 us
  starting transfers between devices: 39.8 us -> 45.5 us
  local copies, waits for them, and re-layouts: 3.28 us -> 5.36 us
    ppermute x15, waiting for transfers between devices: 24.7 us -> 12.6 us  [exchange(): lax.ppermute(part, 'ctx', [(i, i ^ s * unit) for i in range(ctx)])]
    pallas_call x1 -> x2, Pallas kernels: 20.6 us -> 27.8 us  [call(): pl.pallas_call(functools.partial(body, blocks, len(pieces), most), name=n...]
    ppermute x3, waiting for transfers between devices: 4.09 us -> 0.01 us  [shards(): lax.ppermute(own, 'ctx', [(i, i + s * groups) for i in range(ctx - s * gr...]
    ppermute x0 -> x1, starting transfers between devices: none -> 3.51 us  [shards(): lax.ppermute(own[-rows:], 'ctx', [(i, i + groups) for i in range(ctx - gr...]
    ppermute x3, starting transfers between devices: 9.59 us -> 10.9 us  [shards(): lax.ppermute(own, 'ctx', [(i, i + s * groups) for i in range(ctx - s * gr...]
    dynamic_slice x2, local copies, waits for them, and re-layouts: 1.82 us -> 2.96 us  [of_group(): return lax.dynamic_slice_in_dim(a, (number ^ s) * n, n, 1)]
  transfers between devices with their start and end apart: 19 -> 20, of which waited for: 10 -> 5; matrix products, arithmetic and copies ran while one was open for 6% -> 9% of each run, Pallas kernels for 0% -> 11%
where the time goes in v4:
time: 101 us; the launch traced here: 100 us
  starting transfers between devices  45.5 us (45%)
  Pallas kernels  27.8 us (28%)
  waiting for transfers between devices  13.5 us (13%)
  other arithmetic  6.08 us (6%)
  local copies, waits for them, and re-layouts  5.36 us (5%)
  between operations  2.15 us (2%)
    ppermute x15, starting transfers between devices, exchange(): lax.ppermute(part, 'ctx', [(i, i ^ s * unit) for i in range(ctx)])  29.6 us
    pallas_call x2, Pallas kernels, call(): pl.pallas_call(functools.partial(body, blocks, len(pieces), most), name=n...  27.8 us
    ppermute x15, waiting for transfers between devices, exchange(): lax.ppermute(part, 'ctx', [(i, i ^ s * unit) for i in range(ctx)])  12.6 us
    ppermute x3, starting transfers between devices, shards(): lax.ppermute(own, 'ctx', [(i, i + s * groups) for i in range(ctx - s * gr...  10.9 us
    ppermute x1, starting transfers between devices, shards(): lax.ppermute(own[-rows:], 'ctx', [(i, i + groups) for i in range(ctx - gr...  3.51 us
    dynamic_slice x2, local copies, waits for them, and re-layouts, of_group(): return lax.dynamic_slice_in_dim(a, (number ^ s) * n, n, 1)  2.96 us
  transfers between devices with their start and end apart: 20, of which 5 were waited for; matrix products, arithmetic and copies ran while one was open for 9% of the time, Pallas kernels for 11%

profile of v4, /device:TPU:0, one launch (start us, length us, event | category | flops | bytes accessed | tf_op | source)
XLA Modules:
  0.0 100.4 jit_solution(9836257085841981316)
XLA Ops:
  0.6 0.0 copy-start
  0.7 1.0 constant_dynamic-slice_fusion.6
  1.7 0.5 collective-permute-start.3
  2.2 2.6 %collective-permute-start.4 = (bf16[128,256]{1,0:T(8,128)(2,1)S(1)}, bf16[128,256]{1,0:T(8,128)(2,1)S(1)}, u32[]{:S(2)}, u32[]{:S(2)}) collective-permute-start(bf16[128,256]{1,0:T(8,128)(2,1)S(1)} %pad_maximum_fusion.4), channel_id=1, source_target_pairs={{0,4},{2,6},{4,0},{6,2},{8,12},{10,14},{12,8},{14,10},{16,20},{18,... | collective-permute-start | bytes 196616 | tf_op jit(solution)/shard_map/ppermute | solution.py:449
  4.8 0.2 collective-permute-start.5
  5.0 2.0 %constant_dynamic-slice_fusion.9 = (bf16[128,1024]{1,0:T(8,128)(2,1)S(1)}, bf16[128,1024]{1,0:T(8,128)(2,1)S(1)}, bf16[128,1024]{1,0:T(8,128)(2,1)}, bf16[128,1024]{1,0:T(8,128)(2,1)S(1)}) fusion(bf16[128,4096]{1,0:T(8,128)(2,1)} %param.4, s32[]{:T(128)S(6)} %select_n.167, s32[]{:T(128)S(6)} %select_n.165, s32[]{:T(128)S(6)} %select_n.164, s32[]{:T(128)S(6)} %select_n.166), kind=kLoop, calls=%fused_computation.43 | loop fusion | bytes 2097168 | tf_op jit(solution)/shard_map/dynamic_slice | solution.py:506
  7.0 0.1 collective-permute-start
  7.1 1.9 %collective-permute-start.1 = (bf16[128,1024]{1,0:T(8,128)(2,1)S(1)}, bf16[128,1024]{1,0:T(8,128)(2,1)S(1)}, u32[]{:S(2)}, u32[]{:S(2)}) collective-permute-start(bf16[128,1024]{1,0:T(8,128)(2,1)S(1)} %get-tuple-element.30), channel_id=1, source_target_pairs={{0,4},{2,6},{4,0},{6,2},{8,12},{10,14},{12,8},{14,10},{16,20},{18,... | collective-permute-start | bytes 786440 | tf_op jit(solution)/shard_map/ppermute | solution.py:449
  9.0 0.7 constant_dynamic-slice_fusion.8.refs_4_
  9.7 0.6 add_add_fusion.2.where_ref
  10.3 0.0 collective-permute-done.4
  10.3 0.1 broadcast_select_fusion.22
  10.4 3.5 %collective-permute-start.6 = (bf16[128,256]{1,0:T(8,128)(2,1)S(1)}, bf16[128,256]{1,0:T(8,128)(2,1)S(1)}, u32[]{:S(2)}, u32[]{:S(2)}) collective-permute-start(bf16[128,256]{1,0:T(8,128)(2,1)S(1)} %get-tuple-element.38), channel_id=1, source_target_pairs={{0,8},{2,10},{4,12},{6,14},{8,16},{10,18},{12,20},{14,22},{16,24},... | collective-permute-start | bytes 196616 | tf_op jit(solution)/shard_map/ppermute | solution.py:511
  13.9 3.3 %collective-permute-start.7 = (bf16[512,256]{1,0:T(8,128)(2,1)S(1)}, bf16[512,256]{1,0:T(8,128)(2,1)S(1)}, u32[]{:S(2)}, u32[]{:S(2)}) collective-permute-start(bf16[512,256]{1,0:T(8,128)(2,1)S(1)} %pad_maximum_fusion.1.refs_6_.refs_12_), channel_id=1, source_target_pairs={{0,24},{2,26},{4,28},{6,30},{1,25},{3,27},{5,29},{7,31}} | collective-permute-start | bytes 786440 | tf_op jit(solution)/shard_map/ppermute | solution.py:514
  17.3 0.0 collective-permute-done.6.refs_5_
  17.3 4.1 %collective-permute-start.8 = (bf16[512,256]{1,0:T(8,128)(2,1)S(1)}, bf16[512,256]{1,0:T(8,128)(2,1)S(1)}, u32[]{:S(2)}, u32[]{:S(2)}) collective-permute-start(bf16[512,256]{1,0:T(8,128)(2,1)S(1)} %pad_maximum_fusion.1.refs_6_.refs_12_), channel_id=1, source_target_pairs={{0,16},{2,18},{4,20},{6,22},{8,24},{10,26},{12,28},{14,30},{1,17},... | collective-permute-start | bytes 786440 | tf_op jit(solution)/shard_map/ppermute | solution.py:514
  21.4 3.5 %collective-permute-start.9 = (bf16[512,256]{1,0:T(8,128)(2,1)S(1)}, bf16[512,256]{1,0:T(8,128)(2,1)S(1)}, u32[]{:S(2)}, u32[]{:S(2)}) collective-permute-start(bf16[512,256]{1,0:T(8,128)(2,1)S(1)} %pad_maximum_fusion.1.refs_6_.refs_12_), channel_id=1, source_target_pairs={{0,8},{2,10},{4,12},{6,14},{8,16},{10,18},{12,20},{14,22},{16,24},... | collective-permute-start | bytes 786440 | tf_op jit(solution)/shard_map/ppermute | solution.py:514
  24.9 0.6 add_add_fusion.1.where_ref
  25.5 0.0 collective-permute-done.1.refs_2_
  25.5 0.0 collective-permute-done.2.refs_3_
  25.6 0.6 copy-done.3
  26.2 0.1 copy-done.4
  26.3 10.8 %near.1 = (f32[4,1024,128]{2,1,0:T(8,128)}, f32[4,1024,256]{2,1,0:T(8,128)}, f32[4,1024,256]{2,1,0:T(8,128)}, bf16[4,1024,128]{2,1,0:T(8,128)(2,1)}) custom-call(s32[3]{0:T(128)} %add_add_fusion.2.where_ref, bf16[128,1024]{1,0:T(8,128)(2,1)} %get-tuple-element.29.refs_0_, bf16[128,1024]{1,0:T(8,128)(2,1)} %copy-done.2, bf16[128,1024]{1,0:T(8,128)(2,1)} %copy-done.3, ...), custom_call_target="tpu_custom_call" | custom-call | flops 2013265920 | bytes 2424832 | tf_op jit(solution)/shard_map/near/pallas_call | solution.py:382
  37.2 0.6 copy-done.5
  37.8 0.1 copy-done.6
  37.9 0.1 copy-done.7
  38.0 17.0 %far.1 = (bf16[128,1024]{1,0:T(8,128)(2,1)}, bf16[128,1024]{1,0:T(8,128)(2,1)}, bf16[128,1024]{1,0:T(8,128)(2,1)}, bf16[128,1024]{1,0:T(8,128)(2,1)}, bf16[528,128]{1,0:T(8,128)(2,1)}) custom-call(s32[3]{0:T(128)} %add_add_fusion.1.where_ref, bf16[128,1024]{1,0:T(8,128)(2,1)} %get-tuple-element.29.refs_0_, bf16[128,1024]{1,0:T(8,128)(2,1)} %copy-done.2, ...), custom_call_target="tpu_custom_call" | custom-call | flops 6442450944 | bytes 3145728 | tf_op jit(solution)/shard_map/far/pallas_call | solution.py:382
  55.0 12.0 %collective-permute-start.13 = (bf16[528,128]{1,0:T(8,128)(2,1)}, bf16[528,128]{1,0:T(8,128)(2,1)S(1)}, u32[]{:S(2)}, u32[]{:S(2)}) collective-permute-start(bf16[528,128]{1,0:T(8,128)(2,1)} %get-tuple-element.20), channel_id=1, source_target_pairs={{0,8},{2,10},{4,12},{6,14},{8,0},{10,2},{12,4},{14,6},{16,24},{18,... | collective-permute-start | bytes 405512 | tf_op jit(solution)/shard_map/ppermute | solution.py:449
  67.0 7.0 %collective-permute-start.14 = (bf16[528,128]{1,0:T(8,128)(2,1)}, bf16[528,128]{1,0:T(8,128)(2,1)S(1)}, u32[]{:S(2)}, u32[]{:S(2)}) collective-permute-start(bf16[528,128]{1,0:T(8,128)(2,1)} %get-tuple-element.20), channel_id=1, source_target_pairs={{0,16},{2,18},{4,20},{6,22},{8,24},{10,26},{12,28},{14,30},{16,0},... | collective-permute-start | bytes 405512 | tf_op jit(solution)/shard_map/ppermute | solution.py:449
  74.1 1.4 %collective-permute-start.15 = (bf16[528,128]{1,0:T(8,128)(2,1)}, bf16[528,128]{1,0:T(8,128)(2,1)S(1)}, u32[]{:S(2)}, u32[]{:S(2)}) collective-permute-start(bf16[528,128]{1,0:T(8,128)(2,1)} %get-tuple-element.20), channel_id=1, source_target_pairs={{0,24},{2,26},{4,28},{6,30},{8,16},{10,18},{12,20},{14,22},{16,8},... | collective-permute-start | bytes 405512 | tf_op jit(solution)/shard_map/ppermute | solution.py:449
  75.4 0.6 collective-permute-start.10
  76.0 1.0 collective-permute-start.11
  77.0 0.3 collective-permute-start.12
  77.3 1.1 %collective-permute-done.14 = bf16[528,128]{1,0:T(8,128)(2,1)S(1)} collective-permute-done((bf16[528,128]{1,0:T(8,128)(2,1)}, bf16[528,128]{1,0:T(8,128)(2,1)S(1)}, u32[]{:S(2)}, u32[]{:S(2)}) %collective-permute-start.14) | collective-permute-done | bytes 135200 | tf_op jit(solution)/shard_map/ppermute | solution.py:449
  78.4 6.6 %collective-permute-done.15 = bf16[528,128]{1,0:T(8,128)(2,1)S(1)} collective-permute-done((bf16[528,128]{1,0:T(8,128)(2,1)}, bf16[528,128]{1,0:T(8,128)(2,1)S(1)}, u32[]{:S(2)}, u32[]{:S(2)}) %collective-permute-start.15) | collective-permute-done | bytes 135200 | tf_op jit(solution)/shard_map/ppermute | solution.py:449
  85.0 1.0 add_add_fusion
  86.1 0.1 concatenate.43
  86.2 0.1 collective-permute-start.16
  86.2 1.6 %collective-permute-start.17 = (bf16[528,128]{1,0:T(8,128)(2,1)S(1)}, bf16[528,128]{1,0:T(8,128)(2,1)S(1)}, u32[]{:S(2)}, u32[]{:S(2)}) collective-permute-start(bf16[528,128]{1,0:T(8,128)(2,1)S(1)} %concatenate.43), channel_id=1, source_target_pairs={{0,4},{2,6},{4,0},{6,2},{8,12},{10,14},{12,8},{14,10},{16,20},{18,... | collective-permute-start | bytes 405512 | tf_op jit(solution)/shard_map/ppermute | solution.py:449
  87.8 0.4 collective-permute-start.18
  88.2 1.8 %collective-permute-done.11 = bf16[128,1024]{1,0:T(8,128)(2,1)S(1)} collective-permute-done((bf16[128,1024]{1,0:T(8,128)(2,1)}, bf16[128,1024]{1,0:T(8,128)(2,1)S(1)}, u32[]{:S(2)}, u32[]{:S(2)}) %collective-permute-start.11) | collective-permute-done | bytes 262176 | tf_op jit(solution)/shard_map/ppermute | solution.py:449
  89.9 1.0 %broadcast_select_fusion.7 = (bf16[128,1024]{1,0:T(8,128)(2,1)S(1)}, bf16[128,1024]{1,0:T(8,128)(2,1)S(1)}, bf16[128,1024]{1,0:T(8,128)(2,1)S(1)}, bf16[128,1024]{1,0:T(8,128)(2,1)S(1)}) fusion(pred[]{:T(512)S(6)} %gt.6, bf16[128,1024]{1,0:T(8,128)(2,1)S(1)} %collective-permute-done.10, bf16[128,1024]{1,0:T(8,128)(2,1)S(1)} %collective-permute-done.11, ...), kind=kLoop, calls=%fused_computation.13 | loop fusion | flops 1048576 | bytes 2097154 | tf_op jit(solution)/shard_map/jit(_where)/select_n | solution.py:464
  91.0 1.5 %maximum_convert_fusion = f32[128,4096]{1,0:T(8,128)} fusion(bf16[128,1024]{1,0:T(8,128)(2,1)S(1)} %get-tuple-element.26, bf16[128,1024]{1,0:T(8,128)(2,1)S(1)} %get-tuple-element.25, bf16[128,1024]{1,0:T(8,128)(2,1)S(1)} %get-tuple-element.24, bf16[128,1024]{1,0:T(8,128)(2,1)S(1)} %get-tuple-element.23), kind=kLoop, calls=%fused_computation | loop fusion | flops 4194304 | bytes 3145728 | tf_op jit(solution)/shard_map/convert_element_type | solution.py:524
  92.5 3.1 %collective-permute-done.18 = bf16[528,128]{1,0:T(8,128)(2,1)S(1)} collective-permute-done((bf16[528,128]{1,0:T(8,128)(2,1)S(1)}, bf16[528,128]{1,0:T(8,128)(2,1)S(1)}, u32[]{:S(2)}, u32[]{:S(2)}) %collective-permute-start.18) | collective-permute-done | bytes 135200 | tf_op jit(solution)/shard_map/ppermute | solution.py:449
  95.7 1.5 %collective-permute-start.19 = (f32[128]{0:T(128)S(1)}, f32[128]{0:T(128)S(1)}, u32[]{:S(2)}, u32[]{:S(2)}) collective-permute-start(f32[128]{0:T(128)S(1)} %add_bitcast_fusion), channel_id=1, source_target_pairs={{0,1},{1,0},{2,3},{3,2},{4,5},{5,4},{6,7},{7,6},{8,9},{9,8},{10,11... | collective-permute-start | bytes 1544 | tf_op jit(solution)/shard_map/ppermute | solution.py:538
  97.2 0.1 broadcast_select_fusion.15
  97.3 1.1 %convert_bitcast_fusion = f32[32,128,64]{1,2,0:T(8,128)} fusion(bf16[32,64,128]{2,1,0:T(8,128)(2,1)S(1)} %bitcast.15), kind=kLoop, calls=%fused_computation.1 | loop fusion | flops 262144 | bytes 1572864 | tf_op jit(solution)/shard_map/transpose | solution.py:543
  98.4 0.9 collective-permute-done.19
  (41 shorter events, 0.2 us)
Async XLA Ops:
  0.6 8.4 %copy-start = (bf16[32,128,64]{1,2,0:T(8,128)(2,1)S(1)}, bf16[32,128,64]{1,2,0:T(8,128)(2,1)}, u32[]{:S(2)}) copy-start(bf16[32,128,64]{1,2,0:T(8,128)(2,1)} %param.7) | copy-start | bytes 1572868
  1.7 8.6 %collective-permute-start.3 = (bf16[128,256]{1,0:T(8,128)(2,1)S(1)}, bf16[128,256]{1,0:T(8,128)(2,1)S(1)}, u32[]{:S(2)}, u32[]{:S(2)}) collective-permute-start(bf16[128,256]{1,0:T(8,128)(2,1)S(1)} %pad_maximum_fusion.3), channel_id=1, source_target_pairs={{0,2},{2,0},{4,6},{6,4},{8,10},{10,8},{12,14},{14,12},{16,18},{18,... | collective-permute-start | bytes 196616 | tf_op jit(solution)/shard_map/ppermute | solution.py:449
  2.2 8.1 %collective-permute-start.4 = (bf16[128,256]{1,0:T(8,128)(2,1)S(1)}, bf16[128,256]{1,0:T(8,128)(2,1)S(1)}, u32[]{:S(2)}, u32[]{:S(2)}) collective-permute-start(bf16[128,256]{1,0:T(8,128)(2,1)S(1)} %pad_maximum_fusion.4), channel_id=1, source_target_pairs={{0,4},{2,6},{4,0},{6,2},{8,12},{10,14},{12,8},{14,10},{16,20},{18,... | collective-permute-start | bytes 196616 | tf_op jit(solution)/shard_map/ppermute | solution.py:449
  4.8 5.5 %collective-permute-start.5 = (bf16[128,256]{1,0:T(8,128)(2,1)S(1)}, bf16[128,256]{1,0:T(8,128)(2,1)S(1)}, u32[]{:S(2)}, u32[]{:S(2)}) collective-permute-start(bf16[128,256]{1,0:T(8,128)(2,1)S(1)} %pad_maximum_fusion.5), channel_id=1, source_target_pairs={{0,6},{2,4},{4,2},{6,0},{8,14},{10,12},{12,10},{14,8},{16,22},{18,... | collective-permute-start | bytes 196616 | tf_op jit(solution)/shard_map/ppermute | solution.py:449
  7.0 14.4 %collective-permute-start = (bf16[128,1024]{1,0:T(8,128)(2,1)S(1)}, bf16[128,1024]{1,0:T(8,128)(2,1)S(1)}, u32[]{:S(2)}, u32[]{:S(2)}) collective-permute-start(bf16[128,1024]{1,0:T(8,128)(2,1)S(1)} %get-tuple-element.28), channel_id=1, source_target_pairs={{0,2},{2,0},{4,6},{6,4},{8,10},{10,8},{12,14},{14,12},{16,18},{18,... | collective-permute-start | bytes 786440 | tf_op jit(solution)/shard_map/ppermute | solution.py:449
  7.1 18.4 %collective-permute-start.1 = (bf16[128,1024]{1,0:T(8,128)(2,1)S(1)}, bf16[128,1024]{1,0:T(8,128)(2,1)S(1)}, u32[]{:S(2)}, u32[]{:S(2)}) collective-permute-start(bf16[128,1024]{1,0:T(8,128)(2,1)S(1)} %get-tuple-element.30), channel_id=1, source_target_pairs={{0,4},{2,6},{4,0},{6,2},{8,12},{10,14},{12,8},{14,10},{16,20},{18,... | collective-permute-start | bytes 786440 | tf_op jit(solution)/shard_map/ppermute | solution.py:449
  10.3 15.2 %collective-permute-start.2 = (bf16[128,1024]{1,0:T(8,128)(2,1)S(1)}, bf16[128,1024]{1,0:T(8,128)(2,1)S(1)}, u32[]{:S(2)}, u32[]{:S(2)}) collective-permute-start(bf16[128,1024]{1,0:T(8,128)(2,1)S(1)} %get-tuple-element.27), channel_id=1, source_target_pairs={{0,6},{2,4},{4,2},{6,0},{8,14},{10,12},{12,10},{14,8},{16,22},{18,... | collective-permute-start | bytes 786440 | tf_op jit(solution)/shard_map/ppermute | solution.py:449
  10.4 6.9 %collective-permute-start.6 = (bf16[128,256]{1,0:T(8,128)(2,1)S(1)}, bf16[128,256]{1,0:T(8,128)(2,1)S(1)}, u32[]{:S(2)}, u32[]{:S(2)}) collective-permute-start(bf16[128,256]{1,0:T(8,128)(2,1)S(1)} %get-tuple-element.38), channel_id=1, source_target_pairs={{0,8},{2,10},{4,12},{6,14},{8,16},{10,18},{12,20},{14,22},{16,24},... | collective-permute-start | bytes 196616 | tf_op jit(solution)/shard_map/ppermute | solution.py:511
  13.9 11.6 %copy-start.1 = (bf16[512,256]{1,0:T(8,128)(2,1)}, bf16[512,256]{1,0:T(8,128)(2,1)S(1)}, u32[]{:S(2)}) copy-start(bf16[512,256]{1,0:T(8,128)(2,1)S(1)} %pad_maximum_fusion.1.refs_6_.refs_12_) | copy-start | bytes 786436
  13.9 23.2 %collective-permute-start.7 = (bf16[512,256]{1,0:T(8,128)(2,1)S(1)}, bf16[512,256]{1,0:T(8,128)(2,1)S(1)}, u32[]{:S(2)}, u32[]{:S(2)}) collective-permute-start(bf16[512,256]{1,0:T(8,128)(2,1)S(1)} %pad_maximum_fusion.1.refs_6_.refs_12_), channel_id=1, source_target_pairs={{0,24},{2,26},{4,28},{6,30},{1,25},{3,27},{5,29},{7,31}} | collective-permute-start | bytes 786440 | tf_op jit(solution)/shard_map/ppermute | solution.py:514
  17.3 8.2 %copy-start.8 = (bf16[128,256]{1,0:T(8,128)(2,1)}, bf16[128,256]{1,0:T(8,128)(2,1)S(1)}, u32[]{:S(2)}) copy-start(bf16[128,256]{1,0:T(8,128)(2,1)S(1)} %collective-permute-done.6.refs_5_) | copy-start | bytes 196612
  17.3 19.8 %collective-permute-start.8 = (bf16[512,256]{1,0:T(8,128)(2,1)S(1)}, bf16[512,256]{1,0:T(8,128)(2,1)S(1)}, u32[]{:S(2)}, u32[]{:S(2)}) collective-permute-start(bf16[512,256]{1,0:T(8,128)(2,1)S(1)} %pad_maximum_fusion.1.refs_6_.refs_12_), channel_id=1, source_target_pairs={{0,16},{2,18},{4,20},{6,22},{8,24},{10,26},{12,28},{14,30},{1,17},... | collective-permute-start | bytes 786440 | tf_op jit(solution)/shard_map/ppermute | solution.py:514
  21.4 4.1 %copy-start.2 = (bf16[128,1024]{1,0:T(8,128)(2,1)}, bf16[128,1024]{1,0:T(8,128)(2,1)S(1)}, u32[]{:S(2)}) copy-start(bf16[128,1024]{1,0:T(8,128)(2,1)S(1)} %collective-permute-done.refs_1_) | copy-start | bytes 786436
  21.4 15.7 %collective-permute-start.9 = (bf16[512,256]{1,0:T(8,128)(2,1)S(1)}, bf16[512,256]{1,0:T(8,128)(2,1)S(1)}, u32[]{:S(2)}, u32[]{:S(2)}) collective-permute-start(bf16[512,256]{1,0:T(8,128)(2,1)S(1)} %pad_maximum_fusion.1.refs_6_.refs_12_), channel_id=1, source_target_pairs={{0,8},{2,10},{4,12},{6,14},{8,16},{10,18},{12,20},{14,22},{16,24},... | collective-permute-start | bytes 786440 | tf_op jit(solution)/shard_map/ppermute | solution.py:514
  25.5 0.7 copy-start.3
  25.5 0.8 copy-start.4
  37.1 0.7 copy-start.5
  37.1 0.8 copy-start.6
  37.1 0.9 copy-start.7
  55.0 22.0 %collective-permute-start.13 = (bf16[528,128]{1,0:T(8,128)(2,1)}, bf16[528,128]{1,0:T(8,128)(2,1)S(1)}, u32[]{:S(2)}, u32[]{:S(2)}) collective-permute-start(bf16[528,128]{1,0:T(8,128)(2,1)} %get-tuple-element.20), channel_id=1, source_target_pairs={{0,8},{2,10},{4,12},{6,14},{8,0},{10,2},{12,4},{14,6},{16,24},{18,... | collective-permute-start | bytes 405512 | tf_op jit(solution)/shard_map/ppermute | solution.py:449
  67.0 11.4 %collective-permute-start.14 = (bf16[528,128]{1,0:T(8,128)(2,1)}, bf16[528,128]{1,0:T(8,128)(2,1)S(1)}, u32[]{:S(2)}, u32[]{:S(2)}) collective-permute-start(bf16[528,128]{1,0:T(8,128)(2,1)} %get-tuple-element.20), channel_id=1, source_target_pairs={{0,16},{2,18},{4,20},{6,22},{8,24},{10,26},{12,28},{14,30},{16,0},... | collective-permute-start | bytes 405512 | tf_op jit(solution)/shard_map/ppermute | solution.py:449
  74.1 11.0 %collective-permute-start.15 = (bf16[528,128]{1,0:T(8,128)(2,1)}, bf16[528,128]{1,0:T(8,128)(2,1)S(1)}, u32[]{:S(2)}, u32[]{:S(2)}) collective-permute-start(bf16[528,128]{1,0:T(8,128)(2,1)} %get-tuple-element.20), channel_id=1, source_target_pairs={{0,24},{2,26},{4,28},{6,30},{8,16},{10,18},{12,20},{14,22},{16,8},... | collective-permute-start | bytes 405512 | tf_op jit(solution)/shard_map/ppermute | solution.py:449
  75.4 12.4 %collective-permute-start.10 = (bf16[128,1024]{1,0:T(8,128)(2,1)}, bf16[128,1024]{1,0:T(8,128)(2,1)S(1)}, u32[]{:S(2)}, u32[]{:S(2)}) collective-permute-start(bf16[128,1024]{1,0:T(8,128)(2,1)} %get-tuple-element.16), channel_id=1, source_target_pairs={{0,6},{2,4},{4,2},{6,0},{8,14},{10,12},{12,10},{14,8},{16,22},{18,... | collective-permute-start | bytes 786440 | tf_op jit(solution)/shard_map/ppermute | solution.py:449
  76.0 13.9 %collective-permute-start.11 = (bf16[128,1024]{1,0:T(8,128)(2,1)}, bf16[128,1024]{1,0:T(8,128)(2,1)S(1)}, u32[]{:S(2)}, u32[]{:S(2)}) collective-permute-start(bf16[128,1024]{1,0:T(8,128)(2,1)} %get-tuple-element.17), channel_id=1, source_target_pairs={{0,4},{2,6},{4,0},{6,2},{8,12},{10,14},{12,8},{14,10},{16,20},{18,... | collective-permute-start | bytes 786440 | tf_op jit(solution)/shard_map/ppermute | solution.py:449
  77.0 13.0 %collective-permute-start.12 = (bf16[128,1024]{1,0:T(8,128)(2,1)}, bf16[128,1024]{1,0:T(8,128)(2,1)S(1)}, u32[]{:S(2)}, u32[]{:S(2)}) collective-permute-start(bf16[128,1024]{1,0:T(8,128)(2,1)} %get-tuple-element.18), channel_id=1, source_target_pairs={{0,2},{2,0},{4,6},{6,4},{8,10},{10,8},{12,14},{14,12},{16,18},{18,... | collective-permute-start | bytes 786440 | tf_op jit(solution)/shard_map/ppermute | solution.py:449
  86.2 9.5 %collective-permute-start.16 = (bf16[528,128]{1,0:T(8,128)(2,1)S(1)}, bf16[528,128]{1,0:T(8,128)(2,1)S(1)}, u32[]{:S(2)}, u32[]{:S(2)}) collective-permute-start(bf16[528,128]{1,0:T(8,128)(2,1)S(1)} %concatenate.43), channel_id=1, source_target_pairs={{0,2},{2,0},{4,6},{6,4},{8,10},{10,8},{12,14},{14,12},{16,18},{18,... | collective-permute-start | bytes 405512 | tf_op jit(solution)/shard_map/ppermute | solution.py:449
  86.2 9.4 %collective-permute-start.17 = (bf16[528,128]{1,0:T(8,128)(2,1)S(1)}, bf16[528,128]{1,0:T(8,128)(2,1)S(1)}, u32[]{:S(2)}, u32[]{:S(2)}) collective-permute-start(bf16[528,128]{1,0:T(8,128)(2,1)S(1)} %concatenate.43), channel_id=1, source_target_pairs={{0,4},{2,6},{4,0},{6,2},{8,12},{10,14},{12,8},{14,10},{16,20},{18,... | collective-permute-start | bytes 405512 | tf_op jit(solution)/shard_map/ppermute | solution.py:449
  87.8 7.8 %collective-permute-start.18 = (bf16[528,128]{1,0:T(8,128)(2,1)S(1)}, bf16[528,128]{1,0:T(8,128)(2,1)S(1)}, u32[]{:S(2)}, u32[]{:S(2)}) collective-permute-start(bf16[528,128]{1,0:T(8,128)(2,1)S(1)} %concatenate.43), channel_id=1, source_target_pairs={{0,6},{2,4},{4,2},{6,0},{8,14},{10,12},{12,10},{14,8},{16,22},{18,... | collective-permute-start | bytes 405512 | tf_op jit(solution)/shard_map/ppermute | solution.py:449
  95.7 3.6 %collective-permute-start.19 = (f32[128]{0:T(128)S(1)}, f32[128]{0:T(128)S(1)}, u32[]{:S(2)}, u32[]{:S(2)}) collective-permute-start(f32[128]{0:T(128)S(1)} %add_bitcast_fusion), channel_id=1, source_target_pairs={{0,1},{1,0},{2,3},{3,2},{4,5},{5,4},{6,7},{7,6},{8,9},{9,8},{10,11... | collective-permute-start | bytes 1544 | tf_op jit(solution)/shard_map/ppermute | solution.py:538

commit v5 on v4

--- a/solution.py
+++ b/solution.py
@@ -151,8 +151,17 @@
         size = most // 2
         while size:
             left = (stop - low) % (2 * size * rows)
-
-            @pl.when(left >= size * rows)
+            more = left >= size * rows
+            if most >= 8 and size <= 2:
+                last = (stop - low) % (4 * rows)
+                more = jnp.logical_and(more, last != 3 * rows)
+                if size == 2:
+
+                    @pl.when(last == 3 * rows)
+                    def _(last=last):
+                        step(pl.multiple_of(stop - last, rows), 3 * rows)
+
+            @pl.when(more)
             def _(size=size, left=left):
                 step(pl.multiple_of(stop - left, rows), size * rows)
 
@@ -254,8 +263,17 @@
         size = most // 2
         while size:
             left = (stop - low) % (2 * size * rows)
-
-            @pl.when(left >= size * rows)
+            more = left >= size * rows
+            if most >= 8 and size <= 2:
+                last = (stop - low) % (4 * rows)
+                more = jnp.logical_and(more, last != 3 * rows)
+                if size == 2:
+
+                    @pl.when(last == 3 * rows)
+                    def _(last=last):
+                        step(pl.multiple_of(stop - last, rows), 3 * rows)
+
+            @pl.when(more)
             def _(size=size, left=left):
                 step(pl.multiple_of(stop - left, rows), size * rows)
 

time: 101 us -> 98.7 us (0.977)
  starting transfers between devices: 45.5 us -> 43.4 us
    ppermute x15, starting transfers between devices: 29.6 us -> 27.5 us  [exchange(): lax.ppermute(part, 'ctx', [(i, i ^ s * unit) for i in range(ctx)])]
where the time goes in v5:
time: 98.7 us; the launch traced here: 98.3 us
  starting transfers between devices  43.4 us (44%)
  Pallas kernels  27.8 us (28%)
  waiting for transfers between devices  13.5 us (14%)
  other arithmetic  6.08 us (6%)
  local copies, waits for them, and re-layouts  5.36 us (5%)
  between operations  2.15 us (2%)
    pallas_call x2, Pallas kernels, call(): pl.pallas_call(functools.partial(body, blocks, len(pieces), most), name=n...  27.8 us
    ppermute x15, starting transfers between devices, exchange(): lax.ppermute(part, 'ctx', [(i, i ^ s * unit) for i in range(ctx)])  27.5 us
    ppermute x15, waiting for transfers between devices, exchange(): lax.ppermute(part, 'ctx', [(i, i ^ s * unit) for i in range(ctx)])  12.6 us
    ppermute x3, starting transfers between devices, shards(): lax.ppermute(own, 'ctx', [(i, i + s * groups) for i in range(ctx - s * gr...  10.9 us
    ppermute x1, starting transfers between devices, shards(): lax.ppermute(own[-rows:], 'ctx', [(i, i + groups) for i in range(ctx - gr...  3.51 us
    dynamic_slice x2, local copies, waits for them, and re-layouts, of_group(): return lax.dynamic_slice_in_dim(a, (number ^ s) * n, n, 1)  2.96 us
  transfers between devices with their start and end apart: 20, of which 5 were waited for; matrix products, arithmetic and copies ran while one was open for 9% of the time, Pallas kernels for 11%

profile of v5, /device:TPU:0, one launch (start us, length us, event | category | flops | bytes accessed | tf_op | source)
XLA Modules:
  0.0 98.3 jit_solution(2823132232841607232)
XLA Ops:
  0.6 0.0 copy-start
  0.7 1.0 constant_dynamic-slice_fusion.6
  1.7 0.5 collective-permute-start.3
  2.2 2.6 %collective-permute-start.4 = (bf16[128,256]{1,0:T(8,128)(2,1)S(1)}, bf16[128,256]{1,0:T(8,128)(2,1)S(1)}, u32[]{:S(2)}, u32[]{:S(2)}) collective-permute-start(bf16[128,256]{1,0:T(8,128)(2,1)S(1)} %pad_maximum_fusion.4), channel_id=1, source_target_pairs={{0,4},{2,6},{4,0},{6,2},{8,12},{10,14},{12,8},{14,10},{16,20},{18,... | collective-permute-start | bytes 196616 | tf_op jit(solution)/shard_map/ppermute | solution.py:467
  4.8 0.2 collective-permute-start.5
  5.0 2.0 %constant_dynamic-slice_fusion.9 = (bf16[128,1024]{1,0:T(8,128)(2,1)S(1)}, bf16[128,1024]{1,0:T(8,128)(2,1)S(1)}, bf16[128,1024]{1,0:T(8,128)(2,1)}, bf16[128,1024]{1,0:T(8,128)(2,1)S(1)}) fusion(bf16[128,4096]{1,0:T(8,128)(2,1)} %param.4, s32[]{:T(128)S(6)} %select_n.167, s32[]{:T(128)S(6)} %select_n.165, s32[]{:T(128)S(6)} %select_n.164, s32[]{:T(128)S(6)} %select_n.166), kind=kLoop, calls=%fused_computation.43 | loop fusion | bytes 2097168 | tf_op jit(solution)/shard_map/dynamic_slice | solution.py:524
  7.0 0.1 collective-permute-start
  7.1 1.9 %collective-permute-start.1 = (bf16[128,1024]{1,0:T(8,128)(2,1)S(1)}, bf16[128,1024]{1,0:T(8,128)(2,1)S(1)}, u32[]{:S(2)}, u32[]{:S(2)}) collective-permute-start(bf16[128,1024]{1,0:T(8,128)(2,1)S(1)} %get-tuple-element.30), channel_id=1, source_target_pairs={{0,4},{2,6},{4,0},{6,2},{8,12},{10,14},{12,8},{14,10},{16,20},{18,... | collective-permute-start | bytes 786440 | tf_op jit(solution)/shard_map/ppermute | solution.py:467
  9.0 0.7 constant_dynamic-slice_fusion.8.refs_4_
  9.7 0.6 add_add_fusion.2.where_ref
  10.3 0.0 collective-permute-done.3
  10.3 0.0 collective-permute-start.2
  10.3 0.0 collective-permute-done.4
  10.3 0.1 broadcast_select_fusion.22
  10.4 3.5 %collective-permute-start.6 = (bf16[128,256]{1,0:T(8,128)(2,1)S(1)}, bf16[128,256]{1,0:T(8,128)(2,1)S(1)}, u32[]{:S(2)}, u32[]{:S(2)}) collective-permute-start(bf16[128,256]{1,0:T(8,128)(2,1)S(1)} %get-tuple-element.38), channel_id=1, source_target_pairs={{0,8},{2,10},{4,12},{6,14},{8,16},{10,18},{12,20},{14,22},{16,24},... | collective-permute-start | bytes 196616 | tf_op jit(solution)/shard_map/ppermute | solution.py:529
  13.9 3.3 %collective-permute-start.7 = (bf16[512,256]{1,0:T(8,128)(2,1)S(1)}, bf16[512,256]{1,0:T(8,128)(2,1)S(1)}, u32[]{:S(2)}, u32[]{:S(2)}) collective-permute-start(bf16[512,256]{1,0:T(8,128)(2,1)S(1)} %pad_maximum_fusion.1.refs_6_.refs_12_), channel_id=1, source_target_pairs={{0,24},{2,26},{4,28},{6,30},{1,25},{3,27},{5,29},{7,31}} | collective-permute-start | bytes 786440 | tf_op jit(solution)/shard_map/ppermute | solution.py:532
  17.3 0.0 collective-permute-done.6.refs_5_
  17.3 4.1 %collective-permute-start.8 = (bf16[512,256]{1,0:T(8,128)(2,1)S(1)}, bf16[512,256]{1,0:T(8,128)(2,1)S(1)}, u32[]{:S(2)}, u32[]{:S(2)}) collective-permute-start(bf16[512,256]{1,0:T(8,128)(2,1)S(1)} %pad_maximum_fusion.1.refs_6_.refs_12_), channel_id=1, source_target_pairs={{0,16},{2,18},{4,20},{6,22},{8,24},{10,26},{12,28},{14,30},{1,17},... | collective-permute-start | bytes 786440 | tf_op jit(solution)/shard_map/ppermute | solution.py:532
  21.4 3.5 %collective-permute-start.9 = (bf16[512,256]{1,0:T(8,128)(2,1)S(1)}, bf16[512,256]{1,0:T(8,128)(2,1)S(1)}, u32[]{:S(2)}, u32[]{:S(2)}) collective-permute-start(bf16[512,256]{1,0:T(8,128)(2,1)S(1)} %pad_maximum_fusion.1.refs_6_.refs_12_), channel_id=1, source_target_pairs={{0,8},{2,10},{4,12},{6,14},{8,16},{10,18},{12,20},{14,22},{16,24},... | collective-permute-start | bytes 786440 | tf_op jit(solution)/shard_map/ppermute | solution.py:532
  24.9 0.6 add_add_fusion.1.where_ref
  25.6 0.6 copy-done.3
  26.2 0.1 copy-done.4
  26.3 10.8 %near.1 = (f32[4,1024,128]{2,1,0:T(8,128)}, f32[4,1024,256]{2,1,0:T(8,128)}, f32[4,1024,256]{2,1,0:T(8,128)}, bf16[4,1024,128]{2,1,0:T(8,128)(2,1)}) custom-call(s32[3]{0:T(128)} %add_add_fusion.2.where_ref, bf16[128,1024]{1,0:T(8,128)(2,1)} %get-tuple-element.29.refs_0_, bf16[128,1024]{1,0:T(8,128)(2,1)} %copy-done.2, bf16[128,1024]{1,0:T(8,128)(2,1)} %copy-done.3, ...), custom_call_target="tpu_custom_call" | custom-call | flops 2013265920 | bytes 2424832 | tf_op jit(solution)/shard_map/near/pallas_call | solution.py:400
  37.2 0.6 copy-done.5
  37.8 0.1 copy-done.6
  37.9 0.1 copy-done.7
  38.0 17.0 %far.1 = (bf16[128,1024]{1,0:T(8,128)(2,1)}, bf16[128,1024]{1,0:T(8,128)(2,1)}, bf16[128,1024]{1,0:T(8,128)(2,1)}, bf16[128,1024]{1,0:T(8,128)(2,1)}, bf16[528,128]{1,0:T(8,128)(2,1)}) custom-call(s32[3]{0:T(128)} %add_add_fusion.1.where_ref, bf16[128,1024]{1,0:T(8,128)(2,1)} %get-tuple-element.29.refs_0_, bf16[128,1024]{1,0:T(8,128)(2,1)} %copy-done.2, ...), custom_call_target="tpu_custom_call" | custom-call | flops 6442450944 | bytes 3145728 | tf_op jit(solution)/shard_map/far/pallas_call | solution.py:400
  55.1 9.9 %collective-permute-start.13 = (bf16[528,128]{1,0:T(8,128)(2,1)}, bf16[528,128]{1,0:T(8,128)(2,1)S(1)}, u32[]{:S(2)}, u32[]{:S(2)}) collective-permute-start(bf16[528,128]{1,0:T(8,128)(2,1)} %get-tuple-element.20), channel_id=1, source_target_pairs={{0,8},{2,10},{4,12},{6,14},{8,0},{10,2},{12,4},{14,6},{16,24},{18,... | collective-permute-start | bytes 405512 | tf_op jit(solution)/shard_map/ppermute | solution.py:467
  64.9 7.0 %collective-permute-start.14 = (bf16[528,128]{1,0:T(8,128)(2,1)}, bf16[528,128]{1,0:T(8,128)(2,1)S(1)}, u32[]{:S(2)}, u32[]{:S(2)}) collective-permute-start(bf16[528,128]{1,0:T(8,128)(2,1)} %get-tuple-element.20), channel_id=1, source_target_pairs={{0,16},{2,18},{4,20},{6,22},{8,24},{10,26},{12,28},{14,30},{16,0},... | collective-permute-start | bytes 405512 | tf_op jit(solution)/shard_map/ppermute | solution.py:467
  72.0 1.4 %collective-permute-start.15 = (bf16[528,128]{1,0:T(8,128)(2,1)}, bf16[528,128]{1,0:T(8,128)(2,1)S(1)}, u32[]{:S(2)}, u32[]{:S(2)}) collective-permute-start(bf16[528,128]{1,0:T(8,128)(2,1)} %get-tuple-element.20), channel_id=1, source_target_pairs={{0,24},{2,26},{4,28},{6,30},{8,16},{10,18},{12,20},{14,22},{16,8},... | collective-permute-start | bytes 405512 | tf_op jit(solution)/shard_map/ppermute | solution.py:467
  73.3 0.6 collective-permute-start.10
  73.9 1.0 %collective-permute-start.11 = (bf16[128,1024]{1,0:T(8,128)(2,1)}, bf16[128,1024]{1,0:T(8,128)(2,1)S(1)}, u32[]{:S(2)}, u32[]{:S(2)}) collective-permute-start(bf16[128,1024]{1,0:T(8,128)(2,1)} %get-tuple-element.17), channel_id=1, source_target_pairs={{0,4},{2,6},{4,0},{6,2},{8,12},{10,14},{12,8},{14,10},{16,20},{18,... | collective-permute-start | bytes 786440 | tf_op jit(solution)/shard_map/ppermute | solution.py:467
  74.9 0.3 collective-permute-start.12
  75.2 1.1 %collective-permute-done.14 = bf16[528,128]{1,0:T(8,128)(2,1)S(1)} collective-permute-done((bf16[528,128]{1,0:T(8,128)(2,1)}, bf16[528,128]{1,0:T(8,128)(2,1)S(1)}, u32[]{:S(2)}, u32[]{:S(2)}) %collective-permute-start.14) | collective-permute-done | bytes 135200 | tf_op jit(solution)/shard_map/ppermute | solution.py:467
  76.3 6.6 %collective-permute-done.15 = bf16[528,128]{1,0:T(8,128)(2,1)S(1)} collective-permute-done((bf16[528,128]{1,0:T(8,128)(2,1)}, bf16[528,128]{1,0:T(8,128)(2,1)S(1)}, u32[]{:S(2)}, u32[]{:S(2)}) %collective-permute-start.15) | collective-permute-done | bytes 135200 | tf_op jit(solution)/shard_map/ppermute | solution.py:467
  82.9 1.0 add_add_fusion
  84.0 0.1 concatenate.43
  84.1 0.1 collective-permute-start.16
  84.1 1.6 %collective-permute-start.17 = (bf16[528,128]{1,0:T(8,128)(2,1)S(1)}, bf16[528,128]{1,0:T(8,128)(2,1)S(1)}, u32[]{:S(2)}, u32[]{:S(2)}) collective-permute-start(bf16[528,128]{1,0:T(8,128)(2,1)S(1)} %concatenate.43), channel_id=1, source_target_pairs={{0,4},{2,6},{4,0},{6,2},{8,12},{10,14},{12,8},{14,10},{16,20},{18,... | collective-permute-start | bytes 405512 | tf_op jit(solution)/shard_map/ppermute | solution.py:467
  85.7 0.4 collective-permute-start.18
  86.1 1.8 %collective-permute-done.11 = bf16[128,1024]{1,0:T(8,128)(2,1)S(1)} collective-permute-done((bf16[128,1024]{1,0:T(8,128)(2,1)}, bf16[128,1024]{1,0:T(8,128)(2,1)S(1)}, u32[]{:S(2)}, u32[]{:S(2)}) %collective-permute-start.11) | collective-permute-done | bytes 262176 | tf_op jit(solution)/shard_map/ppermute | solution.py:467
  87.9 1.0 %broadcast_select_fusion.7 = (bf16[128,1024]{1,0:T(8,128)(2,1)S(1)}, bf16[128,1024]{1,0:T(8,128)(2,1)S(1)}, bf16[128,1024]{1,0:T(8,128)(2,1)S(1)}, bf16[128,1024]{1,0:T(8,128)(2,1)S(1)}) fusion(pred[]{:T(512)S(6)} %gt.6, bf16[128,1024]{1,0:T(8,128)(2,1)S(1)} %collective-permute-done.10, bf16[128,1024]{1,0:T(8,128)(2,1)S(1)} %collective-permute-done.11, ...), kind=kLoop, calls=%fused_computation.13 | loop fusion | flops 1048576 | bytes 2097154 | tf_op jit(solution)/shard_map/jit(_where)/select_n | solution.py:482
  88.9 1.5 %maximum_convert_fusion = f32[128,4096]{1,0:T(8,128)} fusion(bf16[128,1024]{1,0:T(8,128)(2,1)S(1)} %get-tuple-element.26, bf16[128,1024]{1,0:T(8,128)(2,1)S(1)} %get-tuple-element.25, bf16[128,1024]{1,0:T(8,128)(2,1)S(1)} %get-tuple-element.24, bf16[128,1024]{1,0:T(8,128)(2,1)S(1)} %get-tuple-element.23), kind=kLoop, calls=%fused_computation | loop fusion | flops 4194304 | bytes 3145728 | tf_op jit(solution)/shard_map/convert_element_type | solution.py:542
  90.4 3.1 %collective-permute-done.18 = bf16[528,128]{1,0:T(8,128)(2,1)S(1)} collective-permute-done((bf16[528,128]{1,0:T(8,128)(2,1)S(1)}, bf16[528,128]{1,0:T(8,128)(2,1)S(1)}, u32[]{:S(2)}, u32[]{:S(2)}) %collective-permute-start.18) | collective-permute-done | bytes 135200 | tf_op jit(solution)/shard_map/ppermute | solution.py:467
  93.5 1.5 %collective-permute-start.19 = (f32[128]{0:T(128)S(1)}, f32[128]{0:T(128)S(1)}, u32[]{:S(2)}, u32[]{:S(2)}) collective-permute-start(f32[128]{0:T(128)S(1)} %add_bitcast_fusion), channel_id=1, source_target_pairs={{0,1},{1,0},{2,3},{3,2},{4,5},{5,4},{6,7},{7,6},{8,9},{9,8},{10,11... | collective-permute-start | bytes 1544 | tf_op jit(solution)/shard_map/ppermute | solution.py:556
  95.1 0.1 broadcast_select_fusion.15
  95.2 1.1 %convert_bitcast_fusion = f32[32,128,64]{1,2,0:T(8,128)} fusion(bf16[32,64,128]{2,1,0:T(8,128)(2,1)S(1)} %bitcast.15), kind=kLoop, calls=%fused_computation.1 | loop fusion | flops 262144 | bytes 1572864 | tf_op jit(solution)/shard_map/transpose | solution.py:561
  96.3 0.9 collective-permute-done.19
  (41 shorter events, 0.2 us)
Async XLA Ops:
  0.6 8.4 %copy-start = (bf16[32,128,64]{1,2,0:T(8,128)(2,1)S(1)}, bf16[32,128,64]{1,2,0:T(8,128)(2,1)}, u32[]{:S(2)}) copy-start(bf16[32,128,64]{1,2,0:T(8,128)(2,1)} %param.7) | copy-start | bytes 1572868
  1.7 8.6 %collective-permute-start.3 = (bf16[128,256]{1,0:T(8,128)(2,1)S(1)}, bf16[128,256]{1,0:T(8,128)(2,1)S(1)}, u32[]{:S(2)}, u32[]{:S(2)}) collective-permute-start(bf16[128,256]{1,0:T(8,128)(2,1)S(1)} %pad_maximum_fusion.3), channel_id=1, source_target_pairs={{0,2},{2,0},{4,6},{6,4},{8,10},{10,8},{12,14},{14,12},{16,18},{18,... | collective-permute-start | bytes 196616 | tf_op jit(solution)/shard_map/ppermute | solution.py:467
  2.2 8.1 %collective-permute-start.4 = (bf16[128,256]{1,0:T(8,128)(2,1)S(1)}, bf16[128,256]{1,0:T(8,128)(2,1)S(1)}, u32[]{:S(2)}, u32[]{:S(2)}) collective-permute-start(bf16[128,256]{1,0:T(8,128)(2,1)S(1)} %pad_maximum_fusion.4), channel_id=1, source_target_pairs={{0,4},{2,6},{4,0},{6,2},{8,12},{10,14},{12,8},{14,10},{16,20},{18,... | collective-permute-start | bytes 196616 | tf_op jit(solution)/shard_map/ppermute | solution.py:467
  4.8 5.5 %collective-permute-start.5 = (bf16[128,256]{1,0:T(8,128)(2,1)S(1)}, bf16[128,256]{1,0:T(8,128)(2,1)S(1)}, u32[]{:S(2)}, u32[]{:S(2)}) collective-permute-start(bf16[128,256]{1,0:T(8,128)(2,1)S(1)} %pad_maximum_fusion.5), channel_id=1, source_target_pairs={{0,6},{2,4},{4,2},{6,0},{8,14},{10,12},{12,10},{14,8},{16,22},{18,... | collective-permute-start | bytes 196616 | tf_op jit(solution)/shard_map/ppermute | solution.py:467
  7.0 14.4 %collective-permute-start = (bf16[128,1024]{1,0:T(8,128)(2,1)S(1)}, bf16[128,1024]{1,0:T(8,128)(2,1)S(1)}, u32[]{:S(2)}, u32[]{:S(2)}) collective-permute-start(bf16[128,1024]{1,0:T(8,128)(2,1)S(1)} %get-tuple-element.28), channel_id=1, source_target_pairs={{0,2},{2,0},{4,6},{6,4},{8,10},{10,8},{12,14},{14,12},{16,18},{18,... | collective-permute-start | bytes 786440 | tf_op jit(solution)/shard_map/ppermute | solution.py:467
  7.1 18.4 %collective-permute-start.1 = (bf16[128,1024]{1,0:T(8,128)(2,1)S(1)}, bf16[128,1024]{1,0:T(8,128)(2,1)S(1)}, u32[]{:S(2)}, u32[]{:S(2)}) collective-permute-start(bf16[128,1024]{1,0:T(8,128)(2,1)S(1)} %get-tuple-element.30), channel_id=1, source_target_pairs={{0,4},{2,6},{4,0},{6,2},{8,12},{10,14},{12,8},{14,10},{16,20},{18,... | collective-permute-start | bytes 786440 | tf_op jit(solution)/shard_map/ppermute | solution.py:467
  10.3 15.2 %collective-permute-start.2 = (bf16[128,1024]{1,0:T(8,128)(2,1)S(1)}, bf16[128,1024]{1,0:T(8,128)(2,1)S(1)}, u32[]{:S(2)}, u32[]{:S(2)}) collective-permute-start(bf16[128,1024]{1,0:T(8,128)(2,1)S(1)} %get-tuple-element.27), channel_id=1, source_target_pairs={{0,6},{2,4},{4,2},{6,0},{8,14},{10,12},{12,10},{14,8},{16,22},{18,... | collective-permute-start | bytes 786440 | tf_op jit(solution)/shard_map/ppermute | solution.py:467
  10.4 6.9 %collective-permute-start.6 = (bf16[128,256]{1,0:T(8,128)(2,1)S(1)}, bf16[128,256]{1,0:T(8,128)(2,1)S(1)}, u32[]{:S(2)}, u32[]{:S(2)}) collective-permute-start(bf16[128,256]{1,0:T(8,128)(2,1)S(1)} %get-tuple-element.38), channel_id=1, source_target_pairs={{0,8},{2,10},{4,12},{6,14},{8,16},{10,18},{12,20},{14,22},{16,24},... | collective-permute-start | bytes 196616 | tf_op jit(solution)/shard_map/ppermute | solution.py:529
  13.9 11.6 %copy-start.1 = (bf16[512,256]{1,0:T(8,128)(2,1)}, bf16[512,256]{1,0:T(8,128)(2,1)S(1)}, u32[]{:S(2)}) copy-start(bf16[512,256]{1,0:T(8,128)(2,1)S(1)} %pad_maximum_fusion.1.refs_6_.refs_12_) | copy-start | bytes 786436
  13.9 23.2 %collective-permute-start.7 = (bf16[512,256]{1,0:T(8,128)(2,1)S(1)}, bf16[512,256]{1,0:T(8,128)(2,1)S(1)}, u32[]{:S(2)}, u32[]{:S(2)}) collective-permute-start(bf16[512,256]{1,0:T(8,128)(2,1)S(1)} %pad_maximum_fusion.1.refs_6_.refs_12_), channel_id=1, source_target_pairs={{0,24},{2,26},{4,28},{6,30},{1,25},{3,27},{5,29},{7,31}} | collective-permute-start | bytes 786440 | tf_op jit(solution)/shard_map/ppermute | solution.py:532
  17.3 8.2 %copy-start.8 = (bf16[128,256]{1,0:T(8,128)(2,1)}, bf16[128,256]{1,0:T(8,128)(2,1)S(1)}, u32[]{:S(2)}) copy-start(bf16[128,256]{1,0:T(8,128)(2,1)S(1)} %collective-permute-done.6.refs_5_) | copy-start | bytes 196612
  17.3 19.8 %collective-permute-start.8 = (bf16[512,256]{1,0:T(8,128)(2,1)S(1)}, bf16[512,256]{1,0:T(8,128)(2,1)S(1)}, u32[]{:S(2)}, u32[]{:S(2)}) collective-permute-start(bf16[512,256]{1,0:T(8,128)(2,1)S(1)} %pad_maximum_fusion.1.refs_6_.refs_12_), channel_id=1, source_target_pairs={{0,16},{2,18},{4,20},{6,22},{8,24},{10,26},{12,28},{14,30},{1,17},... | collective-permute-start | bytes 786440 | tf_op jit(solution)/shard_map/ppermute | solution.py:532
  21.4 4.1 %copy-start.2 = (bf16[128,1024]{1,0:T(8,128)(2,1)}, bf16[128,1024]{1,0:T(8,128)(2,1)S(1)}, u32[]{:S(2)}) copy-start(bf16[128,1024]{1,0:T(8,128)(2,1)S(1)} %collective-permute-done.refs_1_) | copy-start | bytes 786436
  21.4 15.7 %collective-permute-start.9 = (bf16[512,256]{1,0:T(8,128)(2,1)S(1)}, bf16[512,256]{1,0:T(8,128)(2,1)S(1)}, u32[]{:S(2)}, u32[]{:S(2)}) collective-permute-start(bf16[512,256]{1,0:T(8,128)(2,1)S(1)} %pad_maximum_fusion.1.refs_6_.refs_12_), channel_id=1, source_target_pairs={{0,8},{2,10},{4,12},{6,14},{8,16},{10,18},{12,20},{14,22},{16,24},... | collective-permute-start | bytes 786440 | tf_op jit(solution)/shard_map/ppermute | solution.py:532
  25.5 0.7 copy-start.3
  25.5 0.8 copy-start.4
  37.1 0.7 copy-start.5
  37.1 0.8 copy-start.6
  37.1 0.9 copy-start.7
  55.1 19.9 %collective-permute-start.13 = (bf16[528,128]{1,0:T(8,128)(2,1)}, bf16[528,128]{1,0:T(8,128)(2,1)S(1)}, u32[]{:S(2)}, u32[]{:S(2)}) collective-permute-start(bf16[528,128]{1,0:T(8,128)(2,1)} %get-tuple-element.20), channel_id=1, source_target_pairs={{0,8},{2,10},{4,12},{6,14},{8,0},{10,2},{12,4},{14,6},{16,24},{18,... | collective-permute-start | bytes 405512 | tf_op jit(solution)/shard_map/ppermute | solution.py:467
  64.9 11.4 %collective-permute-start.14 = (bf16[528,128]{1,0:T(8,128)(2,1)}, bf16[528,128]{1,0:T(8,128)(2,1)S(1)}, u32[]{:S(2)}, u32[]{:S(2)}) collective-permute-start(bf16[528,128]{1,0:T(8,128)(2,1)} %get-tuple-element.20), channel_id=1, source_target_pairs={{0,16},{2,18},{4,20},{6,22},{8,24},{10,26},{12,28},{14,30},{16,0},... | collective-permute-start | bytes 405512 | tf_op jit(solution)/shard_map/ppermute | solution.py:467
  72.0 11.0 %collective-permute-start.15 = (bf16[528,128]{1,0:T(8,128)(2,1)}, bf16[528,128]{1,0:T(8,128)(2,1)S(1)}, u32[]{:S(2)}, u32[]{:S(2)}) collective-permute-start(bf16[528,128]{1,0:T(8,128)(2,1)} %get-tuple-element.20), channel_id=1, source_target_pairs={{0,24},{2,26},{4,28},{6,30},{8,16},{10,18},{12,20},{14,22},{16,8},... | collective-permute-start | bytes 405512 | tf_op jit(solution)/shard_map/ppermute | solution.py:467
  73.3 12.4 %collective-permute-start.10 = (bf16[128,1024]{1,0:T(8,128)(2,1)}, bf16[128,1024]{1,0:T(8,128)(2,1)S(1)}, u32[]{:S(2)}, u32[]{:S(2)}) collective-permute-start(bf16[128,1024]{1,0:T(8,128)(2,1)} %get-tuple-element.16), channel_id=1, source_target_pairs={{0,6},{2,4},{4,2},{6,0},{8,14},{10,12},{12,10},{14,8},{16,22},{18,... | collective-permute-start | bytes 786440 | tf_op jit(solution)/shard_map/ppermute | solution.py:467
  73.9 13.9 %collective-permute-start.11 = (bf16[128,1024]{1,0:T(8,128)(2,1)}, bf16[128,1024]{1,0:T(8,128)(2,1)S(1)}, u32[]{:S(2)}, u32[]{:S(2)}) collective-permute-start(bf16[128,1024]{1,0:T(8,128)(2,1)} %get-tuple-element.17), channel_id=1, source_target_pairs={{0,4},{2,6},{4,0},{6,2},{8,12},{10,14},{12,8},{14,10},{16,20},{18,... | collective-permute-start | bytes 786440 | tf_op jit(solution)/shard_map/ppermute | solution.py:467
  74.9 13.0 %collective-permute-start.12 = (bf16[128,1024]{1,0:T(8,128)(2,1)}, bf16[128,1024]{1,0:T(8,128)(2,1)S(1)}, u32[]{:S(2)}, u32[]{:S(2)}) collective-permute-start(bf16[128,1024]{1,0:T(8,128)(2,1)} %get-tuple-element.18), channel_id=1, source_target_pairs={{0,2},{2,0},{4,6},{6,4},{8,10},{10,8},{12,14},{14,12},{16,18},{18,... | collective-permute-start | bytes 786440 | tf_op jit(solution)/shard_map/ppermute | solution.py:467
  84.1 9.4 %collective-permute-start.16 = (bf16[528,128]{1,0:T(8,128)(2,1)S(1)}, bf16[528,128]{1,0:T(8,128)(2,1)S(1)}, u32[]{:S(2)}, u32[]{:S(2)}) collective-permute-start(bf16[528,128]{1,0:T(8,128)(2,1)S(1)} %concatenate.43), channel_id=1, source_target_pairs={{0,2},{2,0},{4,6},{6,4},{8,10},{10,8},{12,14},{14,12},{16,18},{18,... | collective-permute-start | bytes 405512 | tf_op jit(solution)/shard_map/ppermute | solution.py:467
  84.1 9.4 %collective-permute-start.17 = (bf16[528,128]{1,0:T(8,128)(2,1)S(1)}, bf16[528,128]{1,0:T(8,128)(2,1)S(1)}, u32[]{:S(2)}, u32[]{:S(2)}) collective-permute-start(bf16[528,128]{1,0:T(8,128)(2,1)S(1)} %concatenate.43), channel_id=1, source_target_pairs={{0,4},{2,6},{4,0},{6,2},{8,12},{10,14},{12,8},{14,10},{16,20},{18,... | collective-permute-start | bytes 405512 | tf_op jit(solution)/shard_map/ppermute | solution.py:467
  85.7 7.8 %collective-permute-start.18 = (bf16[528,128]{1,0:T(8,128)(2,1)S(1)}, bf16[528,128]{1,0:T(8,128)(2,1)S(1)}, u32[]{:S(2)}, u32[]{:S(2)}) collective-permute-start(bf16[528,128]{1,0:T(8,128)(2,1)S(1)} %concatenate.43), channel_id=1, source_target_pairs={{0,6},{2,4},{4,2},{6,0},{8,14},{10,12},{12,10},{14,8},{16,22},{18,... | collective-permute-start | bytes 405512 | tf_op jit(solution)/shard_map/ppermute | solution.py:467
  93.5 3.6 %collective-permute-start.19 = (f32[128]{0:T(128)S(1)}, f32[128]{0:T(128)S(1)}, u32[]{:S(2)}, u32[]{:S(2)}) collective-permute-start(f32[128]{0:T(128)S(1)} %add_bitcast_fusion), channel_id=1, source_target_pairs={{0,1},{1,0},{2,3},{3,2},{4,5},{5,4},{6,7},{7,6},{8,9},{9,8},{10,11... | collective-permute-start | bytes 1544 | tf_op jit(solution)/shard_map/ppermute | solution.py:556
